TPU v7x, 256 devices: a whole 4x4x8 slice. The times are simulated.
256 devices in a mesh: ctx: 32 (over z_hi, x, core), tp: 8 (over y, z_lo).
Axes of the slice: x: 4, y: 4, z: 8 (z_hi: 4, z_lo: 2; z = z_hi * 2 + z_lo), core: 2. Of those that a mesh axis runs over, the one named last changes fastest.
Arguments:
- features: bfloat16 [16384, 3, 4096], P('ctx', None, 'tp'), may hold values from -6 to 6
- short_filter: float32 [3, 7, 4096], P(None, None, 'tp'), may hold values from -2 to 2
- decay_rate: float32 [16, 4096], P(None, 'tp'), may hold values from 0 to 1, as said below
- residue: float32 [16, 4096], P(None, 'tp'), may hold values from -2 to 2
- skip_gain: float32 [4096], P('tp'), may hold values from -4 to 4
- norm_gain: float32 [4096], replicated, may hold values from 0.1 to 1.9
- qkv_weight: bfloat16 [4096, 3, 2048], P('ctx', None, 'tp'), may hold values from -2 to 2
Outputs:
- mixer: bfloat16 [16384, 4096], P('ctx', 'tp')
- attended: bfloat16 [16384, 2048], P('ctx', 'tp')
Inputs may be any that keep to these rules, and one draw needn't show every extreme that they name: `decay_rate`: decay rates are positive.
All inputs are finite; a program needn't handle non-finite values.
Results may differ from a plain program's by a relative error of at most 0.01.
Values may be sent and summed in bfloat16 or wider, within the bound.
No kernel may reach another device: no remote copies, remote signals or barrier semaphores. Data moves between devices by JAX's collectives and lax.ppermute only.
A program may use at most 128 MiB of HBM per device.

v0:
```python
from functools import reduce
import math

import jax
import jax.numpy as jnp
from jax import lax
from jax.sharding import PartitionSpec as P
from jax.experimental import pallas as pl
from jax.experimental.pallas import tpu as pltpu

HD = 128
TAPS = 7
WINDOW = 3
CHUNK = 128
GROUP = 8


EPSILON = 1e-06


def from_behind(value, axis, steps):
    count = lax.axis_size(axis)
    leading, last = (max(0, -steps), min(count, count - steps))
    return lax.ppermute(value, axis, [(source, source + steps) for source in range(leading, last)])


def bf16_split(value):
    high = value.astype(jnp.bfloat16)
    low = (value - high.astype(jnp.float32)).astype(jnp.bfloat16)
    return high, low


def intra_kernel(gated_ref, decay_ref, mixing_ref, intra_ref):
    tokens, channels = gated_ref.shape
    chunks = tokens // CHUNK
    offsets = lax.broadcasted_iota(jnp.int32, (CHUNK, channels), 0).astype(jnp.float32) - (CHUNK - 1) / 2.0
    rows = lax.broadcasted_iota(jnp.int32, (CHUNK, CHUNK), 0)
    cols = lax.broadcasted_iota(jnp.int32, (CHUNK, CHUNK), 1)
    tri = (rows >= cols).astype(jnp.float32).astype(jnp.bfloat16)
    intra_ref[...] = jnp.zeros_like(intra_ref)

    def add_mode(mode, unused):
        rate = decay_ref[mode]
        weight = mixing_ref[mode] * jnp.sqrt(rate)
        up = jnp.exp(offsets * rate)
        down = jnp.exp(-offsets * rate)
        for chunk in range(chunks):
            rows_of = pl.ds(chunk * CHUNK, CHUNK)
            high, low = bf16_split(up * gated_ref[rows_of, :])
            summed = jnp.dot(tri, high, preferred_element_type=jnp.float32) + jnp.dot(
                tri, low, preferred_element_type=jnp.float32
            )
            states = down * summed
            intra_ref[rows_of, :] += weight * states
        return unused

    lax.fori_loop(0, decay_ref.shape[0], add_mode, 0)


def front_kernel(feat_ref, halo_ref, taps_ref, decay_ref, first_ref, gated_ref, ends_ref, ext_ref):
    tokens, channels = first_ref.shape
    chunks = tokens // CHUNK
    lead = 8

    def short(stream, rows_of):
        taps = [taps_ref[stream, pl.ds(offset, 1), :] for offset in range(TAPS)]
        total = taps[0] * ext_ref[stream, pl.ds(lead + rows_of, CHUNK), :]
        for offset in range(1, TAPS):
            total = total + taps[offset] * ext_ref[stream, pl.ds(lead - offset + rows_of, CHUNK), :]
        return total

    for stream in range(3):
        cols = pl.ds(stream * channels, channels)
        ext_ref[stream, pl.ds(lead - (TAPS - 1), TAPS - 1), :] = halo_ref[:, cols].astype(jnp.float32)
        ext_ref[stream, pl.ds(lead, tokens), :] = feat_ref[:, cols].astype(jnp.float32)
    for chunk in range(chunks):
        rows_of = chunk * CHUNK
        first_ref[pl.ds(rows_of, CHUNK), :] = short(0, rows_of)
        product = short(1, rows_of) * short(2, rows_of)
        gated_ref[pl.ds(rows_of, CHUNK), :] = product.astype(jnp.bfloat16).astype(jnp.float32)

    tail = (CHUNK - 1) - lax.broadcasted_iota(jnp.int32, (CHUNK, channels), 0).astype(jnp.float32)

    def add_mode(mode, unused):
        fade = jnp.exp(-tail * decay_ref[mode])
        for chunk in range(chunks):
            block = gated_ref[pl.ds(chunk * CHUNK, CHUNK), :]
            ends_ref[mode, pl.ds(chunk, 1), :] = jnp.sum(fade * block, axis=0, keepdims=True)
        return unused

    lax.fori_loop(0, decay_ref.shape[0], add_mode, 0)


def front_call(features, halo, short_filter, decay3):
    tokens, streams, channels = features.shape
    modes = decay3.shape[0]
    chunks = tokens // CHUNK
    return pl.pallas_call(
        front_kernel,
        out_shape=(
            whole((tokens, channels), jnp.float32),
            whole((tokens, channels), jnp.float32),
            whole((modes, chunks, channels), jnp.float32),
        ),
        in_specs=in_vmem(4),
        out_specs=tuple(in_vmem(3)),
        scratch_shapes=[pltpu.VMEM((streams, tokens + 8, channels), jnp.float32)],
        cost_estimate=pl.CostEstimate(
            flops=2 * (3 * TAPS + modes) * tokens * channels, transcendentals=modes * CHUNK * channels,
            bytes_accessed=14 * tokens * channels,
        ),
    )(features.reshape(tokens, streams * channels), halo.reshape(halo.shape[0], streams * channels), short_filter, decay3)


def finish_kernel(intra_ref, state_ref, decay_ref, mixing_ref, gated_ref, first_ref, skip_ref, mixer_ref, acc_ref):
    tokens, channels = gated_ref.shape
    chunks = tokens // CHUNK
    after = lax.broadcasted_iota(jnp.int32, (CHUNK, channels), 0).astype(jnp.float32) + 1.0
    acc_ref[...] = intra_ref[...]

    def add_mode(mode, unused):
        rate = decay_ref[mode]
        decayed = jnp.exp(-after * rate) * (mixing_ref[mode] * jnp.sqrt(rate))
        for chunk in range(chunks):
            rows_of = pl.ds(chunk * CHUNK, CHUNK)
            acc_ref[rows_of, :] += decayed * state_ref[mode, pl.ds(chunk, 1), :]
        return unused

    lax.fori_loop(0, decay_ref.shape[0], add_mode, 0)
    filtered = acc_ref[...] + skip_ref[...] * gated_ref[...]
    filtered = filtered.astype(jnp.bfloat16).astype(jnp.float32)
    mixer_ref[...] = (first_ref[...] * filtered).astype(mixer_ref.dtype)


def whole(shape, dtype):
    return jax.ShapeDtypeStruct(shape, dtype)


def in_vmem(count):
    return [pl.BlockSpec(memory_space=pltpu.VMEM)] * count


def intra_call(gated, decay3, mixing3):
    tokens, channels = gated.shape
    modes = decay3.shape[0]
    return pl.pallas_call(
        intra_kernel,
        out_shape=whole((tokens, channels), jnp.float32),
        in_specs=in_vmem(3),
        out_specs=pl.BlockSpec(memory_space=pltpu.VMEM),
        cost_estimate=pl.CostEstimate(
            flops=4 * modes * tokens * CHUNK * channels, transcendentals=2 * modes * CHUNK * channels,
            bytes_accessed=8 * tokens * channels,
        ),
    )(gated, decay3, mixing3)


def exchange_history(block_end, decay, tok_dev):
    count = lax.axis_size("ctx")
    group = math.gcd(count, GROUP)
    me = lax.axis_index("ctx")
    place = me % group

    def decayed(blocks):
        return jnp.exp(-(blocks.astype(jnp.float32) * float(tok_dev)) * decay)

    prefix = jnp.zeros_like(decay)
    total = decayed(group - 1 - place) * block_end
    for shift in range(1, group):
        pairs = [(g + q, g + (q + shift) % group) for g in range(0, count, group) for q in range(group)]
        arrived = lax.ppermute(block_end, "ctx", pairs)
        source = (place - shift) % group
        prefix = prefix + jnp.where(source < place, decayed(place - 1 - source), 0.0) * arrived
        total = total + decayed(group - 1 - source) * arrived
    entering = jnp.zeros_like(decay)
    for hop in range(1, count // group):
        arrived = from_behind(total, "ctx", hop * group)
        entering = entering + decayed(jnp.int32((hop - 1) * group)) * arrived
    return prefix + decayed(place) * entering


def finish_call(intra, entering, decay3, mixing3, gated, first, skip):
    tokens, channels = gated.shape
    modes = decay3.shape[0]
    return pl.pallas_call(
        finish_kernel,
        out_shape=whole((tokens, channels), jnp.bfloat16),
        in_specs=in_vmem(7),
        out_specs=pl.BlockSpec(memory_space=pltpu.VMEM),
        scratch_shapes=[pltpu.VMEM((tokens, channels), jnp.float32)],
        cost_estimate=pl.CostEstimate(
            flops=2 * modes * tokens * channels, transcendentals=modes * CHUNK * channels,
            bytes_accessed=14 * tokens * channels,
        ),
    )(intra, entering, decay3, mixing3, gated, first, skip)


def chunk_states(ends, decay):
    step = jnp.exp(-float(CHUNK) * decay)
    carry = jnp.zeros_like(decay)
    entering = []
    for chunk in range(ends.shape[1]):
        entering.append(carry)
        carry = step * carry + ends[:, chunk]
    return jnp.stack(entering, axis=1), carry


def block_body(features, short_filter, decay_rate, residue, skip_gain, norm_gain, qkv_weight):
    tok_dev, _, channels = features.shape
    head_cols = qkv_weight.shape[2]
    shard_rows = lax.all_gather(qkv_weight, "ctx", axis=0, tiled=True)
    rim_rows = features[tok_dev - (TAPS - 1) :]
    before = from_behind(rim_rows, "ctx", 1)
    decay3 = decay_rate[:, None, :]
    mixing3 = residue[:, None, :]
    first, gated, ends = front_call(features, before, short_filter, decay3)
    entering, block_end = chunk_states(ends, decay_rate)
    history = exchange_history(block_end, decay_rate, tok_dev)
    intra = intra_call(gated, decay3, mixing3)
    chunks = tok_dev // CHUNK
    lead = jnp.exp(-float(CHUNK) * jnp.arange(chunks, dtype=jnp.float32)[None, :, None] * decay_rate[:, None, :])
    total_state = entering + lead * history[:, None, :]
    mixer = finish_call(intra, total_state, decay3, mixing3, gated, first, skip_gain[None])

    parts = lax.axis_size("tp")
    me = lax.axis_index("tp")
    pieces = [mixer] + [
        lax.ppermute(mixer, "tp", [((source + shift) % parts, source) for source in range(parts)])
        for shift in range(1, parts)
    ]
    doubled = jnp.concatenate(pieces + pieces, axis=1)
    gathered = lax.dynamic_slice_in_dim(doubled, ((parts - me) % parts) * channels, parts * channels, 1)
    as_float = gathered.astype(jnp.float32)
    inverse = lax.rsqrt(jnp.mean(as_float * as_float, axis=1, keepdims=True) + EPSILON)
    normed = (as_float * inverse * norm_gain[None]).astype(jnp.bfloat16)
    flat_rows = shard_rows.reshape(shard_rows.shape[0], 3 * head_cols)
    projected = jnp.dot(normed, flat_rows, preferred_element_type=jnp.float32).astype(jnp.bfloat16)
    heads = head_cols // HD
    query = projected[:, :head_cols].reshape(tok_dev, heads, HD)
    kv_pair = projected[:, head_cols:]
    blocks_kv = [kv_pair]
    for _ in range(WINDOW - 1):
        blocks_kv.append(from_behind(blocks_kv[-1], "ctx", 1))
    position = lax.axis_index("ctx")
    row_ids = jnp.arange(tok_dev)
    causal = row_ids[:, None] >= row_ids[None, :]
    score_list = []
    for lag_step in range(WINDOW):
        keys = blocks_kv[lag_step][:, :head_cols].reshape(tok_dev, heads, HD)
        scores = jnp.einsum(
            "thd,shd->hts", query, keys, preferred_element_type=jnp.float32
        ) / math.sqrt(HD)
        if lag_step == 0:
            allowed = causal
        else:
            allowed = jnp.broadcast_to(position >= lag_step, causal.shape)
        score_list.append(jnp.where(allowed[None], scores, -jnp.inf))
    peak = reduce(jnp.maximum, [jnp.max(entry, axis=2) for entry in score_list])
    total = jnp.zeros((heads, tok_dev), jnp.float32)
    output = jnp.zeros((tok_dev, heads, HD), jnp.float32)
    for lag_step in range(WINDOW):
        expo = jnp.exp(score_list[lag_step] - peak[:, :, None])
        total = total + jnp.sum(expo, axis=2)
        values = blocks_kv[lag_step][:, head_cols:].reshape(tok_dev, heads, HD)
        output = output + jnp.einsum(
            "hts,shd->thd", expo.astype(jnp.bfloat16), values, preferred_element_type=jnp.float32
        )
    attended = (output / total.T[:, :, None]).astype(jnp.bfloat16).reshape(tok_dev, head_cols)
    return (mixer, attended)


def solution(mesh):
    placed = (
        P("ctx", None, "tp"),
        P(None, None, "tp"),
        P(None, "tp"),
        P(None, "tp"),
        P("tp"),
        P(),
        P("ctx", None, "tp"),
    )
    return jax.shard_map(
        block_body,
        mesh=mesh,
        in_specs=placed,
        out_specs=(P("ctx", "tp"), P("ctx", "tp")),
        check_vma=False,
    )
```

profile of v0, /device:TPU:128, one launch (start us, length us, event | category | flops | bytes accessed | tf_op | source)
XLA Modules:
  0.0 194.4 jit_solution(10203416366653851353)
XLA Ops:
  7.2 1.7 copy.37
  9.7 1.9 collective-permute-start
  11.7 1.7 copy.29
  14.0 1.6 copy.30.feat_ref
  15.6 3.5 %collective-permute-done = bf16[6,3,512]{2,0,1:T(8,128)(2,1)S(1)} collective-permute-done((bf16[6,3,512]{2,0,1:T(8,128)(2,1)S(1)}, bf16[6,3,512]{2,0,1:T(8,128)(2,1)S(1)}, u32[]{:S(2)}, u32[]{:S(2)}) %collective-permute-start) | collective-permute-done | bytes 18464 | tf_op jit(solution)/shard_map/ppermute | solution.py:24
  19.7 8.8 %shard_map.86 = (f32[512,512]{1,0:T(8,128)}, f32[512,512]{1,0:T(8,128)}, f32[16,4,512]{2,1,0:T(4,128)}) custom-call(bf16[512,1536]{1,0:T(8,128)(2,1)} %copy.30.feat_ref, bf16[6,1536]{1,0:T(8,128)(2,1)} %bitcast.99, f32[3,7,512]{2,1,0:T(8,128)} %taps_ref.1, f32[16,1,512]{2,1,0:T(1,128)} %broadcast_in_dim.56.decay_ref), custom_call_target="tpu_custom_call" | custom-call | flops 19398656 | bytes 3670016 | tf_op jit(solution)/shard_map/pallas_call | solution.py:98
  29.7 4.2 %collective-permute-start.4 = (f32[16,512]{1,0:T(8,128)S(1)}, f32[16,512]{1,0:T(8,128)S(1)}, u32[]{:S(2)}, u32[]{:S(2)}) collective-permute-start(f32[16,512]{1,0:T(8,128)S(1)} %get-tuple-element.15), channel_id=1, source_target_pairs={{0,32},{8,40},{16,48},{24,56},{32,0},{40,8},{48,16},{56,24},{64,96... | collective-permute-start | bytes 98312 | tf_op jit(solution)/shard_map/ppermute | solution.py:171
  39.6 3.0 %collective-permute-start.8 = (f32[16,512]{1,0:T(8,128)S(1)}, f32[16,512]{1,0:T(8,128)S(1)}, u32[]{:S(2)}, u32[]{:S(2)}) collective-permute-start(f32[16,512]{1,0:T(8,128)S(1)} %multiply_add_fusion.1), channel_id=1, source_target_pairs={{0,64},{8,72},{16,80},{24,88},{32,96},{40,104},{48,112},{56,120},{... | collective-permute-start | bytes 98312 | tf_op jit(solution)/shard_map/ppermute | solution.py:24
  43.9 10.4 %shard_map.87.intra_ref = f32[512,512]{1,0:T(8,128)} custom-call(f32[512,512]{1,0:T(8,128)} %get-tuple-element.5.gated_ref, f32[16,1,512]{2,1,0:T(1,128)} %broadcast_in_dim.56.decay_ref, f32[16,1,512]{2,1,0:T(1,128)} %broadcast_in_dim.57.mixing_ref), custom_call_target="tpu_custom_call" | custom-call | flops 2147483648 | bytes 2097152 | tf_op jit(solution)/shard_map/pallas_call | solution.py:146
  55.4 5.1 %shard_map.88 = bf16[512,512]{1,0:T(8,128)(2,1)} custom-call(f32[512,512]{1,0:T(8,128)} %shard_map.87.intra_ref, f32[16,4,512]{2,1,0:T(4,128)} %maximum_add_fusion.state_ref, f32[16,1,512]{2,1,0:T(1,128)} %broadcast_in_dim.56.decay_ref, f32[16,1,512]{2,1,0:T(1,128)} %broadcast_in_dim.57.mixing_ref, f32[512,512]{1,0:T(8,128)} %get-tuple-element.5.gated_ref, ...), custom_call_target="tpu_custom_call" | custom-call | flops 8388608 | bytes 3670016 | tf_op jit(solution)/shard_map/pallas_call | solution.py:185
  60.5 3.5 %collective-permute-start.11 = (bf16[512,512]{1,0:T(8,128)(2,1)}, bf16[512,512]{1,0:T(8,128)(2,1)S(1)}, u32[]{:S(2)}, u32[]{:S(2)}) collective-permute-start(bf16[512,512]{1,0:T(8,128)(2,1)} %shard_map.88), channel_id=1, source_target_pairs={{1,0},{2,1},{3,2},{4,3},{5,4},{6,5},{7,6},{0,7},{9,8},{10,9},{11,1... | collective-permute-start | bytes 1572872 | tf_op jit(solution)/shard_map/ppermute | solution.py:228
  65.6 2.9 %collective-permute-start.14 = (bf16[512,512]{1,0:T(8,128)(2,1)}, bf16[512,512]{1,0:T(8,128)(2,1)S(1)}, u32[]{:S(2)}, u32[]{:S(2)}) collective-permute-start(bf16[512,512]{1,0:T(8,128)(2,1)} %shard_map.88), channel_id=1, source_target_pairs={{4,0},{5,1},{6,2},{7,3},{0,4},{1,5},{2,6},{3,7},{12,8},{13,9},{14,... | collective-permute-start | bytes 1572872 | tf_op jit(solution)/shard_map/ppermute | solution.py:228
  69.8 20.5 %collective-permute-done.11 = bf16[512,512]{1,0:T(8,128)(2,1)S(1)} collective-permute-done((bf16[512,512]{1,0:T(8,128)(2,1)}, bf16[512,512]{1,0:T(8,128)(2,1)S(1)}, u32[]{:S(2)}, u32[]{:S(2)}) %collective-permute-start.11) | collective-permute-done | bytes 524320 | tf_op jit(solution)/shard_map/ppermute | solution.py:228
  90.3 2.3 %collective-permute-start.16 = (bf16[512,512]{1,0:T(8,128)(2,1)}, bf16[512,512]{1,0:T(8,128)(2,1)S(1)}, u32[]{:S(2)}, u32[]{:S(2)}) collective-permute-start(bf16[512,512]{1,0:T(8,128)(2,1)} %shard_map.88), channel_id=1, source_target_pairs={{6,0},{7,1},{0,2},{1,3},{2,4},{3,5},{4,6},{5,7},{14,8},{15,9},{8,1... | collective-permute-start | bytes 1572872 | tf_op jit(solution)/shard_map/ppermute | solution.py:228
  92.6 18.8 %collective-permute-start.17 = (bf16[512,512]{1,0:T(8,128)(2,1)S(1)}, bf16[512,512]{1,0:T(8,128)(2,1)S(1)}, u32[]{:S(2)}, u32[]{:S(2)}) collective-permute-start(bf16[512,512]{1,0:T(8,128)(2,1)S(1)} %copy-done), channel_id=1, source_target_pairs={{7,0},{0,1},{1,2},{2,3},{3,4},{4,5},{5,6},{6,7},{15,8},{8,9},{9,10... | collective-permute-start | bytes 1572872 | tf_op jit(solution)/shard_map/ppermute | solution.py:228
  111.6 4.8 %collective-permute-done.15 = bf16[512,512]{1,0:T(8,128)(2,1)S(1)} collective-permute-done((bf16[512,512]{1,0:T(8,128)(2,1)}, bf16[512,512]{1,0:T(8,128)(2,1)S(1)}, u32[]{:S(2)}, u32[]{:S(2)}) %collective-permute-start.15) | collective-permute-done | bytes 524320 | tf_op jit(solution)/shard_map/ppermute | solution.py:228
  116.5 12.3 %collective-permute-done.16 = bf16[512,512]{1,0:T(8,128)(2,1)S(1)} collective-permute-done((bf16[512,512]{1,0:T(8,128)(2,1)}, bf16[512,512]{1,0:T(8,128)(2,1)S(1)}, u32[]{:S(2)}, u32[]{:S(2)}) %collective-permute-start.16) | collective-permute-done | bytes 524320 | tf_op jit(solution)/shard_map/ppermute | solution.py:228
  129.6 3.2 %copy-done.1 = bf16[512,8192]{1,0:T(8,128)(2,1)} copy-done((bf16[512,8192]{1,0:T(8,128)(2,1)}, bf16[512,8192]{1,0:T(8,128)(2,1)S(1)}, u32[]{:S(2)}) %copy-start.1) | copy-done | bytes 8388632
  133.7 7.5 %fusion.17 = bf16[512,768]{1,0:T(8,128)(2,1)S(1)} fusion(bf16[4096,768]{0,1:T(8,128)(2,1)} %bitcast.98, f32[4096]{0:T(1024)S(1)} %copy-done.8, f32[512]{0:T(512)S(1)} %add_rsqrt_fusion, bf16[512,8192]{1,0:T(8,128)(2,1)} %copy-done.1, s32[]{:T(128)S(6)} %select_n.119), kind=kOutput, calls=%fused_computation.24 | convolution fusion | flops 3230007296 | bytes 11290628 | tf_op jit(solution)/shard_map/dot_general | solution.py:237
  141.3 1.9 collective-permute-start.18
  144.2 1.9 fusion.8
  146.1 13.0 %collective-permute-done.18 = bf16[512,512]{1,0:T(8,128)(2,1)} collective-permute-done((bf16[512,512]{1,0:T(8,128)(2,1)S(1)}, bf16[512,512]{1,0:T(8,128)(2,1)}, u32[]{:S(2)}, u32[]{:S(2)}) %collective-permute-start.18) | collective-permute-done | bytes 524320 | tf_op jit(solution)/shard_map/ppermute | solution.py:24
  159.0 2.1 %collective-permute-start.19 = (bf16[512,512]{1,0:T(8,128)(2,1)}, bf16[512,512]{1,0:T(8,128)(2,1)}, u32[]{:S(2)}, u32[]{:S(2)}) collective-permute-start(bf16[512,512]{1,0:T(8,128)(2,1)} %collective-permute-done.18), channel_id=1, source_target_pairs={{0,8},{8,16},{16,24},{24,32},{32,40},{40,48},{48,56},{56,64},{64,7... | collective-permute-start | bytes 1572872 | tf_op jit(solution)/shard_map/ppermute | solution.py:24
  162.9 16.7 %collective-permute-done.19 = bf16[512,512]{1,0:T(8,128)(2,1)} collective-permute-done((bf16[512,512]{1,0:T(8,128)(2,1)}, bf16[512,512]{1,0:T(8,128)(2,1)}, u32[]{:S(2)}, u32[]{:S(2)}) %collective-permute-start.19) | collective-permute-done | bytes 524320 | tf_op jit(solution)/shard_map/ppermute | solution.py:24
  (93 shorter events, 26.4 us)
Async XLA Ops:
  7.2 6.2 %copy-start.3 = (f32[16,512]{1,0:T(8,128)S(1)}, f32[16,512]{1,0:T(8,128)}, u32[]{:S(2)}) copy-start(f32[16,512]{1,0:T(8,128)} %param.9) | copy-start | bytes 98308
  7.2 126.5 %all-gather.2.cloned.1.call-start = ((), (), s32[]{:S(2)}) async-start(), calls=%async_computation | async-start | bytes 6488064 | tf_op jit(solution)/shard_map/all_gather | solution.py:211
  9.7 9.4 %collective-permute-start = (bf16[6,3,512]{2,0,1:T(8,128)(2,1)S(1)}, bf16[6,3,512]{2,0,1:T(8,128)(2,1)S(1)}, u32[]{:S(2)}, u32[]{:S(2)}) collective-permute-start(bf16[6,3,512]{2,0,1:T(8,128)(2,1)S(1)} %slice.41), channel_id=1, source_target_pairs={{0,8},{8,16},{16,24},{24,32},{32,40},{40,48},{48,56},{56,64},{64,7... | collective-permute-start | bytes 55304 | tf_op jit(solution)/shard_map/ppermute | solution.py:24
  15.6 20.8 %copy-start.6 = (f32[16,512]{1,0:T(8,128)S(1)}, f32[16,512]{1,0:T(8,128)}, u32[]{:S(2)}) copy-start(f32[16,512]{1,0:T(8,128)} %param.10) | copy-start | bytes 98308
  29.5 5.2 %collective-permute-start.1 = (f32[16,512]{1,0:T(8,128)S(1)}, f32[16,512]{1,0:T(8,128)S(1)}, u32[]{:S(2)}, u32[]{:S(2)}) collective-permute-start(f32[16,512]{1,0:T(8,128)S(1)} %get-tuple-element.15), channel_id=1, source_target_pairs={{0,8},{8,16},{16,24},{24,32},{32,40},{40,48},{48,56},{56,0},{64,72... | collective-permute-start | bytes 98312 | tf_op jit(solution)/shard_map/ppermute | solution.py:171
  29.5 6.8 %collective-permute-start.2 = (f32[16,512]{1,0:T(8,128)S(1)}, f32[16,512]{1,0:T(8,128)S(1)}, u32[]{:S(2)}, u32[]{:S(2)}) collective-permute-start(f32[16,512]{1,0:T(8,128)S(1)} %get-tuple-element.15), channel_id=1, source_target_pairs={{0,16},{8,24},{16,32},{24,40},{32,48},{40,56},{48,0},{56,8},{64,80... | collective-permute-start | bytes 98312 | tf_op jit(solution)/shard_map/ppermute | solution.py:171
  29.6 7.5 %collective-permute-start.3 = (f32[16,512]{1,0:T(8,128)S(1)}, f32[16,512]{1,0:T(8,128)S(1)}, u32[]{:S(2)}, u32[]{:S(2)}) collective-permute-start(f32[16,512]{1,0:T(8,128)S(1)} %get-tuple-element.15), channel_id=1, source_target_pairs={{0,24},{8,32},{16,40},{24,48},{32,56},{40,0},{48,8},{56,16},{64,88... | collective-permute-start | bytes 98312 | tf_op jit(solution)/shard_map/ppermute | solution.py:171
  29.7 7.4 %collective-permute-start.4 = (f32[16,512]{1,0:T(8,128)S(1)}, f32[16,512]{1,0:T(8,128)S(1)}, u32[]{:S(2)}, u32[]{:S(2)}) collective-permute-start(f32[16,512]{1,0:T(8,128)S(1)} %get-tuple-element.15), channel_id=1, source_target_pairs={{0,32},{8,40},{16,48},{24,56},{32,0},{40,8},{48,16},{56,24},{64,96... | collective-permute-start | bytes 98312 | tf_op jit(solution)/shard_map/ppermute | solution.py:171
  33.9 3.4 %collective-permute-start.5 = (f32[16,512]{1,0:T(8,128)S(1)}, f32[16,512]{1,0:T(8,128)S(1)}, u32[]{:S(2)}, u32[]{:S(2)}) collective-permute-start(f32[16,512]{1,0:T(8,128)S(1)} %get-tuple-element.15), channel_id=1, source_target_pairs={{0,40},{8,48},{16,56},{24,0},{32,8},{40,16},{48,24},{56,32},{64,10... | collective-permute-start | bytes 98312 | tf_op jit(solution)/shard_map/ppermute | solution.py:171
  34.7 4.2 %collective-permute-start.6 = (f32[16,512]{1,0:T(8,128)S(1)}, f32[16,512]{1,0:T(8,128)S(1)}, u32[]{:S(2)}, u32[]{:S(2)}) collective-permute-start(f32[16,512]{1,0:T(8,128)S(1)} %get-tuple-element.15), channel_id=1, source_target_pairs={{0,48},{8,56},{16,0},{24,8},{32,16},{40,24},{48,32},{56,40},{64,11... | collective-permute-start | bytes 98312 | tf_op jit(solution)/shard_map/ppermute | solution.py:171
  36.3 2.6 %collective-permute-start.7 = (f32[16,512]{1,0:T(8,128)S(1)}, f32[16,512]{1,0:T(8,128)S(1)}, u32[]{:S(2)}, u32[]{:S(2)}) collective-permute-start(f32[16,512]{1,0:T(8,128)S(1)} %get-tuple-element.15), channel_id=1, source_target_pairs={{0,56},{8,0},{16,8},{24,16},{32,24},{40,32},{48,40},{56,48},{64,12... | collective-permute-start | bytes 98312 | tf_op jit(solution)/shard_map/ppermute | solution.py:171
  38.9 15.5 %collective-permute-start.10 = (f32[16,512]{1,0:T(8,128)S(1)}, f32[16,512]{1,0:T(8,128)S(1)}, u32[]{:S(2)}, u32[]{:S(2)}) collective-permute-start(f32[16,512]{1,0:T(8,128)S(1)} %multiply_add_fusion.1), channel_id=1, source_target_pairs={{0,192},{8,200},{16,208},{24,216},{32,224},{40,232},{48,240},{56,2... | collective-permute-start | bytes 98312 | tf_op jit(solution)/shard_map/ppermute | solution.py:24
  39.6 14.8 %collective-permute-start.8 = (f32[16,512]{1,0:T(8,128)S(1)}, f32[16,512]{1,0:T(8,128)S(1)}, u32[]{:S(2)}, u32[]{:S(2)}) collective-permute-start(f32[16,512]{1,0:T(8,128)S(1)} %multiply_add_fusion.1), channel_id=1, source_target_pairs={{0,64},{8,72},{16,80},{24,88},{32,96},{40,104},{48,112},{56,120},{... | collective-permute-start | bytes 98312 | tf_op jit(solution)/shard_map/ppermute | solution.py:24
  42.6 11.8 %collective-permute-start.9 = (f32[16,512]{1,0:T(8,128)S(1)}, f32[16,512]{1,0:T(8,128)S(1)}, u32[]{:S(2)}, u32[]{:S(2)}) collective-permute-start(f32[16,512]{1,0:T(8,128)S(1)} %multiply_add_fusion.1), channel_id=1, source_target_pairs={{0,128},{8,136},{16,144},{24,152},{32,160},{40,168},{48,176},{56,1... | collective-permute-start | bytes 98312 | tf_op jit(solution)/shard_map/ppermute | solution.py:24
  60.5 32.2 %copy-start = (bf16[512,512]{1,0:T(8,128)(2,1)S(1)}, bf16[512,512]{1,0:T(8,128)(2,1)}, u32[]{:S(2)}) copy-start(bf16[512,512]{1,0:T(8,128)(2,1)} %shard_map.88) | copy-start | bytes 1572868
  60.5 29.8 %collective-permute-start.11 = (bf16[512,512]{1,0:T(8,128)(2,1)}, bf16[512,512]{1,0:T(8,128)(2,1)S(1)}, u32[]{:S(2)}, u32[]{:S(2)}) collective-permute-start(bf16[512,512]{1,0:T(8,128)(2,1)} %shard_map.88), channel_id=1, source_target_pairs={{1,0},{2,1},{3,2},{4,3},{5,4},{6,5},{7,6},{0,7},{9,8},{10,9},{11,1... | collective-permute-start | bytes 1572872 | tf_op jit(solution)/shard_map/ppermute | solution.py:228
  63.9 28.7 %collective-permute-start.12 = (bf16[512,512]{1,0:T(8,128)(2,1)}, bf16[512,512]{1,0:T(8,128)(2,1)S(1)}, u32[]{:S(2)}, u32[]{:S(2)}) collective-permute-start(bf16[512,512]{1,0:T(8,128)(2,1)} %shard_map.88), channel_id=1, source_target_pairs={{2,0},{3,1},{4,2},{5,3},{6,4},{7,5},{0,6},{1,7},{10,8},{11,9},{12,... | collective-permute-start | bytes 1572872 | tf_op jit(solution)/shard_map/ppermute | solution.py:228
  64.7 46.8 %collective-permute-start.13 = (bf16[512,512]{1,0:T(8,128)(2,1)}, bf16[512,512]{1,0:T(8,128)(2,1)S(1)}, u32[]{:S(2)}, u32[]{:S(2)}) collective-permute-start(bf16[512,512]{1,0:T(8,128)(2,1)} %shard_map.88), channel_id=1, source_target_pairs={{3,0},{4,1},{5,2},{6,3},{7,4},{0,5},{1,6},{2,7},{11,8},{12,9},{13,... | collective-permute-start | bytes 1572872 | tf_op jit(solution)/shard_map/ppermute | solution.py:228
  65.6 46.0 %collective-permute-start.14 = (bf16[512,512]{1,0:T(8,128)(2,1)}, bf16[512,512]{1,0:T(8,128)(2,1)S(1)}, u32[]{:S(2)}, u32[]{:S(2)}) collective-permute-start(bf16[512,512]{1,0:T(8,128)(2,1)} %shard_map.88), channel_id=1, source_target_pairs={{4,0},{5,1},{6,2},{7,3},{0,4},{1,5},{2,6},{3,7},{12,8},{13,9},{14,... | collective-permute-start | bytes 1572872 | tf_op jit(solution)/shard_map/ppermute | solution.py:228
  68.6 47.9 %collective-permute-start.15 = (bf16[512,512]{1,0:T(8,128)(2,1)}, bf16[512,512]{1,0:T(8,128)(2,1)S(1)}, u32[]{:S(2)}, u32[]{:S(2)}) collective-permute-start(bf16[512,512]{1,0:T(8,128)(2,1)} %shard_map.88), channel_id=1, source_target_pairs={{5,0},{6,1},{7,2},{0,3},{1,4},{2,5},{3,6},{4,7},{13,8},{14,9},{15,... | collective-permute-start | bytes 1572872 | tf_op jit(solution)/shard_map/ppermute | solution.py:228
  90.3 38.5 %collective-permute-start.16 = (bf16[512,512]{1,0:T(8,128)(2,1)}, bf16[512,512]{1,0:T(8,128)(2,1)S(1)}, u32[]{:S(2)}, u32[]{:S(2)}) collective-permute-start(bf16[512,512]{1,0:T(8,128)(2,1)} %shard_map.88), channel_id=1, source_target_pairs={{6,0},{7,1},{0,2},{1,3},{2,4},{3,5},{4,6},{5,7},{14,8},{15,9},{8,1... | collective-permute-start | bytes 1572872 | tf_op jit(solution)/shard_map/ppermute | solution.py:228
  92.6 36.2 %collective-permute-start.17 = (bf16[512,512]{1,0:T(8,128)(2,1)S(1)}, bf16[512,512]{1,0:T(8,128)(2,1)S(1)}, u32[]{:S(2)}, u32[]{:S(2)}) collective-permute-start(bf16[512,512]{1,0:T(8,128)(2,1)S(1)} %copy-done), channel_id=1, source_target_pairs={{7,0},{0,1},{1,2},{2,3},{3,4},{4,5},{5,6},{6,7},{15,8},{8,9},{9,10... | collective-permute-start | bytes 1572872 | tf_op jit(solution)/shard_map/ppermute | solution.py:228
  141.3 17.7 %collective-permute-start.18 = (bf16[512,512]{1,0:T(8,128)(2,1)S(1)}, bf16[512,512]{1,0:T(8,128)(2,1)}, u32[]{:S(2)}, u32[]{:S(2)}) collective-permute-start(bf16[512,512]{1,0:T(8,128)(2,1)S(1)} %slice.61), channel_id=1, source_target_pairs={{0,8},{8,16},{16,24},{24,32},{32,40},{40,48},{48,56},{56,64},{64,7... | collective-permute-start | bytes 1572872 | tf_op jit(solution)/shard_map/ppermute | solution.py:24
  159.0 20.5 %collective-permute-start.19 = (bf16[512,512]{1,0:T(8,128)(2,1)}, bf16[512,512]{1,0:T(8,128)(2,1)}, u32[]{:S(2)}, u32[]{:S(2)}) collective-permute-start(bf16[512,512]{1,0:T(8,128)(2,1)} %collective-permute-done.18), channel_id=1, source_target_pairs={{0,8},{8,16},{16,24},{24,32},{32,40},{40,48},{48,56},{56,64},{64,7... | collective-permute-start | bytes 1572872 | tf_op jit(solution)/shard_map/ppermute | solution.py:24
  (6 other events, 8.9 us)
Sparse Core Ops, SparseCore 0:
  11.0 75.3 all-gather.1
where the time goes:
time: 195 us; the launch traced here: 194 us
  waiting for transfers between devices  72.6 us (37%)
  starting transfers between devices  46.8 us (24%)
  Pallas kernels  24.3 us (12%)
  local copies, waits for them, and re-layouts  20.4 us (10%)
  between operations  14.7 us (8%)
  matrix products  12.2 us (6%)
  other arithmetic  3.33 us (2%)
    ppermute x7, waiting for transfers between devices, block_body(): lax.ppermute(mixer, 'tp', [((source + shift) % parts, source) for source...  37.6 us
    ppermute x6, waiting for transfers between devices, from_behind(): lax.ppermute(value, axis, [(source, source + steps) for source in range(l...  33.2 us
    ppermute x7, starting transfers between devices, block_body(): lax.ppermute(mixer, 'tp', [((source + shift) % parts, source) for source...  29.1 us
    unnamed x37, local copies, waits for them, and re-layouts  11.7 us
    ppermute x6, starting transfers between devices, from_behind(): lax.ppermute(value, axis, [(source, source + steps) for source in range(l...  10.9 us
    pallas_call x1, Pallas kernels, intra_call(): pl.pallas_call(intra_kernel, out_shape=whole((tokens, channels), jnp.floa...  10.4 us
    pallas_call x1, Pallas kernels, front_call(): pl.pallas_call(front_kernel, out_shape=(whole((tokens, channels), jnp.flo...  8.79 us
    dot_general x1, matrix products, block_body(): jnp.dot(normed, flat_rows, preferred_element_type=jnp.float32)  7.53 us
  transfers between devices with their start and end apart: 21, of which 8 were waited for; matrix products, arithmetic and copies ran while one was open for 8% of the time, Pallas kernels for 12%

commit v1 on v0

--- a/solution.py
+++ b/solution.py
@@ -205,8 +205,26 @@
     return jnp.stack(entering, axis=1), carry
 
 
+def gather_channels(block):
+    parts = lax.axis_size("tp")
+    me = lax.axis_index("tp")
+    channels = block.shape[1]
+    partner = lax.ppermute(block, "tp", [(source, source ^ 1) for source in range(parts)])
+    low = me % 2 == 0
+    pair = jnp.where(low, jnp.concatenate([block, partner], axis=1), jnp.concatenate([partner, block], axis=1))
+    rings = parts // 2
+    pieces = [pair] + [
+        lax.ppermute(pair, "tp", [(source, (source + 2 * shift) % parts) for source in range(parts)])
+        for shift in range(1, rings)
+    ]
+    ordered = [pieces[(-place) % rings] for place in range(rings)]
+    doubled = jnp.concatenate(ordered + ordered, axis=1)
+    first_pair = ((rings - me // 2) % rings) * 2 * channels
+    return lax.dynamic_slice_in_dim(doubled, first_pair, parts * channels, 1)
+
+
 def block_body(features, short_filter, decay_rate, residue, skip_gain, norm_gain, qkv_weight):
-    tok_dev, _, channels = features.shape
+    tok_dev, _, _ = features.shape
     head_cols = qkv_weight.shape[2]
     shard_rows = lax.all_gather(qkv_weight, "ctx", axis=0, tiled=True)
     rim_rows = features[tok_dev - (TAPS - 1) :]
@@ -222,14 +240,7 @@
     total_state = entering + lead * history[:, None, :]
     mixer = finish_call(intra, total_state, decay3, mixing3, gated, first, skip_gain[None])
 
-    parts = lax.axis_size("tp")
-    me = lax.axis_index("tp")
-    pieces = [mixer] + [
-        lax.ppermute(mixer, "tp", [((source + shift) % parts, source) for source in range(parts)])
-        for shift in range(1, parts)
-    ]
-    doubled = jnp.concatenate(pieces + pieces, axis=1)
-    gathered = lax.dynamic_slice_in_dim(doubled, ((parts - me) % parts) * channels, parts * channels, 1)
+    gathered = gather_channels(mixer)
     as_float = gathered.astype(jnp.float32)
     inverse = lax.rsqrt(jnp.mean(as_float * as_float, axis=1, keepdims=True) + EPSILON)
     normed = (as_float * inverse * norm_gain[None]).astype(jnp.bfloat16)

time: 195 us -> 219 us (1.12)
  waiting for transfers between devices: 72.6 us -> 109 us
  starting transfers between devices: 46.8 us -> 24.4 us
  other arithmetic: 3.33 us -> 8.36 us
  local copies, waits for them, and re-layouts: 20.4 us -> 25.1 us
    ppermute x7 -> x4, waiting for transfers between devices: 37.6 us -> 73.4 us  [the longest x3 45.1 us: gather_channels(): lax.ppermute(pair, 'tp', [(source, (source + 2 * shift) % parts) for sour...]
    ppermute x7 -> x4, starting transfers between devices: 29.1 us -> 6.87 us  [the longest x3 5.85 us: gather_channels(): lax.ppermute(pair, 'tp', [(source, (source + 2 * shift) % parts) for sour...]
    unnamed x0 -> x1, other arithmetic: none -> 2.82 us
    unnamed x37 -> x24, local copies, waits for them, and re-layouts: 11.7 us -> 14.1 us
    concatenate x1, local copies, waits for them, and re-layouts: 0.06 us -> 2.33 us  [gather_channels(): doubled = jnp.concatenate(ordered + ordered, axis=1)]
    reduce_sum x1, other arithmetic: 0.89 us -> 3.09 us  [block_body(): jnp.mean(as_float * as_float, axis=1, keepdims=True) + EPSILON]
  transfers between devices with their start and end apart: 21 -> 18, of which waited for: 8 -> 8; matrix products, arithmetic and copies ran while one was open for 8% -> 13% of each run, Pallas kernels for 12% -> 11%
where the time goes in v1:
time: 219 us; the launch traced here: 218 us
  waiting for transfers between devices  109 us (50%)
  local copies, waits for them, and re-layouts  25.1 us (11%)
  starting transfers between devices  24.4 us (11%)
  Pallas kernels  24.2 us (11%)
  between operations  14.5 us (7%)
  matrix products  12.2 us (6%)
  other arithmetic  8.36 us (4%)
    ppermute x3, waiting for transfers between devices, gather_channels(): lax.ppermute(pair, 'tp', [(source, (source + 2 * shift) % parts) for sour...  45.1 us
    ppermute x6, waiting for transfers between devices, from_behind(): lax.ppermute(value, axis, [(source, source + steps) for source in range(l...  34.2 us
    ppermute x1, waiting for transfers between devices, gather_channels(): lax.ppermute(block, 'tp', [(source, source ^ 1) for source in range(parts)])  28.3 us
    unnamed x24, local copies, waits for them, and re-layouts  14.1 us
    ppermute x6, starting transfers between devices, from_behind(): lax.ppermute(value, axis, [(source, source + steps) for source in range(l...  10.7 us
    pallas_call x1, Pallas kernels, intra_call(): pl.pallas_call(intra_kernel, out_shape=whole((tokens, channels), jnp.floa...  10.4 us
    pallas_call x1, Pallas kernels, front_call(): pl.pallas_call(front_kernel, out_shape=(whole((tokens, channels), jnp.flo...  8.79 us
    dot_general x1, matrix products, block_body(): jnp.dot(normed, flat_rows, preferred_element_type=jnp.float32)  7.53 us
  transfers between devices with their start and end apart: 18, of which 8 were waited for; matrix products, arithmetic and copies ran while one was open for 13% of the time, Pallas kernels for 11%

profile of v1, /device:TPU:128, one launch (start us, length us, event | category | flops | bytes accessed | tf_op | source)
XLA Modules:
  0.0 218.2 jit_solution(1637752522496169136)
XLA Ops:
  7.2 1.7 copy.37
  9.7 1.9 collective-permute-start
  11.7 1.7 copy.29
  14.0 1.6 copy.30.feat_ref
  15.6 3.5 %collective-permute-done = bf16[6,3,512]{2,0,1:T(8,128)(2,1)S(1)} collective-permute-done((bf16[6,3,512]{2,0,1:T(8,128)(2,1)S(1)}, bf16[6,3,512]{2,0,1:T(8,128)(2,1)S(1)}, u32[]{:S(2)}, u32[]{:S(2)}) %collective-permute-start) | collective-permute-done | bytes 18464 | tf_op jit(solution)/shard_map/ppermute | solution.py:24
  19.7 8.8 %shard_map.86 = (f32[512,512]{1,0:T(8,128)}, f32[512,512]{1,0:T(8,128)}, f32[16,4,512]{2,1,0:T(4,128)}) custom-call(bf16[512,1536]{1,0:T(8,128)(2,1)} %copy.30.feat_ref, bf16[6,1536]{1,0:T(8,128)(2,1)} %bitcast.99, f32[3,7,512]{2,1,0:T(8,128)} %taps_ref.1, f32[16,1,512]{2,1,0:T(1,128)} %broadcast_in_dim.56.decay_ref), custom_call_target="tpu_custom_call" | custom-call | flops 19398656 | bytes 3670016 | tf_op jit(solution)/shard_map/pallas_call | solution.py:98
  29.7 4.2 %collective-permute-start.4 = (f32[16,512]{1,0:T(8,128)S(1)}, f32[16,512]{1,0:T(8,128)S(1)}, u32[]{:S(2)}, u32[]{:S(2)}) collective-permute-start(f32[16,512]{1,0:T(8,128)S(1)} %get-tuple-element.17), channel_id=1, source_target_pairs={{0,32},{8,40},{16,48},{24,56},{32,0},{40,8},{48,16},{56,24},{64,96... | collective-permute-start | bytes 98312 | tf_op jit(solution)/shard_map/ppermute | solution.py:171
  39.6 3.0 %collective-permute-start.8 = (f32[16,512]{1,0:T(8,128)S(1)}, f32[16,512]{1,0:T(8,128)S(1)}, u32[]{:S(2)}, u32[]{:S(2)}) collective-permute-start(f32[16,512]{1,0:T(8,128)S(1)} %multiply_add_fusion.1), channel_id=1, source_target_pairs={{0,64},{8,72},{16,80},{24,88},{32,96},{40,104},{48,112},{56,120},{... | collective-permute-start | bytes 98312 | tf_op jit(solution)/shard_map/ppermute | solution.py:24
  43.9 10.4 %shard_map.87.intra_ref = f32[512,512]{1,0:T(8,128)} custom-call(f32[512,512]{1,0:T(8,128)} %get-tuple-element.5.gated_ref, f32[16,1,512]{2,1,0:T(1,128)} %broadcast_in_dim.56.decay_ref, f32[16,1,512]{2,1,0:T(1,128)} %broadcast_in_dim.57.mixing_ref), custom_call_target="tpu_custom_call" | custom-call | flops 2147483648 | bytes 2097152 | tf_op jit(solution)/shard_map/pallas_call | solution.py:146
  55.4 5.1 %shard_map.88 = bf16[512,512]{1,0:T(8,128)(2,1)} custom-call(f32[512,512]{1,0:T(8,128)} %shard_map.87.intra_ref, f32[16,4,512]{2,1,0:T(4,128)} %maximum_add_fusion.state_ref, f32[16,1,512]{2,1,0:T(1,128)} %broadcast_in_dim.56.decay_ref, f32[16,1,512]{2,1,0:T(1,128)} %broadcast_in_dim.57.mixing_ref, f32[512,512]{1,0:T(8,128)} %get-tuple-element.5.gated_ref, ...), custom_call_target="tpu_custom_call" | custom-call | flops 8388608 | bytes 3670016 | tf_op jit(solution)/shard_map/pallas_call | solution.py:185
  61.5 28.3 %collective-permute-done.11 = bf16[512,512]{1,0:T(8,128)(2,1)S(1)} collective-permute-done((bf16[512,512]{1,0:T(8,128)(2,1)}, bf16[512,512]{1,0:T(8,128)(2,1)S(1)}, u32[]{:S(2)}, u32[]{:S(2)}) %collective-permute-start.11) | collective-permute-done | bytes 524320 | tf_op jit(solution)/shard_map/ppermute | solution.py:212
  89.7 2.8 %constant_dynamic-update-slice_fusion.7 = (bf16[512,8192]{1,0:T(8,128)(2,1)}, bf16[512,1024]{1,0:T(8,128)(2,1)S(1)}) fusion(bf16[512,512]{1,0:T(8,128)(2,1)} %shard_map.88, bf16[512,512]{1,0:T(8,128)(2,1)S(1)} %collective-permute-done.11, pred[]{:T(512)S(6)} %eq.14), kind=kLoop, calls=%fused_computation.84 | loop fusion | flops 4718591 | bytes 3145729
  92.6 4.2 %collective-permute-start.12 = (bf16[512,1024]{1,0:T(8,128)(2,1)S(1)}, bf16[512,1024]{1,0:T(8,128)(2,1)S(1)}, u32[]{:S(2)}, u32[]{:S(2)}) collective-permute-start(bf16[512,1024]{1,0:T(8,128)(2,1)S(1)} %get-tuple-element.16), channel_id=1, source_target_pairs={{0,6},{1,7},{2,0},{3,1},{4,2},{5,3},{6,4},{7,5},{8,14},{9,15},{10,... | collective-permute-start | bytes 3145736 | tf_op jit(solution)/shard_map/ppermute | solution.py:217
  98.5 43.4 %collective-permute-done.12 = bf16[512,1024]{1,0:T(8,128)(2,1)S(1)} collective-permute-done((bf16[512,1024]{1,0:T(8,128)(2,1)S(1)}, bf16[512,1024]{1,0:T(8,128)(2,1)S(1)}, u32[]{:S(2)}, u32[]{:S(2)}) %collective-permute-start.12) | collective-permute-done | bytes 1048608 | tf_op jit(solution)/shard_map/ppermute | solution.py:217
  144.0 1.7 collective-permute-done.14
  145.7 2.3 %constant_dynamic-update-slice_fusion.4 = bf16[512,8192]{1,0:T(8,128)(2,1)} fusion(bf16[512,8192]{1,0:T(8,128)(2,1)} %constant_dynamic-update-slice_fusion.5, bf16[512,1024]{1,0:T(8,128)(2,1)} %collective-permute-done.14), kind=kLoop, calls=%fused_computation.81 | loop fusion | bytes 2097152
  151.3 2.3 %constant_dynamic-update-slice_fusion = bf16[512,8192]{1,0:T(8,128)(2,1)} fusion(bf16[512,8192]{1,0:T(8,128)(2,1)} %constant_dynamic-update-slice_fusion.1, bf16[512,1024]{1,0:T(8,128)(2,1)} %collective-permute-done.14), kind=kLoop, calls=%fused_computation.77 | loop fusion | bytes 2097152 | tf_op jit(solution)/shard_map/concatenate | solution.py:221
  153.6 3.1 %fusion = f32[512]{0:T(512)S(1)} fusion(bf16[512,8192]{1,0:T(8,128)(2,1)} %constant_dynamic-update-slice_fusion, s32[]{:T(128)S(6)} %select_n.139), kind=kLoop, calls=%fused_computation.2 | loop fusion | flops 6290944 | bytes 4196356 | tf_op jit(solution)/shard_map/reduce_sum | solution.py:245
  156.7 7.5 %fusion.17 = bf16[512,768]{1,0:T(8,128)(2,1)S(1)} fusion(bf16[4096,768]{0,1:T(8,128)(2,1)} %bitcast.98, f32[4096]{0:T(1024)S(1)} %copy-done.6, f32[512]{0:T(512)S(1)} %add_rsqrt_fusion, bf16[512,8192]{1,0:T(8,128)(2,1)} %constant_dynamic-update-slice_fusion, s32[]{:T(128)S(6)} %select_n.139), kind=kOutput, calls=%fused_computation.24 | convolution fusion | flops 3230007296 | bytes 11290628 | tf_op jit(solution)/shard_map/dot_general | solution.py:248
  164.3 1.9 collective-permute-start.15
  167.2 1.9 fusion.8
  169.1 14.1 %collective-permute-done.15 = bf16[512,512]{1,0:T(8,128)(2,1)} collective-permute-done((bf16[512,512]{1,0:T(8,128)(2,1)S(1)}, bf16[512,512]{1,0:T(8,128)(2,1)}, u32[]{:S(2)}, u32[]{:S(2)}) %collective-permute-start.15) | collective-permute-done | bytes 524320 | tf_op jit(solution)/shard_map/ppermute | solution.py:24
  183.2 1.9 collective-permute-start.16
  186.8 16.6 %collective-permute-done.16 = bf16[512,512]{1,0:T(8,128)(2,1)} collective-permute-done((bf16[512,512]{1,0:T(8,128)(2,1)}, bf16[512,512]{1,0:T(8,128)(2,1)}, u32[]{:S(2)}, u32[]{:S(2)}) %collective-permute-start.16) | collective-permute-done | bytes 524320 | tf_op jit(solution)/shard_map/ppermute | solution.py:24
  (75 shorter events, 29.8 us)
Async XLA Ops:
  7.2 6.2 %copy-start.1 = (f32[16,512]{1,0:T(8,128)S(1)}, f32[16,512]{1,0:T(8,128)}, u32[]{:S(2)}) copy-start(f32[16,512]{1,0:T(8,128)} %param.9) | copy-start | bytes 98308
  7.2 149.5 %all-gather.2.cloned.1.call-start = ((), (), s32[]{:S(2)}) async-start(), calls=%async_computation | async-start | bytes 6488064 | tf_op jit(solution)/shard_map/all_gather | solution.py:229
  9.7 9.4 %collective-permute-start = (bf16[6,3,512]{2,0,1:T(8,128)(2,1)S(1)}, bf16[6,3,512]{2,0,1:T(8,128)(2,1)S(1)}, u32[]{:S(2)}, u32[]{:S(2)}) collective-permute-start(bf16[6,3,512]{2,0,1:T(8,128)(2,1)S(1)} %slice.41), channel_id=1, source_target_pairs={{0,8},{8,16},{16,24},{24,32},{32,40},{40,48},{48,56},{56,64},{64,7... | collective-permute-start | bytes 55304 | tf_op jit(solution)/shard_map/ppermute | solution.py:24
  15.6 20.8 %copy-start.4 = (f32[16,512]{1,0:T(8,128)S(1)}, f32[16,512]{1,0:T(8,128)}, u32[]{:S(2)}) copy-start(f32[16,512]{1,0:T(8,128)} %param.10) | copy-start | bytes 98308
  29.5 5.2 %collective-permute-start.1 = (f32[16,512]{1,0:T(8,128)S(1)}, f32[16,512]{1,0:T(8,128)S(1)}, u32[]{:S(2)}, u32[]{:S(2)}) collective-permute-start(f32[16,512]{1,0:T(8,128)S(1)} %get-tuple-element.17), channel_id=1, source_target_pairs={{0,8},{8,16},{16,24},{24,32},{32,40},{40,48},{48,56},{56,0},{64,72... | collective-permute-start | bytes 98312 | tf_op jit(solution)/shard_map/ppermute | solution.py:171
  29.5 6.8 %collective-permute-start.2 = (f32[16,512]{1,0:T(8,128)S(1)}, f32[16,512]{1,0:T(8,128)S(1)}, u32[]{:S(2)}, u32[]{:S(2)}) collective-permute-start(f32[16,512]{1,0:T(8,128)S(1)} %get-tuple-element.17), channel_id=1, source_target_pairs={{0,16},{8,24},{16,32},{24,40},{32,48},{40,56},{48,0},{56,8},{64,80... | collective-permute-start | bytes 98312 | tf_op jit(solution)/shard_map/ppermute | solution.py:171
  29.6 7.5 %collective-permute-start.3 = (f32[16,512]{1,0:T(8,128)S(1)}, f32[16,512]{1,0:T(8,128)S(1)}, u32[]{:S(2)}, u32[]{:S(2)}) collective-permute-start(f32[16,512]{1,0:T(8,128)S(1)} %get-tuple-element.17), channel_id=1, source_target_pairs={{0,24},{8,32},{16,40},{24,48},{32,56},{40,0},{48,8},{56,16},{64,88... | collective-permute-start | bytes 98312 | tf_op jit(solution)/shard_map/ppermute | solution.py:171
  29.7 7.4 %collective-permute-start.4 = (f32[16,512]{1,0:T(8,128)S(1)}, f32[16,512]{1,0:T(8,128)S(1)}, u32[]{:S(2)}, u32[]{:S(2)}) collective-permute-start(f32[16,512]{1,0:T(8,128)S(1)} %get-tuple-element.17), channel_id=1, source_target_pairs={{0,32},{8,40},{16,48},{24,56},{32,0},{40,8},{48,16},{56,24},{64,96... | collective-permute-start | bytes 98312 | tf_op jit(solution)/shard_map/ppermute | solution.py:171
  33.9 3.4 %collective-permute-start.5 = (f32[16,512]{1,0:T(8,128)S(1)}, f32[16,512]{1,0:T(8,128)S(1)}, u32[]{:S(2)}, u32[]{:S(2)}) collective-permute-start(f32[16,512]{1,0:T(8,128)S(1)} %get-tuple-element.17), channel_id=1, source_target_pairs={{0,40},{8,48},{16,56},{24,0},{32,8},{40,16},{48,24},{56,32},{64,10... | collective-permute-start | bytes 98312 | tf_op jit(solution)/shard_map/ppermute | solution.py:171
  34.7 4.2 %collective-permute-start.6 = (f32[16,512]{1,0:T(8,128)S(1)}, f32[16,512]{1,0:T(8,128)S(1)}, u32[]{:S(2)}, u32[]{:S(2)}) collective-permute-start(f32[16,512]{1,0:T(8,128)S(1)} %get-tuple-element.17), channel_id=1, source_target_pairs={{0,48},{8,56},{16,0},{24,8},{32,16},{40,24},{48,32},{56,40},{64,11... | collective-permute-start | bytes 98312 | tf_op jit(solution)/shard_map/ppermute | solution.py:171
  36.3 2.6 %collective-permute-start.7 = (f32[16,512]{1,0:T(8,128)S(1)}, f32[16,512]{1,0:T(8,128)S(1)}, u32[]{:S(2)}, u32[]{:S(2)}) collective-permute-start(f32[16,512]{1,0:T(8,128)S(1)} %get-tuple-element.17), channel_id=1, source_target_pairs={{0,56},{8,0},{16,8},{24,16},{32,24},{40,32},{48,40},{56,48},{64,12... | collective-permute-start | bytes 98312 | tf_op jit(solution)/shard_map/ppermute | solution.py:171
  38.9 15.5 %collective-permute-start.10 = (f32[16,512]{1,0:T(8,128)S(1)}, f32[16,512]{1,0:T(8,128)S(1)}, u32[]{:S(2)}, u32[]{:S(2)}) collective-permute-start(f32[16,512]{1,0:T(8,128)S(1)} %multiply_add_fusion.1), channel_id=1, source_target_pairs={{0,192},{8,200},{16,208},{24,216},{32,224},{40,232},{48,240},{56,2... | collective-permute-start | bytes 98312 | tf_op jit(solution)/shard_map/ppermute | solution.py:24
  39.6 14.8 %collective-permute-start.8 = (f32[16,512]{1,0:T(8,128)S(1)}, f32[16,512]{1,0:T(8,128)S(1)}, u32[]{:S(2)}, u32[]{:S(2)}) collective-permute-start(f32[16,512]{1,0:T(8,128)S(1)} %multiply_add_fusion.1), channel_id=1, source_target_pairs={{0,64},{8,72},{16,80},{24,88},{32,96},{40,104},{48,112},{56,120},{... | collective-permute-start | bytes 98312 | tf_op jit(solution)/shard_map/ppermute | solution.py:24
  42.6 11.8 %collective-permute-start.9 = (f32[16,512]{1,0:T(8,128)S(1)}, f32[16,512]{1,0:T(8,128)S(1)}, u32[]{:S(2)}, u32[]{:S(2)}) collective-permute-start(f32[16,512]{1,0:T(8,128)S(1)} %multiply_add_fusion.1), channel_id=1, source_target_pairs={{0,128},{8,136},{16,144},{24,152},{32,160},{40,168},{48,176},{56,1... | collective-permute-start | bytes 98312 | tf_op jit(solution)/shard_map/ppermute | solution.py:24
  60.4 29.3 %collective-permute-start.11 = (bf16[512,512]{1,0:T(8,128)(2,1)}, bf16[512,512]{1,0:T(8,128)(2,1)S(1)}, u32[]{:S(2)}, u32[]{:S(2)}) collective-permute-start(bf16[512,512]{1,0:T(8,128)(2,1)} %shard_map.88), channel_id=1, source_target_pairs={{0,1},{1,0},{2,3},{3,2},{4,5},{5,4},{6,7},{7,6},{8,9},{9,8},{10,11... | collective-permute-start | bytes 1572872 | tf_op jit(solution)/shard_map/ppermute | solution.py:212
  92.6 49.4 %collective-permute-start.12 = (bf16[512,1024]{1,0:T(8,128)(2,1)S(1)}, bf16[512,1024]{1,0:T(8,128)(2,1)S(1)}, u32[]{:S(2)}, u32[]{:S(2)}) collective-permute-start(bf16[512,1024]{1,0:T(8,128)(2,1)S(1)} %get-tuple-element.16), channel_id=1, source_target_pairs={{0,6},{1,7},{2,0},{3,1},{4,2},{5,3},{6,4},{7,5},{8,14},{9,15},{10,... | collective-permute-start | bytes 3145736 | tf_op jit(solution)/shard_map/ppermute | solution.py:217
  96.8 46.2 %collective-permute-start.13 = (bf16[512,1024]{1,0:T(8,128)(2,1)S(1)}, bf16[512,1024]{1,0:T(8,128)(2,1)S(1)}, u32[]{:S(2)}, u32[]{:S(2)}) collective-permute-start(bf16[512,1024]{1,0:T(8,128)(2,1)S(1)} %get-tuple-element.16), channel_id=1, source_target_pairs={{0,4},{1,5},{2,6},{3,7},{4,0},{5,1},{6,2},{7,3},{8,12},{9,13},{10,... | collective-permute-start | bytes 3145736 | tf_op jit(solution)/shard_map/ppermute | solution.py:217
  97.4 48.3 %collective-permute-start.14 = (bf16[512,1024]{1,0:T(8,128)(2,1)S(1)}, bf16[512,1024]{1,0:T(8,128)(2,1)}, u32[]{:S(2)}, u32[]{:S(2)}) collective-permute-start(bf16[512,1024]{1,0:T(8,128)(2,1)S(1)} %get-tuple-element.16), channel_id=1, source_target_pairs={{0,2},{1,3},{2,4},{3,5},{4,6},{5,7},{6,0},{7,1},{8,10},{9,11},{10,... | collective-permute-start | bytes 3145736 | tf_op jit(solution)/shard_map/ppermute | solution.py:217
  153.6 3.1 %copy-start.6 = (f32[4096]{0:T(1024)S(1)}, f32[4096]{0:T(1024)}, u32[]{:S(2)}) copy-start(f32[4096]{0:T(1024)} %param.12) | copy-start | bytes 49156
  164.3 18.9 %collective-permute-start.15 = (bf16[512,512]{1,0:T(8,128)(2,1)S(1)}, bf16[512,512]{1,0:T(8,128)(2,1)}, u32[]{:S(2)}, u32[]{:S(2)}) collective-permute-start(bf16[512,512]{1,0:T(8,128)(2,1)S(1)} %slice.61), channel_id=1, source_target_pairs={{0,8},{8,16},{16,24},{24,32},{32,40},{40,48},{48,56},{56,64},{64,7... | collective-permute-start | bytes 1572872 | tf_op jit(solution)/shard_map/ppermute | solution.py:24
  183.2 20.2 %collective-permute-start.16 = (bf16[512,512]{1,0:T(8,128)(2,1)}, bf16[512,512]{1,0:T(8,128)(2,1)}, u32[]{:S(2)}, u32[]{:S(2)}) collective-permute-start(bf16[512,512]{1,0:T(8,128)(2,1)} %collective-permute-done.15), channel_id=1, source_target_pairs={{0,8},{8,16},{16,24},{24,32},{32,40},{40,48},{48,56},{56,64},{64,7... | collective-permute-start | bytes 1572872 | tf_op jit(solution)/shard_map/ppermute | solution.py:24
  205.4 1.6 copy-start
  205.4 1.6 copy-start.2
  209.0 1.0 copy-start.3
  (1 other events, 0.6 us)
Sparse Core Ops, SparseCore 0:
  11.0 79.2 all-gather.1

commit v2 on v0

--- a/solution.py
+++ b/solution.py
@@ -223,13 +223,8 @@
     mixer = finish_call(intra, total_state, decay3, mixing3, gated, first, skip_gain[None])
 
     parts = lax.axis_size("tp")
-    me = lax.axis_index("tp")
-    pieces = [mixer] + [
-        lax.ppermute(mixer, "tp", [((source + shift) % parts, source) for source in range(parts)])
-        for shift in range(1, parts)
-    ]
-    doubled = jnp.concatenate(pieces + pieces, axis=1)
-    gathered = lax.dynamic_slice_in_dim(doubled, ((parts - me) % parts) * channels, parts * channels, 1)
+    copies = jnp.broadcast_to(mixer[None], (parts, tok_dev, channels))
+    gathered = lax.all_to_all(copies, "tp", 0, 2, tiled=True).reshape(tok_dev, parts * channels)
     as_float = gathered.astype(jnp.float32)
     inverse = lax.rsqrt(jnp.mean(as_float * as_float, axis=1, keepdims=True) + EPSILON)
     normed = (as_float * inverse * norm_gain[None]).astype(jnp.bfloat16)

time: 195 us -> 195 us (level)
  starting transfers between devices: 46.8 us -> 22.6 us
  waiting for transfers between devices: 72.6 us -> 92.3 us
  other arithmetic: 3.33 us -> 9.73 us
    all_to_all x0 -> x1, waiting for transfers between devices: none -> 58.3 us  [block_body(): lax.all_to_all(copies, 'tp', 0, 2, tiled=True)]
    ppermute x7 -> x0, waiting for transfers between devices: 37.6 us -> none  [block_body(): lax.ppermute(mixer, 'tp', [((source + shift) % parts, source) for source...]
    ppermute x7 -> x0, starting transfers between devices: 29.1 us -> none  [block_body(): lax.ppermute(mixer, 'tp', [((source + shift) % parts, source) for source...]
    unnamed x37 -> x18, local copies, waits for them, and re-layouts: 11.7 us -> 6.47 us
    all_to_all x0 -> x1, starting transfers between devices: none -> 5.05 us  [block_body(): lax.all_to_all(copies, 'tp', 0, 2, tiled=True)]
    convert_element_type x0 -> x1, other arithmetic: none -> 4.16 us  [block_body(): normed = (as_float * inverse * norm_gain[None]).astype(jnp.bfloat16)]
    broadcast_in_dim x0 -> x1, local copies, waits for them, and re-layouts: none -> 2.4 us  [block_body(): copies = jnp.broadcast_to(mixer[None], (parts, tok_dev, channels))]
    reduce_sum x1, other arithmetic: 0.89 us -> 3.14 us  [block_body(): jnp.mean(as_float * as_float, axis=1, keepdims=True) + EPSILON]
  transfers between devices with their start and end apart: 21 -> 15, of which waited for: 8 -> 6; matrix products, arithmetic and copies ran while one was open for 8% -> 12% of each run, Pallas kernels for 12% -> 13%
where the time goes in v2:
time: 195 us; the launch traced here: 194 us
  waiting for transfers between devices  92.3 us (47%)
  Pallas kernels  24.3 us (12%)
  starting transfers between devices  22.6 us (12%)
  local copies, waits for them, and re-layouts  18.7 us (10%)
  between operations  14.5 us (7%)
  matrix products  12.2 us (6%)
  other arithmetic  9.73 us (5%)
    all_to_all x1, waiting for transfers between devices, block_body(): lax.all_to_all(copies, 'tp', 0, 2, tiled=True)  58.3 us
    ppermute x6, waiting for transfers between devices, from_behind(): lax.ppermute(value, axis, [(source, source + steps) for source in range(l...  32.2 us
    ppermute x6, starting transfers between devices, from_behind(): lax.ppermute(value, axis, [(source, source + steps) for source in range(l...  10.7 us
    pallas_call x1, Pallas kernels, intra_call(): pl.pallas_call(intra_kernel, out_shape=whole((tokens, channels), jnp.floa...  10.4 us
    pallas_call x1, Pallas kernels, front_call(): pl.pallas_call(front_kernel, out_shape=(whole((tokens, channels), jnp.flo...  8.87 us
    dot_general x1, matrix products, block_body(): jnp.dot(normed, flat_rows, preferred_element_type=jnp.float32)  7.52 us
    ppermute x7, starting transfers between devices, exchange_history(): arrived = lax.ppermute(block_end, 'ctx', pairs)  6.77 us
    unnamed x18, local copies, waits for them, and re-layouts  6.47 us
  transfers between devices with their start and end apart: 15, of which 6 were waited for; matrix products, arithmetic and copies ran while one was open for 12% of the time, Pallas kernels for 13%

profile of v2, /device:TPU:128, one launch (start us, length us, event | category | flops | bytes accessed | tf_op | source)
XLA Modules:
  0.0 194.4 jit_solution(369212359929409534)
XLA Ops:
  7.2 1.7 copy.38
  9.7 1.9 collective-permute-start
  11.7 1.7 copy.29
  14.0 1.6 copy.30.feat_ref
  15.6 3.5 %collective-permute-done = bf16[6,3,512]{2,0,1:T(8,128)(2,1)S(1)} collective-permute-done((bf16[6,3,512]{2,0,1:T(8,128)(2,1)S(1)}, bf16[6,3,512]{2,0,1:T(8,128)(2,1)S(1)}, u32[]{:S(2)}, u32[]{:S(2)}) %collective-permute-start) | collective-permute-done | bytes 18464 | tf_op jit(solution)/shard_map/ppermute | solution.py:24
  19.7 8.9 %shard_map.86 = (f32[512,512]{1,0:T(8,128)}, f32[512,512]{1,0:T(8,128)}, f32[16,4,512]{2,1,0:T(4,128)}) custom-call(bf16[512,1536]{1,0:T(8,128)(2,1)} %copy.30.feat_ref, bf16[6,1536]{1,0:T(8,128)(2,1)} %bitcast.108, f32[3,7,512]{2,1,0:T(8,128)} %taps_ref.1, f32[16,1,512]{2,1,0:T(1,128)} %broadcast_in_dim.62.decay_ref), custom_call_target="tpu_custom_call" | custom-call | flops 19398656 | bytes 3670016 | tf_op jit(solution)/shard_map/pallas_call | solution.py:98
  29.8 4.2 %collective-permute-start.4 = (f32[16,512]{1,0:T(8,128)S(1)}, f32[16,512]{1,0:T(8,128)S(1)}, u32[]{:S(2)}, u32[]{:S(2)}) collective-permute-start(f32[16,512]{1,0:T(8,128)S(1)} %get-tuple-element.15), channel_id=1, source_target_pairs={{0,32},{8,40},{16,48},{24,56},{32,0},{40,8},{48,16},{56,24},{64,96... | collective-permute-start | bytes 98312 | tf_op jit(solution)/shard_map/ppermute | solution.py:171
  34.7 1.6 collective-permute-start.6
  37.3 1.6 collective-permute-done.6
  39.7 2.9 %collective-permute-start.8 = (f32[16,512]{1,0:T(8,128)S(1)}, f32[16,512]{1,0:T(8,128)S(1)}, u32[]{:S(2)}, u32[]{:S(2)}) collective-permute-start(f32[16,512]{1,0:T(8,128)S(1)} %multiply_add_fusion.1), channel_id=1, source_target_pairs={{0,64},{8,72},{16,80},{24,88},{32,96},{40,104},{48,112},{56,120},{... | collective-permute-start | bytes 98312 | tf_op jit(solution)/shard_map/ppermute | solution.py:24
  43.9 10.4 %shard_map.87.intra_ref = f32[512,512]{1,0:T(8,128)} custom-call(f32[512,512]{1,0:T(8,128)} %get-tuple-element.5.gated_ref, f32[16,1,512]{2,1,0:T(1,128)} %broadcast_in_dim.62.decay_ref, f32[16,1,512]{2,1,0:T(1,128)} %broadcast_in_dim.63.mixing_ref), custom_call_target="tpu_custom_call" | custom-call | flops 2147483648 | bytes 2097152 | tf_op jit(solution)/shard_map/pallas_call | solution.py:146
  55.4 5.1 %shard_map.88 = bf16[512,512]{1,0:T(8,128)(2,1)} custom-call(f32[512,512]{1,0:T(8,128)} %shard_map.87.intra_ref, f32[16,4,512]{2,1,0:T(4,128)} %maximum_add_fusion.state_ref, f32[16,1,512]{2,1,0:T(1,128)} %broadcast_in_dim.62.decay_ref, f32[16,1,512]{2,1,0:T(1,128)} %broadcast_in_dim.63.mixing_ref, f32[512,512]{1,0:T(8,128)} %get-tuple-element.5.gated_ref, ...), custom_call_target="tpu_custom_call" | custom-call | flops 8388608 | bytes 3670016 | tf_op jit(solution)/shard_map/pallas_call | solution.py:185
  61.7 2.4 %broadcast_in_dim.66 = bf16[8,512,512]{1,2,0:T(8,128)(2,1)} broadcast(bf16[512,512]{0,1:T(8,128)(2,1)S(1)} %copy.37), dimensions={1,2} | broadcast | bytes 4718592 | tf_op jit(solution)/shard_map/broadcast_in_dim | solution.py:226
  64.1 5.1 %all-to-all-start = ((bf16[8,512,512]{1,2,0:T(8,128)(2,1)}), bf16[8,512,512]{1,2,0:T(8,128)(2,1)}, u32[]{:S(2)}, u32[]{:S(2)}) async-start(bf16[8,512,512]{1,2,0:T(8,128)(2,1)} %broadcast_in_dim.66), calls=%async_computation | async-start | bytes 8388608 | tf_op jit(solution)/shard_map/all_to_all | solution.py:227
  69.3 58.3 %all-to-all-done = bf16[8,512,512]{1,2,0:T(8,128)(2,1)} async-done(((bf16[8,512,512]{1,2,0:T(8,128)(2,1)}), bf16[8,512,512]{1,2,0:T(8,128)(2,1)}, u32[]{:S(2)}, u32[]{:S(2)}) %all-to-all-start) | async-done | bytes 4194336 | tf_op jit(solution)/shard_map/all_to_all | solution.py:227
  127.6 3.1 %fusion = f32[512]{0:T(512)S(1)} fusion(bf16[8,512,512]{1,2,0:T(8,128)(2,1)} %all-to-all-done), kind=kLoop, calls=%fused_computation.2 | loop fusion | flops 6290944 | bytes 4196352 | tf_op jit(solution)/shard_map/reduce_sum | solution.py:229
  130.7 4.2 %fusion.2 = bf16[8,1,512,512]{2,3,0,1:T(8,128)(2,1)} fusion(bf16[8,512,512]{1,2,0:T(8,128)(2,1)} %all-to-all-done, f32[8,512]{1,0:T(8,128)S(1)} %mul.381, f32[512]{0:T(512)S(1)} %add_rsqrt_fusion), kind=kLoop, calls=%fused_computation.4 | loop fusion | flops 8388608 | bytes 8407040 | tf_op jit(solution)/shard_map/convert_element_type | solution.py:230
  134.9 7.5 %convolution_convert_fusion = bf16[512,768]{1,0:T(8,128)(2,1)S(1)} fusion(bf16[512,4096]{0,1:T(8,128)(2,1)} %bitcast.101, bf16[4096,768]{0,1:T(8,128)(2,1)} %bitcast.107), kind=kOutput, calls=%fused_computation.20 | convolution fusion | flops 3221618688 | bytes 11272192 | tf_op jit(solution)/shard_map/dot_general | solution.py:232
  142.5 2.0 %collective-permute-start.11 = (bf16[512,512]{1,0:T(8,128)(2,1)S(1)}, bf16[512,512]{1,0:T(8,128)(2,1)}, u32[]{:S(2)}, u32[]{:S(2)}) collective-permute-start(bf16[512,512]{1,0:T(8,128)(2,1)S(1)} %slice.61), channel_id=1, source_target_pairs={{0,8},{8,16},{16,24},{24,32},{32,40},{40,48},{48,56},{56,64},{64,7... | collective-permute-start | bytes 1572872 | tf_op jit(solution)/shard_map/ppermute | solution.py:24
  145.4 1.9 fusion.3
  147.3 11.7 %collective-permute-done.11 = bf16[512,512]{1,0:T(8,128)(2,1)} collective-permute-done((bf16[512,512]{1,0:T(8,128)(2,1)S(1)}, bf16[512,512]{1,0:T(8,128)(2,1)}, u32[]{:S(2)}, u32[]{:S(2)}) %collective-permute-start.11) | collective-permute-done | bytes 524320 | tf_op jit(solution)/shard_map/ppermute | solution.py:24
  158.9 1.9 collective-permute-start.12
  162.5 17.0 %collective-permute-done.12 = bf16[512,512]{1,0:T(8,128)(2,1)} collective-permute-done((bf16[512,512]{1,0:T(8,128)(2,1)}, bf16[512,512]{1,0:T(8,128)(2,1)}, u32[]{:S(2)}, u32[]{:S(2)}) %collective-permute-start.12) | collective-permute-done | bytes 524320 | tf_op jit(solution)/shard_map/ppermute | solution.py:24
  183.8 1.3 fusion.8
  (65 shorter events, 18.4 us)
Async XLA Ops:
  7.2 6.2 %copy-start.1 = (f32[16,512]{1,0:T(8,128)S(1)}, f32[16,512]{1,0:T(8,128)}, u32[]{:S(2)}) copy-start(f32[16,512]{1,0:T(8,128)} %param.9) | copy-start | bytes 98308
  7.2 127.7 %all-gather.2.cloned.1.call-start = ((), (), s32[]{:S(2)}) async-start(), calls=%async_computation.1 | async-start | bytes 6488064 | tf_op jit(solution)/shard_map/all_gather | solution.py:211
  9.7 9.4 %collective-permute-start = (bf16[6,3,512]{2,0,1:T(8,128)(2,1)S(1)}, bf16[6,3,512]{2,0,1:T(8,128)(2,1)S(1)}, u32[]{:S(2)}, u32[]{:S(2)}) collective-permute-start(bf16[6,3,512]{2,0,1:T(8,128)(2,1)S(1)} %slice.41), channel_id=1, source_target_pairs={{0,8},{8,16},{16,24},{24,32},{32,40},{40,48},{48,56},{56,64},{64,7... | collective-permute-start | bytes 55304 | tf_op jit(solution)/shard_map/ppermute | solution.py:24
  15.6 21.0 %copy-start.4 = (f32[16,512]{1,0:T(8,128)S(1)}, f32[16,512]{1,0:T(8,128)}, u32[]{:S(2)}) copy-start(f32[16,512]{1,0:T(8,128)} %param.10) | copy-start | bytes 98308
  19.1 0.6 copy-start.6
  29.5 5.2 %collective-permute-start.1 = (f32[16,512]{1,0:T(8,128)S(1)}, f32[16,512]{1,0:T(8,128)S(1)}, u32[]{:S(2)}, u32[]{:S(2)}) collective-permute-start(f32[16,512]{1,0:T(8,128)S(1)} %get-tuple-element.15), channel_id=1, source_target_pairs={{0,8},{8,16},{16,24},{24,32},{32,40},{40,48},{48,56},{56,0},{64,72... | collective-permute-start | bytes 98312 | tf_op jit(solution)/shard_map/ppermute | solution.py:171
  29.6 6.8 %collective-permute-start.2 = (f32[16,512]{1,0:T(8,128)S(1)}, f32[16,512]{1,0:T(8,128)S(1)}, u32[]{:S(2)}, u32[]{:S(2)}) collective-permute-start(f32[16,512]{1,0:T(8,128)S(1)} %get-tuple-element.15), channel_id=1, source_target_pairs={{0,16},{8,24},{16,32},{24,40},{32,48},{40,56},{48,0},{56,8},{64,80... | collective-permute-start | bytes 98312 | tf_op jit(solution)/shard_map/ppermute | solution.py:171
  29.7 7.5 %collective-permute-start.3 = (f32[16,512]{1,0:T(8,128)S(1)}, f32[16,512]{1,0:T(8,128)S(1)}, u32[]{:S(2)}, u32[]{:S(2)}) collective-permute-start(f32[16,512]{1,0:T(8,128)S(1)} %get-tuple-element.15), channel_id=1, source_target_pairs={{0,24},{8,32},{16,40},{24,48},{32,56},{40,0},{48,8},{56,16},{64,88... | collective-permute-start | bytes 98312 | tf_op jit(solution)/shard_map/ppermute | solution.py:171
  29.8 7.5 %collective-permute-start.4 = (f32[16,512]{1,0:T(8,128)S(1)}, f32[16,512]{1,0:T(8,128)S(1)}, u32[]{:S(2)}, u32[]{:S(2)}) collective-permute-start(f32[16,512]{1,0:T(8,128)S(1)} %get-tuple-element.15), channel_id=1, source_target_pairs={{0,32},{8,40},{16,48},{24,56},{32,0},{40,8},{48,16},{56,24},{64,96... | collective-permute-start | bytes 98312 | tf_op jit(solution)/shard_map/ppermute | solution.py:171
  34.0 3.4 %collective-permute-start.5 = (f32[16,512]{1,0:T(8,128)S(1)}, f32[16,512]{1,0:T(8,128)S(1)}, u32[]{:S(2)}, u32[]{:S(2)}) collective-permute-start(f32[16,512]{1,0:T(8,128)S(1)} %get-tuple-element.15), channel_id=1, source_target_pairs={{0,40},{8,48},{16,56},{24,0},{32,8},{40,16},{48,24},{56,32},{64,10... | collective-permute-start | bytes 98312 | tf_op jit(solution)/shard_map/ppermute | solution.py:171
  34.7 4.2 %collective-permute-start.6 = (f32[16,512]{1,0:T(8,128)S(1)}, f32[16,512]{1,0:T(8,128)S(1)}, u32[]{:S(2)}, u32[]{:S(2)}) collective-permute-start(f32[16,512]{1,0:T(8,128)S(1)} %get-tuple-element.15), channel_id=1, source_target_pairs={{0,48},{8,56},{16,0},{24,8},{32,16},{40,24},{48,32},{56,40},{64,11... | collective-permute-start | bytes 98312 | tf_op jit(solution)/shard_map/ppermute | solution.py:171
  36.3 2.6 %collective-permute-start.7 = (f32[16,512]{1,0:T(8,128)S(1)}, f32[16,512]{1,0:T(8,128)S(1)}, u32[]{:S(2)}, u32[]{:S(2)}) collective-permute-start(f32[16,512]{1,0:T(8,128)S(1)} %get-tuple-element.15), channel_id=1, source_target_pairs={{0,56},{8,0},{16,8},{24,16},{32,24},{40,32},{48,40},{56,48},{64,12... | collective-permute-start | bytes 98312 | tf_op jit(solution)/shard_map/ppermute | solution.py:171
  39.0 15.4 %collective-permute-start.10 = (f32[16,512]{1,0:T(8,128)S(1)}, f32[16,512]{1,0:T(8,128)S(1)}, u32[]{:S(2)}, u32[]{:S(2)}) collective-permute-start(f32[16,512]{1,0:T(8,128)S(1)} %multiply_add_fusion.1), channel_id=1, source_target_pairs={{0,192},{8,200},{16,208},{24,216},{32,224},{40,232},{48,240},{56,2... | collective-permute-start | bytes 98312 | tf_op jit(solution)/shard_map/ppermute | solution.py:24
  39.7 14.8 %collective-permute-start.8 = (f32[16,512]{1,0:T(8,128)S(1)}, f32[16,512]{1,0:T(8,128)S(1)}, u32[]{:S(2)}, u32[]{:S(2)}) collective-permute-start(f32[16,512]{1,0:T(8,128)S(1)} %multiply_add_fusion.1), channel_id=1, source_target_pairs={{0,64},{8,72},{16,80},{24,88},{32,96},{40,104},{48,112},{56,120},{... | collective-permute-start | bytes 98312 | tf_op jit(solution)/shard_map/ppermute | solution.py:24
  42.6 11.8 %collective-permute-start.9 = (f32[16,512]{1,0:T(8,128)S(1)}, f32[16,512]{1,0:T(8,128)S(1)}, u32[]{:S(2)}, u32[]{:S(2)}) collective-permute-start(f32[16,512]{1,0:T(8,128)S(1)} %multiply_add_fusion.1), channel_id=1, source_target_pairs={{0,128},{8,136},{16,144},{24,152},{32,160},{40,168},{48,176},{56,1... | collective-permute-start | bytes 98312 | tf_op jit(solution)/shard_map/ppermute | solution.py:24
  64.1 5.1 %copy-start.5 = (f32[4096]{0:T(1024)S(1)}, f32[4096]{0:T(1024)}, u32[]{:S(2)}) copy-start(f32[4096]{0:T(1024)} %param.12) | copy-start | bytes 49156
  64.1 63.5 %all-to-all-start = ((bf16[8,512,512]{1,2,0:T(8,128)(2,1)}), bf16[8,512,512]{1,2,0:T(8,128)(2,1)}, u32[]{:S(2)}, u32[]{:S(2)}) async-start(bf16[8,512,512]{1,2,0:T(8,128)(2,1)} %broadcast_in_dim.66), calls=%async_computation | async-start | bytes 8388608 | tf_op jit(solution)/shard_map/all_to_all | solution.py:227
  142.5 16.5 %collective-permute-start.11 = (bf16[512,512]{1,0:T(8,128)(2,1)S(1)}, bf16[512,512]{1,0:T(8,128)(2,1)}, u32[]{:S(2)}, u32[]{:S(2)}) collective-permute-start(bf16[512,512]{1,0:T(8,128)(2,1)S(1)} %slice.61), channel_id=1, source_target_pairs={{0,8},{8,16},{16,24},{24,32},{32,40},{40,48},{48,56},{56,64},{64,7... | collective-permute-start | bytes 1572872 | tf_op jit(solution)/shard_map/ppermute | solution.py:24
  158.9 20.6 %collective-permute-start.12 = (bf16[512,512]{1,0:T(8,128)(2,1)}, bf16[512,512]{1,0:T(8,128)(2,1)}, u32[]{:S(2)}, u32[]{:S(2)}) collective-permute-start(bf16[512,512]{1,0:T(8,128)(2,1)} %collective-permute-done.11), channel_id=1, source_target_pairs={{0,8},{8,16},{16,24},{24,32},{32,40},{40,48},{48,56},{56,64},{64,7... | collective-permute-start | bytes 1572872 | tf_op jit(solution)/shard_map/ppermute | solution.py:24
  181.5 1.6 copy-start
  181.5 1.6 copy-start.2
  185.1 1.0 copy-start.3
Sparse Core Ops, SparseCore 0:
  11.0 72.1 all-gather.1

commit v3 on v2

--- a/solution.py
+++ b/solution.py
@@ -209,6 +209,7 @@
     tok_dev, _, channels = features.shape
     head_cols = qkv_weight.shape[2]
     shard_rows = lax.all_gather(qkv_weight, "ctx", axis=0, tiled=True)
+    flat_rows = shard_rows.reshape(shard_rows.shape[0], 3 * head_cols)
     rim_rows = features[tok_dev - (TAPS - 1) :]
     before = from_behind(rim_rows, "ctx", 1)
     decay3 = decay_rate[:, None, :]
@@ -223,13 +224,18 @@
     mixer = finish_call(intra, total_state, decay3, mixing3, gated, first, skip_gain[None])
 
     parts = lax.axis_size("tp")
-    copies = jnp.broadcast_to(mixer[None], (parts, tok_dev, channels))
-    gathered = lax.all_to_all(copies, "tp", 0, 2, tiled=True).reshape(tok_dev, parts * channels)
-    as_float = gathered.astype(jnp.float32)
-    inverse = lax.rsqrt(jnp.mean(as_float * as_float, axis=1, keepdims=True) + EPSILON)
-    normed = (as_float * inverse * norm_gain[None]).astype(jnp.bfloat16)
-    flat_rows = shard_rows.reshape(shard_rows.shape[0], 3 * head_cols)
-    projected = jnp.dot(normed, flat_rows, preferred_element_type=jnp.float32).astype(jnp.bfloat16)
+    half = tok_dev // 4
+    gathered_top = lax.all_gather(mixer[:half], "tp", axis=1, tiled=True)
+    copies = jnp.broadcast_to(mixer[None, half:], (parts, tok_dev - half, channels))
+    gathered_low = lax.all_to_all(copies, "tp", 0, 2, tiled=True).reshape(tok_dev - half, parts * channels)
+
+    def project(gathered):
+        as_float = gathered.astype(jnp.float32)
+        inverse = lax.rsqrt(jnp.mean(as_float * as_float, axis=1, keepdims=True) + EPSILON)
+        normed = (as_float * inverse * norm_gain[None]).astype(jnp.bfloat16)
+        return jnp.dot(normed, flat_rows, preferred_element_type=jnp.float32).astype(jnp.bfloat16)
+
+    projected = jnp.concatenate([project(gathered_top), project(gathered_low)], axis=0)
     heads = head_cols // HD
     query = projected[:, :head_cols].reshape(tok_dev, heads, HD)
     kv_pair = projected[:, head_cols:]

time: 195 us -> 253 us (1.30)
  waiting for transfers between devices: 92.3 us -> 152 us
  other arithmetic: 9.73 us -> 6.99 us
    all_gather x1, waiting for transfers between devices: 0.01 us -> 60.4 us  [block_body(): shard_rows = lax.all_gather(qkv_weight, 'ctx', axis=0, tiled=True)]
    all_to_all x1, waiting for transfers between devices: 58.3 us -> 9.32 us  [block_body(): lax.all_to_all(copies, 'tp', 0, 2, tiled=True)]
    all_gather x0 -> x1, waiting for transfers between devices: none -> 46.2 us  [block_body(): gathered_top = lax.all_gather(mixer[:half], 'tp', axis=1, tiled=True)]
    slice x1 -> x3, local copies, waits for them, and re-layouts: 0.04 us -> 2.81 us  [the longest x1 1.57 us: block_body(): gathered_top = lax.all_gather(mixer[:half], 'tp', axis=1, tiled=True)]
    dot_general x1 -> x2, matrix products: 7.52 us -> 8.77 us  [project(): jnp.dot(normed, flat_rows, preferred_element_type=jnp.float32)]
    unnamed x18 -> x23, local copies, waits for them, and re-layouts: 6.47 us -> 5.46 us
  transfers between devices with their start and end apart: 15 -> 16, of which waited for: 6 -> 10; matrix products, arithmetic and copies ran while one was open for 12% -> 7% of each run, Pallas kernels for 13% -> 4%
where the time goes in v3:
time: 253 us; the launch traced here: 252 us
  waiting for transfers between devices  152 us (60%)
  Pallas kernels  24.3 us (10%)
  starting transfers between devices  22 us (9%)
  local copies, waits for them, and re-layouts  18.9 us (7%)
  between operations  14.3 us (6%)
  matrix products  13.4 us (5%)
  other arithmetic  6.99 us (3%)
    all_gather x1, waiting for transfers between devices, block_body(): shard_rows = lax.all_gather(qkv_weight, 'ctx', axis=0, tiled=True)  60.4 us
    all_gather x1, waiting for transfers between devices, block_body(): gathered_top = lax.all_gather(mixer[:half], 'tp', axis=1, tiled=True)  46.2 us
    ppermute x6, waiting for transfers between devices, from_behind(): lax.ppermute(value, axis, [(source, source + steps) for source in range(l...  32.4 us
    ppermute x6, starting transfers between devices, from_behind(): lax.ppermute(value, axis, [(source, source + steps) for source in range(l...  11.1 us
    pallas_call x1, Pallas kernels, intra_call(): pl.pallas_call(intra_kernel, out_shape=whole((tokens, channels), jnp.floa...  10.4 us
    all_to_all x1, waiting for transfers between devices, block_body(): lax.all_to_all(copies, 'tp', 0, 2, tiled=True)  9.32 us
    pallas_call x1, Pallas kernels, front_call(): pl.pallas_call(front_kernel, out_shape=(whole((tokens, channels), jnp.flo...  8.79 us
    dot_general x2, matrix products, project(): jnp.dot(normed, flat_rows, preferred_element_type=jnp.float32)  8.77 us
  transfers between devices with their start and end apart: 16, of which 10 were waited for; matrix products, arithmetic and copies ran while one was open for 7% of the time, Pallas kernels for 4%

profile of v3, /device:TPU:128, one launch (start us, length us, event | category | flops | bytes accessed | tf_op | source)
XLA Modules:
  0.0 252.2 jit_solution(7059414126541975374)
XLA Ops:
  8.0 1.9 collective-permute-start
  9.9 1.7 copy.29
  11.6 1.6 copy.30.feat_ref
  13.9 3.4 %collective-permute-done = bf16[6,3,512]{2,0,1:T(8,128)(2,1)S(1)} collective-permute-done((bf16[6,3,512]{2,0,1:T(8,128)(2,1)S(1)}, bf16[6,3,512]{2,0,1:T(8,128)(2,1)S(1)}, u32[]{:S(2)}, u32[]{:S(2)}) %collective-permute-start) | collective-permute-done | bytes 18464 | tf_op jit(solution)/shard_map/ppermute | solution.py:24
  17.9 8.8 %shard_map.86 = (f32[512,512]{1,0:T(8,128)}, f32[512,512]{1,0:T(8,128)}, f32[16,4,512]{2,1,0:T(4,128)}) custom-call(bf16[512,1536]{1,0:T(8,128)(2,1)} %copy.30.feat_ref, bf16[6,1536]{1,0:T(8,128)(2,1)} %bitcast.110, f32[3,7,512]{2,1,0:T(8,128)} %taps_ref.1, f32[16,1,512]{2,1,0:T(1,128)} %broadcast_in_dim.64.decay_ref), custom_call_target="tpu_custom_call" | custom-call | flops 19398656 | bytes 3670016 | tf_op jit(solution)/shard_map/pallas_call | solution.py:98
  28.8 2.6 %collective-permute-start.4 = (f32[16,512]{1,0:T(8,128)S(1)}, f32[16,512]{1,0:T(8,128)S(1)}, u32[]{:S(2)}, u32[]{:S(2)}) collective-permute-start(f32[16,512]{1,0:T(8,128)S(1)} %get-tuple-element.15), channel_id=1, source_target_pairs={{0,32},{8,40},{16,48},{24,56},{32,0},{40,8},{48,16},{56,24},{64,96... | collective-permute-start | bytes 98312 | tf_op jit(solution)/shard_map/ppermute | solution.py:171
  31.5 1.6 collective-permute-start.2
  34.5 2.2 collective-permute-done.3
  40.0 3.1 %collective-permute-start.8 = (f32[16,512]{1,0:T(8,128)S(1)}, f32[16,512]{1,0:T(8,128)S(1)}, u32[]{:S(2)}, u32[]{:S(2)}) collective-permute-start(f32[16,512]{1,0:T(8,128)S(1)} %multiply_add_fusion.1), channel_id=1, source_target_pairs={{0,64},{8,72},{16,80},{24,88},{32,96},{40,104},{48,112},{56,120},{... | collective-permute-start | bytes 98312 | tf_op jit(solution)/shard_map/ppermute | solution.py:24
  43.1 10.4 %shard_map.87.intra_ref = f32[512,512]{1,0:T(8,128)} custom-call(f32[512,512]{1,0:T(8,128)} %get-tuple-element.5.gated_ref, f32[16,1,512]{2,1,0:T(1,128)} %broadcast_in_dim.64.decay_ref, f32[16,1,512]{2,1,0:T(1,128)} %broadcast_in_dim.65.mixing_ref), custom_call_target="tpu_custom_call" | custom-call | flops 2147483648 | bytes 2097152 | tf_op jit(solution)/shard_map/pallas_call | solution.py:146
  54.6 5.1 %shard_map.88 = bf16[512,512]{1,0:T(8,128)(2,1)} custom-call(f32[512,512]{1,0:T(8,128)} %shard_map.87.intra_ref, f32[16,4,512]{2,1,0:T(4,128)} %maximum_add_fusion.state_ref, f32[16,1,512]{2,1,0:T(1,128)} %broadcast_in_dim.64.decay_ref, f32[16,1,512]{2,1,0:T(1,128)} %broadcast_in_dim.65.mixing_ref, f32[512,512]{1,0:T(8,128)} %get-tuple-element.5.gated_ref, ...), custom_call_target="tpu_custom_call" | custom-call | flops 8388608 | bytes 3670016 | tf_op jit(solution)/shard_map/pallas_call | solution.py:185
  63.4 2.0 broadcast_in_dim.68
  65.4 5.1 %all-to-all-start = ((bf16[8,384,512]{1,2,0:T(8,128)(2,1)}), bf16[8,384,512]{1,2,0:T(8,128)(2,1)S(1)}, u32[]{:S(2)}, u32[]{:S(2)}) async-start(bf16[8,384,512]{1,2,0:T(8,128)(2,1)} %broadcast_in_dim.68), calls=%async_computation | async-start | bytes 6291456 | tf_op jit(solution)/shard_map/all_to_all | solution.py:230
  70.5 46.2 %all-gather.3.cloned.1.call-done = bf16[128,4096]{1,0:T(8,128)(2,1)} async-done(((bf16[128,512]{1,0:T(8,128)(2,1)}), bf16[128,4096]{1,0:T(8,128)(2,1)}) %all-gather.3.cloned.1.call-update) | async-done | bytes 1048592 | tf_op jit(solution)/shard_map/all_gather | solution.py:228
  118.3 9.3 %all-to-all-done = bf16[8,384,512]{1,2,0:T(8,128)(2,1)S(1)} async-done(((bf16[8,384,512]{1,2,0:T(8,128)(2,1)}), bf16[8,384,512]{1,2,0:T(8,128)(2,1)S(1)}, u32[]{:S(2)}, u32[]{:S(2)}) %all-to-all-start) | async-done | bytes 3145760 | tf_op jit(solution)/shard_map/all_to_all | solution.py:230
  128.3 2.1 fusion.2
  130.5 60.4 %all-gather.5.cloned.1.call-done = bf16[4096,3,256]{0,2,1:T(8,128)(2,1)} async-done(((bf16[128,3,256]{0,2,1:T(8,128)(2,1)}), bf16[4096,3,256]{0,2,1:T(8,128)(2,1)}) %all-gather.5.cloned.1.call-update) | async-done | bytes 6291472 | tf_op jit(solution)/shard_map/all_gather | solution.py:211
  190.9 6.5 %convolution_convert_fusion = bf16[384,768]{1,0:T(8,128)(2,1)S(1)} fusion(bf16[384,4096]{0,1:T(8,128)(2,1)} %bitcast.102, bf16[4096,768]{0,1:T(8,128)(2,1)} %bitcast.108), kind=kOutput, calls=%fused_computation.25 | convolution fusion | flops 2416214016 | bytes 10027008 | tf_op jit(solution)/shard_map/dot_general | solution.py:236
  197.4 2.2 convolution_convert_fusion.1
  199.7 2.2 collective-permute-start.11
  202.9 1.9 fusion.6
  204.8 11.8 %collective-permute-done.11 = bf16[512,512]{1,0:T(8,128)(2,1)} collective-permute-done((bf16[512,512]{1,0:T(8,128)(2,1)S(1)}, bf16[512,512]{1,0:T(8,128)(2,1)}, u32[]{:S(2)}, u32[]{:S(2)}) %collective-permute-start.11) | collective-permute-done | bytes 524320 | tf_op jit(solution)/shard_map/ppermute | solution.py:24
  216.6 1.9 collective-permute-start.12
  220.2 17.1 %collective-permute-done.12 = bf16[512,512]{1,0:T(8,128)(2,1)} collective-permute-done((bf16[512,512]{1,0:T(8,128)(2,1)}, bf16[512,512]{1,0:T(8,128)(2,1)}, u32[]{:S(2)}, u32[]{:S(2)}) %collective-permute-start.12) | collective-permute-done | bytes 524320 | tf_op jit(solution)/shard_map/ppermute | solution.py:24
  (79 shorter events, 26.5 us)
Async XLA Ops:
  7.2 109.6 %all-gather.3.cloned.1.call-start = ((), (), s32[]{:S(2)}) async-start(), calls=%async_computation.1 | async-start | bytes 1179648 | tf_op jit(solution)/shard_map/all_gather | solution.py:228
  8.0 9.4 %collective-permute-start = (bf16[6,3,512]{2,0,1:T(8,128)(2,1)S(1)}, bf16[6,3,512]{2,0,1:T(8,128)(2,1)S(1)}, u32[]{:S(2)}, u32[]{:S(2)}) collective-permute-start(bf16[6,3,512]{2,0,1:T(8,128)(2,1)S(1)} %slice.47), channel_id=1, source_target_pairs={{0,8},{8,16},{16,24},{24,32},{32,40},{40,48},{48,56},{56,64},{64,7... | collective-permute-start | bytes 55304 | tf_op jit(solution)/shard_map/ppermute | solution.py:24
  11.6 1.6 copy-start.2
  13.2 20.3 %copy-start.6 = (f32[16,512]{1,0:T(8,128)S(1)}, f32[16,512]{1,0:T(8,128)}, u32[]{:S(2)}) copy-start(f32[16,512]{1,0:T(8,128)} %param.10) | copy-start | bytes 98308
  27.7 3.8 %collective-permute-start.7 = (f32[16,512]{1,0:T(8,128)S(1)}, f32[16,512]{1,0:T(8,128)S(1)}, u32[]{:S(2)}, u32[]{:S(2)}) collective-permute-start(f32[16,512]{1,0:T(8,128)S(1)} %get-tuple-element.15), channel_id=1, source_target_pairs={{0,56},{8,0},{16,8},{24,16},{32,24},{40,32},{48,40},{56,48},{64,12... | collective-permute-start | bytes 98312 | tf_op jit(solution)/shard_map/ppermute | solution.py:171
  28.1 5.0 %collective-permute-start.6 = (f32[16,512]{1,0:T(8,128)S(1)}, f32[16,512]{1,0:T(8,128)S(1)}, u32[]{:S(2)}, u32[]{:S(2)}) collective-permute-start(f32[16,512]{1,0:T(8,128)S(1)} %get-tuple-element.15), channel_id=1, source_target_pairs={{0,48},{8,56},{16,0},{24,8},{32,16},{40,24},{48,32},{56,40},{64,11... | collective-permute-start | bytes 98312 | tf_op jit(solution)/shard_map/ppermute | solution.py:171
  28.8 5.4 %collective-permute-start.5 = (f32[16,512]{1,0:T(8,128)S(1)}, f32[16,512]{1,0:T(8,128)S(1)}, u32[]{:S(2)}, u32[]{:S(2)}) collective-permute-start(f32[16,512]{1,0:T(8,128)S(1)} %get-tuple-element.15), channel_id=1, source_target_pairs={{0,40},{8,48},{16,56},{24,0},{32,8},{40,16},{48,24},{56,32},{64,10... | collective-permute-start | bytes 98312 | tf_op jit(solution)/shard_map/ppermute | solution.py:171
  28.8 5.7 %collective-permute-start.4 = (f32[16,512]{1,0:T(8,128)S(1)}, f32[16,512]{1,0:T(8,128)S(1)}, u32[]{:S(2)}, u32[]{:S(2)}) collective-permute-start(f32[16,512]{1,0:T(8,128)S(1)} %get-tuple-element.15), channel_id=1, source_target_pairs={{0,32},{8,40},{16,48},{24,56},{32,0},{40,8},{48,16},{56,24},{64,96... | collective-permute-start | bytes 98312 | tf_op jit(solution)/shard_map/ppermute | solution.py:171
  31.5 5.2 %collective-permute-start.3 = (f32[16,512]{1,0:T(8,128)S(1)}, f32[16,512]{1,0:T(8,128)S(1)}, u32[]{:S(2)}, u32[]{:S(2)}) collective-permute-start(f32[16,512]{1,0:T(8,128)S(1)} %get-tuple-element.15), channel_id=1, source_target_pairs={{0,24},{8,32},{16,40},{24,48},{32,56},{40,0},{48,8},{56,16},{64,88... | collective-permute-start | bytes 98312 | tf_op jit(solution)/shard_map/ppermute | solution.py:171
  31.5 6.3 %collective-permute-start.2 = (f32[16,512]{1,0:T(8,128)S(1)}, f32[16,512]{1,0:T(8,128)S(1)}, u32[]{:S(2)}, u32[]{:S(2)}) collective-permute-start(f32[16,512]{1,0:T(8,128)S(1)} %get-tuple-element.15), channel_id=1, source_target_pairs={{0,16},{8,24},{16,32},{24,40},{32,48},{40,56},{48,0},{56,8},{64,80... | collective-permute-start | bytes 98312 | tf_op jit(solution)/shard_map/ppermute | solution.py:171
  33.1 4.8 %collective-permute-start.1 = (f32[16,512]{1,0:T(8,128)S(1)}, f32[16,512]{1,0:T(8,128)S(1)}, u32[]{:S(2)}, u32[]{:S(2)}) collective-permute-start(f32[16,512]{1,0:T(8,128)S(1)} %get-tuple-element.15), channel_id=1, source_target_pairs={{0,8},{8,16},{16,24},{24,32},{32,40},{40,48},{48,56},{56,0},{64,72... | collective-permute-start | bytes 98312 | tf_op jit(solution)/shard_map/ppermute | solution.py:171
  38.0 15.6 %collective-permute-start.10 = (f32[16,512]{1,0:T(8,128)S(1)}, f32[16,512]{1,0:T(8,128)S(1)}, u32[]{:S(2)}, u32[]{:S(2)}) collective-permute-start(f32[16,512]{1,0:T(8,128)S(1)} %multiply_add_fusion.1), channel_id=1, source_target_pairs={{0,192},{8,200},{16,208},{24,216},{32,224},{40,232},{48,240},{56,2... | collective-permute-start | bytes 98312 | tf_op jit(solution)/shard_map/ppermute | solution.py:24
  38.7 15.0 %collective-permute-start.9 = (f32[16,512]{1,0:T(8,128)S(1)}, f32[16,512]{1,0:T(8,128)S(1)}, u32[]{:S(2)}, u32[]{:S(2)}) collective-permute-start(f32[16,512]{1,0:T(8,128)S(1)} %multiply_add_fusion.1), channel_id=1, source_target_pairs={{0,128},{8,136},{16,144},{24,152},{32,160},{40,168},{48,176},{56,1... | collective-permute-start | bytes 98312 | tf_op jit(solution)/shard_map/ppermute | solution.py:24
  40.0 13.7 %collective-permute-start.8 = (f32[16,512]{1,0:T(8,128)S(1)}, f32[16,512]{1,0:T(8,128)S(1)}, u32[]{:S(2)}, u32[]{:S(2)}) collective-permute-start(f32[16,512]{1,0:T(8,128)S(1)} %multiply_add_fusion.1), channel_id=1, source_target_pairs={{0,64},{8,72},{16,80},{24,88},{32,96},{40,104},{48,112},{56,120},{... | collective-permute-start | bytes 98312 | tf_op jit(solution)/shard_map/ppermute | solution.py:24
  54.6 6.7 %copy-start.5 = (bf16[128,3,256]{2,0,1:T(8,128)(2,1)S(1)}, bf16[128,3,256]{2,0,1:T(8,128)(2,1)}, u32[]{:S(2)}) copy-start(bf16[128,3,256]{2,0,1:T(8,128)(2,1)} %param.13) | copy-start | bytes 589828
  61.3 129.6 %all-gather.5.cloned.1.call-start = ((), (), s32[]{:S(2)}) async-start(), calls=%async_computation.2 | async-start | bytes 6488064 | tf_op jit(solution)/shard_map/all_gather | solution.py:211
  65.4 5.1 %copy-start.7 = (f32[4096]{0:T(1024)S(1)}, f32[4096]{0:T(1024)}, u32[]{:S(2)}) copy-start(f32[4096]{0:T(1024)} %param.12) | copy-start | bytes 49156
  65.4 62.2 %all-to-all-start = ((bf16[8,384,512]{1,2,0:T(8,128)(2,1)}), bf16[8,384,512]{1,2,0:T(8,128)(2,1)S(1)}, u32[]{:S(2)}, u32[]{:S(2)}) async-start(bf16[8,384,512]{1,2,0:T(8,128)(2,1)} %broadcast_in_dim.68), calls=%async_computation | async-start | bytes 6291456 | tf_op jit(solution)/shard_map/all_to_all | solution.py:230
  190.9 6.5 %copy-start.1 = (bf16[128,4096]{1,0:T(8,128)(2,1)S(1)}, bf16[128,4096]{1,0:T(8,128)(2,1)}, u32[]{:S(2)}) copy-start(bf16[128,4096]{1,0:T(8,128)(2,1)} %all-gather.3.cloned.1.call-done) | copy-start | bytes 3145732
  190.9 6.6 %copy-start.8 = (bf16[4096,3,256]{0,2,1:T(8,128)(2,1)S(1)}, bf16[4096,3,256]{0,2,1:T(8,128)(2,1)}, u32[]{:S(2)}) copy-start(bf16[4096,3,256]{0,2,1:T(8,128)(2,1)} %all-gather.5.cloned.1.call-done) | copy-start | bytes 18874372
  199.7 16.9 %collective-permute-start.11 = (bf16[512,512]{1,0:T(8,128)(2,1)S(1)}, bf16[512,512]{1,0:T(8,128)(2,1)}, u32[]{:S(2)}, u32[]{:S(2)}) collective-permute-start(bf16[512,512]{1,0:T(8,128)(2,1)S(1)} %pad_maximum_fusion), channel_id=1, source_target_pairs={{0,8},{8,16},{16,24},{24,32},{32,40},{40,48},{48,56},{56,64},{64,7... | collective-permute-start | bytes 1572872 | tf_op jit(solution)/shard_map/ppermute | solution.py:24
  216.6 20.7 %collective-permute-start.12 = (bf16[512,512]{1,0:T(8,128)(2,1)}, bf16[512,512]{1,0:T(8,128)(2,1)}, u32[]{:S(2)}, u32[]{:S(2)}) collective-permute-start(bf16[512,512]{1,0:T(8,128)(2,1)} %collective-permute-done.11), channel_id=1, source_target_pairs={{0,8},{8,16},{16,24},{24,32},{32,40},{40,48},{48,56},{56,64},{64,7... | collective-permute-start | bytes 1572872 | tf_op jit(solution)/shard_map/ppermute | solution.py:24
  239.3 1.6 copy-start
  239.3 1.6 copy-start.3
  (2 other events, 1.6 us)
Sparse Core Ops, SparseCore 0:
  61.4 55.2 all-gather.2
  119.8 71.0 all-gather.4

commit v4 on v0

--- a/solution.py
+++ b/solution.py
@@ -234,13 +234,13 @@
     inverse = lax.rsqrt(jnp.mean(as_float * as_float, axis=1, keepdims=True) + EPSILON)
     normed = (as_float * inverse * norm_gain[None]).astype(jnp.bfloat16)
     flat_rows = shard_rows.reshape(shard_rows.shape[0], 3 * head_cols)
-    projected = jnp.dot(normed, flat_rows, preferred_element_type=jnp.float32).astype(jnp.bfloat16)
+    kv_pair = jnp.dot(normed, flat_rows[:, head_cols:], preferred_element_type=jnp.float32).astype(jnp.bfloat16)
     heads = head_cols // HD
-    query = projected[:, :head_cols].reshape(tok_dev, heads, HD)
-    kv_pair = projected[:, head_cols:]
     blocks_kv = [kv_pair]
     for _ in range(WINDOW - 1):
         blocks_kv.append(from_behind(blocks_kv[-1], "ctx", 1))
+    projected_q = jnp.dot(normed, flat_rows[:, :head_cols], preferred_element_type=jnp.float32).astype(jnp.bfloat16)
+    query = projected_q.reshape(tok_dev, heads, HD)
     position = lax.axis_index("ctx")
     row_ids = jnp.arange(tok_dev)
     causal = row_ids[:, None] >= row_ids[None, :]

time: 195 us -> 193 us (0.990)
  local copies, waits for them, and re-layouts: 20.4 us -> 15.9 us
    ppermute x6, waiting for transfers between devices: 33.2 us -> 35.3 us  [from_behind(): lax.ppermute(value, axis, [(source, source + steps) for source in range(l...]
    slice x2, local copies, waits for them, and re-layouts: 2.15 us -> 0.07 us  [block_body(): values = blocks_kv[lag_step][:, head_cols:].reshape(tok_dev, heads, HD)]
    dot_general x1 -> x2, matrix products: 7.53 us -> 9.05 us  [the longest x1 6.05 us: block_body(): jnp.dot(normed, flat_rows[:, head_cols:], preferred_element_type=jnp.floa...]
    unnamed x37 -> x32, local copies, waits for them, and re-layouts: 11.7 us -> 10.3 us
  transfers between devices with their start and end apart: 21 -> 21, of which waited for: 8 -> 7; matrix products, arithmetic and copies ran while one was open for 8% -> 7% of each run, Pallas kernels for 12% -> 13%
where the time goes in v4:
time: 193 us; the launch traced here: 192 us
  waiting for transfers between devices  73.8 us (38%)
  starting transfers between devices  47.5 us (25%)
  Pallas kernels  24.3 us (13%)
  local copies, waits for them, and re-layouts  15.9 us (8%)
  between operations  14.7 us (8%)
  matrix products  12.6 us (7%)
  other arithmetic  3.35 us (2%)
    ppermute x7, waiting for transfers between devices, block_body(): lax.ppermute(mixer, 'tp', [((source + shift) % parts, source) for source...  36.3 us
    ppermute x6, waiting for transfers between devices, from_behind(): lax.ppermute(value, axis, [(source, source + steps) for source in range(l...  35.3 us
    ppermute x7, starting transfers between devices, block_body(): lax.ppermute(mixer, 'tp', [((source + shift) % parts, source) for source...  29.4 us
    ppermute x6, starting transfers between devices, from_behind(): lax.ppermute(value, axis, [(source, source + steps) for source in range(l...  10.9 us
    pallas_call x1, Pallas kernels, intra_call(): pl.pallas_call(intra_kernel, out_shape=whole((tokens, channels), jnp.floa...  10.4 us
    unnamed x32, local copies, waits for them, and re-layouts  10.3 us
    pallas_call x1, Pallas kernels, front_call(): pl.pallas_call(front_kernel, out_shape=(whole((tokens, channels), jnp.flo...  8.79 us
    ppermute x7, starting transfers between devices, exchange_history(): arrived = lax.ppermute(block_end, 'ctx', pairs)  7.21 us
  transfers between devices with their start and end apart: 21, of which 7 were waited for; matrix products, arithmetic and copies ran while one was open for 7% of the time, Pallas kernels for 13%

profile of v4, /device:TPU:128, one launch (start us, length us, event | category | flops | bytes accessed | tf_op | source)
XLA Modules:
  0.0 192.1 jit_solution(12575635720132348391)
XLA Ops:
  7.2 1.7 copy.34
  9.7 1.9 collective-permute-start
  11.7 1.7 copy.26
  16.4 2.7 %collective-permute-done = bf16[6,3,512]{2,0,1:T(8,128)(2,1)S(1)} collective-permute-done((bf16[6,3,512]{2,0,1:T(8,128)(2,1)S(1)}, bf16[6,3,512]{2,0,1:T(8,128)(2,1)S(1)}, u32[]{:S(2)}, u32[]{:S(2)}) %collective-permute-start) | collective-permute-done | bytes 18464 | tf_op jit(solution)/shard_map/ppermute | solution.py:24
  19.7 8.8 %shard_map.86 = (f32[512,512]{1,0:T(8,128)}, f32[512,512]{1,0:T(8,128)}, f32[16,4,512]{2,1,0:T(4,128)}) custom-call(bf16[512,1536]{1,0:T(8,128)(2,1)} %copy.27.feat_ref, bf16[6,1536]{1,0:T(8,128)(2,1)} %bitcast.79, f32[3,7,512]{2,1,0:T(8,128)} %taps_ref.1, f32[16,1,512]{2,1,0:T(1,128)} %broadcast_in_dim.56.decay_ref), custom_call_target="tpu_custom_call" | custom-call | flops 19398656 | bytes 3670016 | tf_op jit(solution)/shard_map/pallas_call | solution.py:98
  30.5 3.4 %collective-permute-start.4 = (f32[16,512]{1,0:T(8,128)S(1)}, f32[16,512]{1,0:T(8,128)S(1)}, u32[]{:S(2)}, u32[]{:S(2)}) collective-permute-start(f32[16,512]{1,0:T(8,128)S(1)} %get-tuple-element.15), channel_id=1, source_target_pairs={{0,32},{8,40},{16,48},{24,56},{32,0},{40,8},{48,16},{56,24},{64,96... | collective-permute-start | bytes 98312 | tf_op jit(solution)/shard_map/ppermute | solution.py:171
  37.6 2.1 %collective-permute-done.6 = f32[16,512]{1,0:T(8,128)S(1)} collective-permute-done((f32[16,512]{1,0:T(8,128)S(1)}, f32[16,512]{1,0:T(8,128)S(1)}, u32[]{:S(2)}, u32[]{:S(2)}) %collective-permute-start.6) | collective-permute-done | bytes 32800 | tf_op jit(solution)/shard_map/ppermute | solution.py:171
  40.4 2.9 %collective-permute-start.8 = (f32[16,512]{1,0:T(8,128)S(1)}, f32[16,512]{1,0:T(8,128)S(1)}, u32[]{:S(2)}, u32[]{:S(2)}) collective-permute-start(f32[16,512]{1,0:T(8,128)S(1)} %multiply_add_fusion.1), channel_id=1, source_target_pairs={{0,64},{8,72},{16,80},{24,88},{32,96},{40,104},{48,112},{56,120},{... | collective-permute-start | bytes 98312 | tf_op jit(solution)/shard_map/ppermute | solution.py:24
  44.7 10.4 %shard_map.87.intra_ref = f32[512,512]{1,0:T(8,128)} custom-call(f32[512,512]{1,0:T(8,128)} %get-tuple-element.5.gated_ref, f32[16,1,512]{2,1,0:T(1,128)} %broadcast_in_dim.56.decay_ref, f32[16,1,512]{2,1,0:T(1,128)} %broadcast_in_dim.57.mixing_ref), custom_call_target="tpu_custom_call" | custom-call | flops 2147483648 | bytes 2097152 | tf_op jit(solution)/shard_map/pallas_call | solution.py:146
  56.2 5.1 %shard_map.88 = bf16[512,512]{1,0:T(8,128)(2,1)} custom-call(f32[512,512]{1,0:T(8,128)} %shard_map.87.intra_ref, f32[16,4,512]{2,1,0:T(4,128)} %maximum_add_fusion.state_ref, f32[16,1,512]{2,1,0:T(1,128)} %broadcast_in_dim.56.decay_ref, f32[16,1,512]{2,1,0:T(1,128)} %broadcast_in_dim.57.mixing_ref, f32[512,512]{1,0:T(8,128)} %get-tuple-element.5.gated_ref, ...), custom_call_target="tpu_custom_call" | custom-call | flops 8388608 | bytes 3670016 | tf_op jit(solution)/shard_map/pallas_call | solution.py:185
  61.3 3.5 %collective-permute-start.11 = (bf16[512,512]{1,0:T(8,128)(2,1)}, bf16[512,512]{1,0:T(8,128)(2,1)S(1)}, u32[]{:S(2)}, u32[]{:S(2)}) collective-permute-start(bf16[512,512]{1,0:T(8,128)(2,1)} %shard_map.88), channel_id=1, source_target_pairs={{1,0},{2,1},{3,2},{4,3},{5,4},{6,5},{7,6},{0,7},{9,8},{10,9},{11,1... | collective-permute-start | bytes 1572872 | tf_op jit(solution)/shard_map/ppermute | solution.py:228
  66.4 2.9 %collective-permute-start.14 = (bf16[512,512]{1,0:T(8,128)(2,1)}, bf16[512,512]{1,0:T(8,128)(2,1)S(1)}, u32[]{:S(2)}, u32[]{:S(2)}) collective-permute-start(bf16[512,512]{1,0:T(8,128)(2,1)} %shard_map.88), channel_id=1, source_target_pairs={{4,0},{5,1},{6,2},{7,3},{0,4},{1,5},{2,6},{3,7},{12,8},{13,9},{14,... | collective-permute-start | bytes 1572872 | tf_op jit(solution)/shard_map/ppermute | solution.py:228
  70.8 19.4 %collective-permute-done.11 = bf16[512,512]{1,0:T(8,128)(2,1)S(1)} collective-permute-done((bf16[512,512]{1,0:T(8,128)(2,1)}, bf16[512,512]{1,0:T(8,128)(2,1)S(1)}, u32[]{:S(2)}, u32[]{:S(2)}) %collective-permute-start.11) | collective-permute-done | bytes 524320 | tf_op jit(solution)/shard_map/ppermute | solution.py:228
  90.1 2.5 %collective-permute-start.16 = (bf16[512,512]{1,0:T(8,128)(2,1)}, bf16[512,512]{1,0:T(8,128)(2,1)S(1)}, u32[]{:S(2)}, u32[]{:S(2)}) collective-permute-start(bf16[512,512]{1,0:T(8,128)(2,1)} %shard_map.88), channel_id=1, source_target_pairs={{6,0},{7,1},{0,2},{1,3},{2,4},{3,5},{4,6},{5,7},{14,8},{15,9},{8,1... | collective-permute-start | bytes 1572872 | tf_op jit(solution)/shard_map/ppermute | solution.py:228
  92.7 18.8 %collective-permute-start.17 = (bf16[512,512]{1,0:T(8,128)(2,1)}, bf16[512,512]{1,0:T(8,128)(2,1)S(1)}, u32[]{:S(2)}, u32[]{:S(2)}) collective-permute-start(bf16[512,512]{1,0:T(8,128)(2,1)} %shard_map.88), channel_id=1, source_target_pairs={{7,0},{0,1},{1,2},{2,3},{3,4},{4,5},{5,6},{6,7},{15,8},{8,9},{9,10... | collective-permute-start | bytes 1572872 | tf_op jit(solution)/shard_map/ppermute | solution.py:228
  111.7 4.8 %collective-permute-done.15 = bf16[512,512]{1,0:T(8,128)(2,1)S(1)} collective-permute-done((bf16[512,512]{1,0:T(8,128)(2,1)}, bf16[512,512]{1,0:T(8,128)(2,1)S(1)}, u32[]{:S(2)}, u32[]{:S(2)}) %collective-permute-start.15) | collective-permute-done | bytes 524320 | tf_op jit(solution)/shard_map/ppermute | solution.py:228
  116.6 12.2 %collective-permute-done.16 = bf16[512,512]{1,0:T(8,128)(2,1)S(1)} collective-permute-done((bf16[512,512]{1,0:T(8,128)(2,1)}, bf16[512,512]{1,0:T(8,128)(2,1)S(1)}, u32[]{:S(2)}, u32[]{:S(2)}) %collective-permute-start.16) | collective-permute-done | bytes 524320 | tf_op jit(solution)/shard_map/ppermute | solution.py:228
  129.4 3.2 %copy-done.1 = bf16[512,8192]{1,0:T(8,128)(2,1)} copy-done((bf16[512,8192]{1,0:T(8,128)(2,1)}, bf16[512,8192]{1,0:T(8,128)(2,1)S(1)}, u32[]{:S(2)}) %copy-start.1) | copy-done | bytes 8388632
  133.6 6.0 %fusion.16 = bf16[512,512]{0,1:T(8,128)(2,1)S(1)} fusion(bf16[4096,768]{0,1:T(8,128)(2,1)} %bitcast.77, f32[4096]{0:T(1024)S(1)} %copy-done.6, f32[512]{0:T(512)S(1)} %add_rsqrt_fusion, bf16[512,8192]{1,0:T(8,128)(2,1)} %copy-done.1, s32[]{:T(128)S(6)} %select_n.119), kind=kOutput, calls=%fused_computation.24 | convolution fusion | flops 2156134400 | bytes 8931332 | tf_op jit(solution)/shard_map/dot_general | solution.py:237
  139.7 3.0 %fusion.22 = bf16[512,256]{0,1:T(8,128)(2,1)S(1)} fusion(bf16[4096,768]{0,1:T(8,128)(2,1)} %bitcast.78, f32[4096]{0:T(1024)S(1)} %copy-done.6, f32[512]{0:T(512)S(1)} %add_rsqrt_fusion, bf16[512,8192]{1,0:T(8,128)(2,1)S(1)} %copy-done.2, s32[]{:T(128)S(6)} %select_n.119), kind=kOutput, calls=%fused_computation.30 | convolution fusion | flops 1082261504 | bytes 6572036 | tf_op jit(solution)/shard_map/dot_general | solution.py:242
  142.7 1.9 collective-permute-start.18
  145.3 15.0 %collective-permute-done.18 = bf16[512,512]{0,1:T(8,128)(2,1)S(1)} collective-permute-done((bf16[512,512]{0,1:T(8,128)(2,1)S(1)}, bf16[512,512]{0,1:T(8,128)(2,1)S(1)}, u32[]{:S(2)}, u32[]{:S(2)}) %collective-permute-start.18) | collective-permute-done | bytes 524320 | tf_op jit(solution)/shard_map/ppermute | solution.py:24
  160.3 2.1 %collective-permute-start.19 = (bf16[512,512]{0,1:T(8,128)(2,1)S(1)}, bf16[512,512]{0,1:T(8,128)(2,1)S(1)}, u32[]{:S(2)}, u32[]{:S(2)}) collective-permute-start(bf16[512,512]{0,1:T(8,128)(2,1)S(1)} %collective-permute-done.18), channel_id=1, source_target_pairs={{0,8},{8,16},{16,24},{24,32},{32,40},{40,48},{48,56},{56,64},{64,7... | collective-permute-start | bytes 1572872 | tf_op jit(solution)/shard_map/ppermute | solution.py:24
  163.0 17.6 %collective-permute-done.19 = bf16[512,512]{0,1:T(8,128)(2,1)S(1)} collective-permute-done((bf16[512,512]{0,1:T(8,128)(2,1)S(1)}, bf16[512,512]{0,1:T(8,128)(2,1)S(1)}, u32[]{:S(2)}, u32[]{:S(2)}) %collective-permute-start.19) | collective-permute-done | bytes 524320 | tf_op jit(solution)/shard_map/ppermute | solution.py:24
  (86 shorter events, 23.6 us)
Async XLA Ops:
  7.2 126.4 %all-gather.2.cloned.1.call-start = ((), (), s32[]{:S(2)}) async-start(), calls=%async_computation | async-start | bytes 6488064 | tf_op jit(solution)/shard_map/all_gather | solution.py:211
  9.7 19.7 %copy-start.3 = (f32[16,512]{1,0:T(8,128)S(1)}, f32[16,512]{1,0:T(8,128)}, u32[]{:S(2)}) copy-start(f32[16,512]{1,0:T(8,128)} %param.9) | copy-start | bytes 98308
  9.7 27.2 %copy-start.4 = (f32[16,512]{1,0:T(8,128)S(1)}, f32[16,512]{1,0:T(8,128)}, u32[]{:S(2)}) copy-start(f32[16,512]{1,0:T(8,128)} %param.10) | copy-start | bytes 98308
  9.7 9.4 %collective-permute-start = (bf16[6,3,512]{2,0,1:T(8,128)(2,1)S(1)}, bf16[6,3,512]{2,0,1:T(8,128)(2,1)S(1)}, u32[]{:S(2)}, u32[]{:S(2)}) collective-permute-start(bf16[6,3,512]{2,0,1:T(8,128)(2,1)S(1)} %slice.39), channel_id=1, source_target_pairs={{0,8},{8,16},{16,24},{24,32},{32,40},{40,48},{48,56},{56,64},{64,7... | collective-permute-start | bytes 55304 | tf_op jit(solution)/shard_map/ppermute | solution.py:24
  29.5 6.0 %collective-permute-start.1 = (f32[16,512]{1,0:T(8,128)S(1)}, f32[16,512]{1,0:T(8,128)S(1)}, u32[]{:S(2)}, u32[]{:S(2)}) collective-permute-start(f32[16,512]{1,0:T(8,128)S(1)} %get-tuple-element.15), channel_id=1, source_target_pairs={{0,8},{8,16},{16,24},{24,32},{32,40},{40,48},{48,56},{56,0},{64,72... | collective-permute-start | bytes 98312 | tf_op jit(solution)/shard_map/ppermute | solution.py:171
  29.5 7.2 %collective-permute-start.2 = (f32[16,512]{1,0:T(8,128)S(1)}, f32[16,512]{1,0:T(8,128)S(1)}, u32[]{:S(2)}, u32[]{:S(2)}) collective-permute-start(f32[16,512]{1,0:T(8,128)S(1)} %get-tuple-element.15), channel_id=1, source_target_pairs={{0,16},{8,24},{16,32},{24,40},{32,48},{40,56},{48,0},{56,8},{64,80... | collective-permute-start | bytes 98312 | tf_op jit(solution)/shard_map/ppermute | solution.py:171
  29.9 7.7 %collective-permute-start.3 = (f32[16,512]{1,0:T(8,128)S(1)}, f32[16,512]{1,0:T(8,128)S(1)}, u32[]{:S(2)}, u32[]{:S(2)}) collective-permute-start(f32[16,512]{1,0:T(8,128)S(1)} %get-tuple-element.15), channel_id=1, source_target_pairs={{0,24},{8,32},{16,40},{24,48},{32,56},{40,0},{48,8},{56,16},{64,88... | collective-permute-start | bytes 98312 | tf_op jit(solution)/shard_map/ppermute | solution.py:171
  30.5 7.1 %collective-permute-start.4 = (f32[16,512]{1,0:T(8,128)S(1)}, f32[16,512]{1,0:T(8,128)S(1)}, u32[]{:S(2)}, u32[]{:S(2)}) collective-permute-start(f32[16,512]{1,0:T(8,128)S(1)} %get-tuple-element.15), channel_id=1, source_target_pairs={{0,32},{8,40},{16,48},{24,56},{32,0},{40,8},{48,16},{56,24},{64,96... | collective-permute-start | bytes 98312 | tf_op jit(solution)/shard_map/ppermute | solution.py:171
  33.9 3.7 %collective-permute-start.5 = (f32[16,512]{1,0:T(8,128)S(1)}, f32[16,512]{1,0:T(8,128)S(1)}, u32[]{:S(2)}, u32[]{:S(2)}) collective-permute-start(f32[16,512]{1,0:T(8,128)S(1)} %get-tuple-element.15), channel_id=1, source_target_pairs={{0,40},{8,48},{16,56},{24,0},{32,8},{40,16},{48,24},{56,32},{64,10... | collective-permute-start | bytes 98312 | tf_op jit(solution)/shard_map/ppermute | solution.py:171
  35.5 4.2 %collective-permute-start.6 = (f32[16,512]{1,0:T(8,128)S(1)}, f32[16,512]{1,0:T(8,128)S(1)}, u32[]{:S(2)}, u32[]{:S(2)}) collective-permute-start(f32[16,512]{1,0:T(8,128)S(1)} %get-tuple-element.15), channel_id=1, source_target_pairs={{0,48},{8,56},{16,0},{24,8},{32,16},{40,24},{48,32},{56,40},{64,11... | collective-permute-start | bytes 98312 | tf_op jit(solution)/shard_map/ppermute | solution.py:171
  36.7 3.0 %collective-permute-start.7 = (f32[16,512]{1,0:T(8,128)S(1)}, f32[16,512]{1,0:T(8,128)S(1)}, u32[]{:S(2)}, u32[]{:S(2)}) collective-permute-start(f32[16,512]{1,0:T(8,128)S(1)} %get-tuple-element.15), channel_id=1, source_target_pairs={{0,56},{8,0},{16,8},{24,16},{32,24},{40,32},{48,40},{56,48},{64,12... | collective-permute-start | bytes 98312 | tf_op jit(solution)/shard_map/ppermute | solution.py:171
  39.8 15.4 %collective-permute-start.10 = (f32[16,512]{1,0:T(8,128)S(1)}, f32[16,512]{1,0:T(8,128)S(1)}, u32[]{:S(2)}, u32[]{:S(2)}) collective-permute-start(f32[16,512]{1,0:T(8,128)S(1)} %multiply_add_fusion.1), channel_id=1, source_target_pairs={{0,192},{8,200},{16,208},{24,216},{32,224},{40,232},{48,240},{56,2... | collective-permute-start | bytes 98312 | tf_op jit(solution)/shard_map/ppermute | solution.py:24
  40.4 14.8 %collective-permute-start.8 = (f32[16,512]{1,0:T(8,128)S(1)}, f32[16,512]{1,0:T(8,128)S(1)}, u32[]{:S(2)}, u32[]{:S(2)}) collective-permute-start(f32[16,512]{1,0:T(8,128)S(1)} %multiply_add_fusion.1), channel_id=1, source_target_pairs={{0,64},{8,72},{16,80},{24,88},{32,96},{40,104},{48,112},{56,120},{... | collective-permute-start | bytes 98312 | tf_op jit(solution)/shard_map/ppermute | solution.py:24
  43.4 11.8 %collective-permute-start.9 = (f32[16,512]{1,0:T(8,128)S(1)}, f32[16,512]{1,0:T(8,128)S(1)}, u32[]{:S(2)}, u32[]{:S(2)}) collective-permute-start(f32[16,512]{1,0:T(8,128)S(1)} %multiply_add_fusion.1), channel_id=1, source_target_pairs={{0,128},{8,136},{16,144},{24,152},{32,160},{40,168},{48,176},{56,1... | collective-permute-start | bytes 98312 | tf_op jit(solution)/shard_map/ppermute | solution.py:24
  61.3 28.9 %collective-permute-start.11 = (bf16[512,512]{1,0:T(8,128)(2,1)}, bf16[512,512]{1,0:T(8,128)(2,1)S(1)}, u32[]{:S(2)}, u32[]{:S(2)}) collective-permute-start(bf16[512,512]{1,0:T(8,128)(2,1)} %shard_map.88), channel_id=1, source_target_pairs={{1,0},{2,1},{3,2},{4,3},{5,4},{6,5},{7,6},{0,7},{9,8},{10,9},{11,1... | collective-permute-start | bytes 1572872 | tf_op jit(solution)/shard_map/ppermute | solution.py:228
  64.7 27.9 %collective-permute-start.12 = (bf16[512,512]{1,0:T(8,128)(2,1)}, bf16[512,512]{1,0:T(8,128)(2,1)S(1)}, u32[]{:S(2)}, u32[]{:S(2)}) collective-permute-start(bf16[512,512]{1,0:T(8,128)(2,1)} %shard_map.88), channel_id=1, source_target_pairs={{2,0},{3,1},{4,2},{5,3},{6,4},{7,5},{0,6},{1,7},{10,8},{11,9},{12,... | collective-permute-start | bytes 1572872 | tf_op jit(solution)/shard_map/ppermute | solution.py:228
  65.5 46.1 %collective-permute-start.13 = (bf16[512,512]{1,0:T(8,128)(2,1)}, bf16[512,512]{1,0:T(8,128)(2,1)S(1)}, u32[]{:S(2)}, u32[]{:S(2)}) collective-permute-start(bf16[512,512]{1,0:T(8,128)(2,1)} %shard_map.88), channel_id=1, source_target_pairs={{3,0},{4,1},{5,2},{6,3},{7,4},{0,5},{1,6},{2,7},{11,8},{12,9},{13,... | collective-permute-start | bytes 1572872 | tf_op jit(solution)/shard_map/ppermute | solution.py:228
  66.4 45.2 %collective-permute-start.14 = (bf16[512,512]{1,0:T(8,128)(2,1)}, bf16[512,512]{1,0:T(8,128)(2,1)S(1)}, u32[]{:S(2)}, u32[]{:S(2)}) collective-permute-start(bf16[512,512]{1,0:T(8,128)(2,1)} %shard_map.88), channel_id=1, source_target_pairs={{4,0},{5,1},{6,2},{7,3},{0,4},{1,5},{2,6},{3,7},{12,8},{13,9},{14,... | collective-permute-start | bytes 1572872 | tf_op jit(solution)/shard_map/ppermute | solution.py:228
  69.4 59.5 %copy-start = (bf16[512,512]{1,0:T(8,128)(2,1)S(1)}, bf16[512,512]{1,0:T(8,128)(2,1)}, u32[]{:S(2)}) copy-start(bf16[512,512]{1,0:T(8,128)(2,1)} %shard_map.88) | copy-start | bytes 1572868
  69.4 47.1 %collective-permute-start.15 = (bf16[512,512]{1,0:T(8,128)(2,1)}, bf16[512,512]{1,0:T(8,128)(2,1)S(1)}, u32[]{:S(2)}, u32[]{:S(2)}) collective-permute-start(bf16[512,512]{1,0:T(8,128)(2,1)} %shard_map.88), channel_id=1, source_target_pairs={{5,0},{6,1},{7,2},{0,3},{1,4},{2,5},{3,6},{4,7},{13,8},{14,9},{15,... | collective-permute-start | bytes 1572872 | tf_op jit(solution)/shard_map/ppermute | solution.py:228
  90.1 38.6 %collective-permute-start.16 = (bf16[512,512]{1,0:T(8,128)(2,1)}, bf16[512,512]{1,0:T(8,128)(2,1)S(1)}, u32[]{:S(2)}, u32[]{:S(2)}) collective-permute-start(bf16[512,512]{1,0:T(8,128)(2,1)} %shard_map.88), channel_id=1, source_target_pairs={{6,0},{7,1},{0,2},{1,3},{2,4},{3,5},{4,6},{5,7},{14,8},{15,9},{8,1... | collective-permute-start | bytes 1572872 | tf_op jit(solution)/shard_map/ppermute | solution.py:228
  92.7 36.1 %collective-permute-start.17 = (bf16[512,512]{1,0:T(8,128)(2,1)}, bf16[512,512]{1,0:T(8,128)(2,1)S(1)}, u32[]{:S(2)}, u32[]{:S(2)}) collective-permute-start(bf16[512,512]{1,0:T(8,128)(2,1)} %shard_map.88), channel_id=1, source_target_pairs={{7,0},{0,1},{1,2},{2,3},{3,4},{4,5},{5,6},{6,7},{15,8},{8,9},{9,10... | collective-permute-start | bytes 1572872 | tf_op jit(solution)/shard_map/ppermute | solution.py:228
  142.7 17.6 %collective-permute-start.18 = (bf16[512,512]{0,1:T(8,128)(2,1)S(1)}, bf16[512,512]{0,1:T(8,128)(2,1)S(1)}, u32[]{:S(2)}, u32[]{:S(2)}) collective-permute-start(bf16[512,512]{0,1:T(8,128)(2,1)S(1)} %fusion.16), channel_id=1, source_target_pairs={{0,8},{8,16},{16,24},{24,32},{32,40},{40,48},{48,56},{56,64},{64,7... | collective-permute-start | bytes 1572872 | tf_op jit(solution)/shard_map/ppermute | solution.py:24
  160.3 20.3 %collective-permute-start.19 = (bf16[512,512]{0,1:T(8,128)(2,1)S(1)}, bf16[512,512]{0,1:T(8,128)(2,1)S(1)}, u32[]{:S(2)}, u32[]{:S(2)}) collective-permute-start(bf16[512,512]{0,1:T(8,128)(2,1)S(1)} %collective-permute-done.18), channel_id=1, source_target_pairs={{0,8},{8,16},{16,24},{24,32},{32,40},{40,48},{48,56},{56,64},{64,7... | collective-permute-start | bytes 1572872 | tf_op jit(solution)/shard_map/ppermute | solution.py:24
  (4 other events, 14.4 us)
Sparse Core Ops, SparseCore 0:
  11.0 75.2 all-gather.1

commit v5 on v4

--- a/solution.py
+++ b/solution.py
@@ -236,9 +236,11 @@
     flat_rows = shard_rows.reshape(shard_rows.shape[0], 3 * head_cols)
     kv_pair = jnp.dot(normed, flat_rows[:, head_cols:], preferred_element_type=jnp.float32).astype(jnp.bfloat16)
     heads = head_cols // HD
-    blocks_kv = [kv_pair]
+    blocks_k = [kv_pair[:, :head_cols]]
+    blocks_v = [kv_pair[:, head_cols:]]
     for _ in range(WINDOW - 1):
-        blocks_kv.append(from_behind(blocks_kv[-1], "ctx", 1))
+        blocks_k.append(from_behind(blocks_k[-1], "ctx", 1))
+        blocks_v.append(from_behind(blocks_v[-1], "ctx", 1))
     projected_q = jnp.dot(normed, flat_rows[:, :head_cols], preferred_element_type=jnp.float32).astype(jnp.bfloat16)
     query = projected_q.reshape(tok_dev, heads, HD)
     position = lax.axis_index("ctx")
@@ -246,7 +248,7 @@
     causal = row_ids[:, None] >= row_ids[None, :]
     score_list = []
     for lag_step in range(WINDOW):
-        keys = blocks_kv[lag_step][:, :head_cols].reshape(tok_dev, heads, HD)
+        keys = blocks_k[lag_step].reshape(tok_dev, heads, HD)
         scores = jnp.einsum(
             "thd,shd->hts", query, keys, preferred_element_type=jnp.float32
         ) / math.sqrt(HD)
@@ -261,7 +263,7 @@
     for lag_step in range(WINDOW):
         expo = jnp.exp(score_list[lag_step] - peak[:, :, None])
         total = total + jnp.sum(expo, axis=2)
-        values = blocks_kv[lag_step][:, head_cols:].reshape(tok_dev, heads, HD)
+        values = blocks_v[lag_step].reshape(tok_dev, heads, HD)
         output = output + jnp.einsum(
             "hts,shd->thd", expo.astype(jnp.bfloat16), values, preferred_element_type=jnp.float32
         )

time: 193 us -> 184 us (0.953)
  waiting for transfers between devices: 73.8 us -> 58.9 us
  starting transfers between devices: 47.5 us -> 53.2 us
    ppermute x6 -> x8, waiting for transfers between devices: 35.3 us -> 20.4 us  [from_behind(): lax.ppermute(value, axis, [(source, source + steps) for source in range(l...]
    ppermute x6 -> x8, starting transfers between devices: 10.9 us -> 16.6 us  [from_behind(): lax.ppermute(value, axis, [(source, source + steps) for source in range(l...]
  transfers between devices with their start and end apart: 21 -> 23, of which waited for: 7 -> 9; matrix products, arithmetic and copies ran while one was open for 7% -> 9% of each run, Pallas kernels for 13% -> 13%
where the time goes in v5:
time: 184 us
  waiting for transfers between devices  58.9 us (32%)
  starting transfers between devices  53.2 us (29%)
  Pallas kernels  24.3 us (13%)
  local copies, waits for them, and re-layouts  16.7 us (9%)
  between operations  14.7 us (8%)
  matrix products  12.6 us (7%)
  other arithmetic  3.36 us (2%)
    ppermute x7, waiting for transfers between devices, block_body(): lax.ppermute(mixer, 'tp', [((source + shift) % parts, source) for source...  36.3 us
    ppermute x7, starting transfers between devices, block_body(): lax.ppermute(mixer, 'tp', [((source + shift) % parts, source) for source...  29.4 us
    ppermute x8, waiting for transfers between devices, from_behind(): lax.ppermute(value, axis, [(source, source + steps) for source in range(l...  20.4 us
    ppermute x8, starting transfers between devices, from_behind(): lax.ppermute(value, axis, [(source, source + steps) for source in range(l...  16.6 us
    unnamed x32, local copies, waits for them, and re-layouts  11.2 us
    pallas_call x1, Pallas kernels, intra_call(): pl.pallas_call(intra_kernel, out_shape=whole((tokens, channels), jnp.floa...  10.4 us
    pallas_call x1, Pallas kernels, front_call(): pl.pallas_call(front_kernel, out_shape=(whole((tokens, channels), jnp.flo...  8.79 us
    ppermute x7, starting transfers between devices, exchange_history(): arrived = lax.ppermute(block_end, 'ctx', pairs)  7.21 us
  transfers between devices with their start and end apart: 23, of which 9 were waited for; matrix products, arithmetic and copies ran while one was open for 9% of the time, Pallas kernels for 13%

profile of v5, /device:TPU:128, one launch (start us, length us, event | category | flops | bytes accessed | tf_op | source)
XLA Modules:
  0.0 183.8 jit_solution(2342931605895180720)
XLA Ops:
  9.7 1.9 %collective-permute-start = (bf16[6,3,512]{2,0,1:T(8,128)(2,1)S(1)}, bf16[6,3,512]{2,0,1:T(8,128)(2,1)S(1)}, u32[]{:S(2)}, u32[]{:S(2)}) collective-permute-start(bf16[6,3,512]{2,0,1:T(8,128)(2,1)S(1)} %slice.27), channel_id=1, source_target_pairs={{0,8},{8,16},{16,24},{24,32},{32,40},{40,48},{48,56},{56,64},{64,7... | collective-permute-start | bytes 55304 | tf_op jit(solution)/shard_map/ppermute | solution.py:24
  16.4 2.7 %collective-permute-done = bf16[6,3,512]{2,0,1:T(8,128)(2,1)S(1)} collective-permute-done((bf16[6,3,512]{2,0,1:T(8,128)(2,1)S(1)}, bf16[6,3,512]{2,0,1:T(8,128)(2,1)S(1)}, u32[]{:S(2)}, u32[]{:S(2)}) %collective-permute-start) | collective-permute-done | bytes 18464 | tf_op jit(solution)/shard_map/ppermute | solution.py:24
  19.7 8.8 %shard_map.86 = (f32[512,512]{1,0:T(8,128)}, f32[512,512]{1,0:T(8,128)}, f32[16,4,512]{2,1,0:T(4,128)}) custom-call(bf16[512,1536]{1,0:T(8,128)(2,1)} %copy.27.feat_ref, bf16[6,1536]{1,0:T(8,128)(2,1)} %bitcast.79, f32[3,7,512]{2,1,0:T(8,128)} %taps_ref.1, f32[16,1,512]{2,1,0:T(1,128)} %broadcast_in_dim.56.decay_ref), custom_call_target="tpu_custom_call" | custom-call | flops 19398656 | bytes 3670016 | tf_op jit(solution)/shard_map/pallas_call | solution.py:98
  30.5 3.4 %collective-permute-start.4 = (f32[16,512]{1,0:T(8,128)S(1)}, f32[16,512]{1,0:T(8,128)S(1)}, u32[]{:S(2)}, u32[]{:S(2)}) collective-permute-start(f32[16,512]{1,0:T(8,128)S(1)} %get-tuple-element.15), channel_id=1, source_target_pairs={{0,32},{8,40},{16,48},{24,56},{32,0},{40,8},{48,16},{56,24},{64,96... | collective-permute-start | bytes 98312 | tf_op jit(solution)/shard_map/ppermute | solution.py:171
  37.6 2.1 %collective-permute-done.6 = f32[16,512]{1,0:T(8,128)S(1)} collective-permute-done((f32[16,512]{1,0:T(8,128)S(1)}, f32[16,512]{1,0:T(8,128)S(1)}, u32[]{:S(2)}, u32[]{:S(2)}) %collective-permute-start.6) | collective-permute-done | bytes 32800 | tf_op jit(solution)/shard_map/ppermute | solution.py:171
  40.4 2.9 %collective-permute-start.8 = (f32[16,512]{1,0:T(8,128)S(1)}, f32[16,512]{1,0:T(8,128)S(1)}, u32[]{:S(2)}, u32[]{:S(2)}) collective-permute-start(f32[16,512]{1,0:T(8,128)S(1)} %multiply_add_fusion.1), channel_id=1, source_target_pairs={{0,64},{8,72},{16,80},{24,88},{32,96},{40,104},{48,112},{56,120},{... | collective-permute-start | bytes 98312 | tf_op jit(solution)/shard_map/ppermute | solution.py:24
  44.7 10.4 %shard_map.87.intra_ref = f32[512,512]{1,0:T(8,128)} custom-call(f32[512,512]{1,0:T(8,128)} %get-tuple-element.5.gated_ref, f32[16,1,512]{2,1,0:T(1,128)} %broadcast_in_dim.56.decay_ref, f32[16,1,512]{2,1,0:T(1,128)} %broadcast_in_dim.57.mixing_ref), custom_call_target="tpu_custom_call" | custom-call | flops 2147483648 | bytes 2097152 | tf_op jit(solution)/shard_map/pallas_call | solution.py:146
  56.2 5.1 %shard_map.88 = bf16[512,512]{1,0:T(8,128)(2,1)} custom-call(f32[512,512]{1,0:T(8,128)} %shard_map.87.intra_ref, f32[16,4,512]{2,1,0:T(4,128)} %maximum_add_fusion.state_ref, f32[16,1,512]{2,1,0:T(1,128)} %broadcast_in_dim.56.decay_ref, f32[16,1,512]{2,1,0:T(1,128)} %broadcast_in_dim.57.mixing_ref, f32[512,512]{1,0:T(8,128)} %get-tuple-element.5.gated_ref, ...), custom_call_target="tpu_custom_call" | custom-call | flops 8388608 | bytes 3670016 | tf_op jit(solution)/shard_map/pallas_call | solution.py:185
  61.3 3.5 %collective-permute-start.11 = (bf16[512,512]{1,0:T(8,128)(2,1)}, bf16[512,512]{1,0:T(8,128)(2,1)S(1)}, u32[]{:S(2)}, u32[]{:S(2)}) collective-permute-start(bf16[512,512]{1,0:T(8,128)(2,1)} %shard_map.88), channel_id=1, source_target_pairs={{1,0},{2,1},{3,2},{4,3},{5,4},{6,5},{7,6},{0,7},{9,8},{10,9},{11,1... | collective-permute-start | bytes 1572872 | tf_op jit(solution)/shard_map/ppermute | solution.py:228
  66.4 2.9 %collective-permute-start.14 = (bf16[512,512]{1,0:T(8,128)(2,1)}, bf16[512,512]{1,0:T(8,128)(2,1)S(1)}, u32[]{:S(2)}, u32[]{:S(2)}) collective-permute-start(bf16[512,512]{1,0:T(8,128)(2,1)} %shard_map.88), channel_id=1, source_target_pairs={{4,0},{5,1},{6,2},{7,3},{0,4},{1,5},{2,6},{3,7},{12,8},{13,9},{14,... | collective-permute-start | bytes 1572872 | tf_op jit(solution)/shard_map/ppermute | solution.py:228
  70.8 19.4 %collective-permute-done.11 = bf16[512,512]{1,0:T(8,128)(2,1)S(1)} collective-permute-done((bf16[512,512]{1,0:T(8,128)(2,1)}, bf16[512,512]{1,0:T(8,128)(2,1)S(1)}, u32[]{:S(2)}, u32[]{:S(2)}) %collective-permute-start.11) | collective-permute-done | bytes 524320 | tf_op jit(solution)/shard_map/ppermute | solution.py:228
  90.1 2.5 %collective-permute-start.16 = (bf16[512,512]{1,0:T(8,128)(2,1)}, bf16[512,512]{1,0:T(8,128)(2,1)S(1)}, u32[]{:S(2)}, u32[]{:S(2)}) collective-permute-start(bf16[512,512]{1,0:T(8,128)(2,1)} %shard_map.88), channel_id=1, source_target_pairs={{6,0},{7,1},{0,2},{1,3},{2,4},{3,5},{4,6},{5,7},{14,8},{15,9},{8,1... | collective-permute-start | bytes 1572872 | tf_op jit(solution)/shard_map/ppermute | solution.py:228
  92.7 18.8 %collective-permute-start.17 = (bf16[512,512]{1,0:T(8,128)(2,1)}, bf16[512,512]{1,0:T(8,128)(2,1)S(1)}, u32[]{:S(2)}, u32[]{:S(2)}) collective-permute-start(bf16[512,512]{1,0:T(8,128)(2,1)} %shard_map.88), channel_id=1, source_target_pairs={{7,0},{0,1},{1,2},{2,3},{3,4},{4,5},{5,6},{6,7},{15,8},{8,9},{9,10... | collective-permute-start | bytes 1572872 | tf_op jit(solution)/shard_map/ppermute | solution.py:228
  111.7 4.8 %collective-permute-done.15 = bf16[512,512]{1,0:T(8,128)(2,1)S(1)} collective-permute-done((bf16[512,512]{1,0:T(8,128)(2,1)}, bf16[512,512]{1,0:T(8,128)(2,1)S(1)}, u32[]{:S(2)}, u32[]{:S(2)}) %collective-permute-start.15) | collective-permute-done | bytes 524320 | tf_op jit(solution)/shard_map/ppermute | solution.py:228
  116.6 12.2 %collective-permute-done.16 = bf16[512,512]{1,0:T(8,128)(2,1)S(1)} collective-permute-done((bf16[512,512]{1,0:T(8,128)(2,1)}, bf16[512,512]{1,0:T(8,128)(2,1)S(1)}, u32[]{:S(2)}, u32[]{:S(2)}) %collective-permute-start.16) | collective-permute-done | bytes 524320 | tf_op jit(solution)/shard_map/ppermute | solution.py:228
  129.4 3.2 %copy-done.1 = bf16[512,8192]{1,0:T(8,128)(2,1)} copy-done((bf16[512,8192]{1,0:T(8,128)(2,1)}, bf16[512,8192]{1,0:T(8,128)(2,1)S(1)}, u32[]{:S(2)}) %copy-start.1) | copy-done | bytes 8388632
  133.6 4.4 %fusion.22 = bf16[512,256]{0,1:T(8,128)(2,1)S(1)} fusion(bf16[4096,768]{0,1:T(8,128)(2,1)} %bitcast.76, f32[4096]{0:T(1024)S(1)} %copy-done.6, f32[512]{0:T(512)S(1)} %add_rsqrt_fusion, bf16[512,8192]{1,0:T(8,128)(2,1)} %copy-done.1, s32[]{:T(128)S(6)} %select_n.119), kind=kOutput, calls=%fused_computation.30 | convolution fusion | flops 1082261504 | bytes 6572036 | tf_op jit(solution)/shard_map/dot_general | solution.py:244
  138.9 4.7 %fusion.16 = bf16[512,512]{0,1:T(8,128)(2,1)S(1)} fusion(bf16[4096,768]{0,1:T(8,128)(2,1)} %bitcast.77, f32[4096]{0:T(1024)S(1)} %copy-done.6, f32[512]{0:T(512)S(1)} %add_rsqrt_fusion, bf16[512,8192]{1,0:T(8,128)(2,1)S(1)} %copy-done.2, s32[]{:T(128)S(6)} %select_n.119), kind=kOutput, calls=%fused_computation.24 | convolution fusion | flops 2156134400 | bytes 8931332 | tf_op jit(solution)/shard_map/dot_general | solution.py:237
  143.6 1.9 %collective-permute-start.18 = (bf16[512,256]{0,1:T(8,128)(2,1)S(1)}, bf16[512,256]{0,1:T(8,128)(2,1)S(1)}, u32[]{:S(2)}, u32[]{:S(2)}) collective-permute-start(bf16[512,256]{0,1:T(8,128)(2,1)S(1)} %get-tuple-element.17), channel_id=1, source_target_pairs={{0,8},{8,16},{16,24},{24,32},{32,40},{40,48},{48,56},{56,64},{64,7... | collective-permute-start | bytes 786440 | tf_op jit(solution)/shard_map/ppermute | solution.py:24
  145.5 3.8 %collective-permute-start.20 = (bf16[512,256]{0,1:T(8,128)(2,1)S(1)}, bf16[512,256]{0,1:T(8,128)(2,1)S(1)}, u32[]{:S(2)}, u32[]{:S(2)}) collective-permute-start(bf16[512,256]{0,1:T(8,128)(2,1)S(1)} %get-tuple-element.18), channel_id=1, source_target_pairs={{0,8},{8,16},{16,24},{24,32},{32,40},{40,48},{48,56},{56,64},{64,7... | collective-permute-start | bytes 786440 | tf_op jit(solution)/shard_map/ppermute | solution.py:24
  150.0 5.6 %collective-permute-done.18 = bf16[512,256]{0,1:T(8,128)(2,1)S(1)} collective-permute-done((bf16[512,256]{0,1:T(8,128)(2,1)S(1)}, bf16[512,256]{0,1:T(8,128)(2,1)S(1)}, u32[]{:S(2)}, u32[]{:S(2)}) %collective-permute-start.18) | collective-permute-done | bytes 262176 | tf_op jit(solution)/shard_map/ppermute | solution.py:24
  157.5 6.1 %collective-permute-done.20 = bf16[512,256]{0,1:T(8,128)(2,1)S(1)} collective-permute-done((bf16[512,256]{0,1:T(8,128)(2,1)S(1)}, bf16[512,256]{0,1:T(8,128)(2,1)S(1)}, u32[]{:S(2)}, u32[]{:S(2)}) %collective-permute-start.20) | collective-permute-done | bytes 262176 | tf_op jit(solution)/shard_map/ppermute | solution.py:24
  163.6 2.1 %collective-permute-start.21 = (bf16[512,256]{0,1:T(8,128)(2,1)S(1)}, bf16[512,256]{0,1:T(8,128)(2,1)S(1)}, u32[]{:S(2)}, u32[]{:S(2)}) collective-permute-start(bf16[512,256]{0,1:T(8,128)(2,1)S(1)} %collective-permute-done.20), channel_id=1, source_target_pairs={{0,8},{8,16},{16,24},{24,32},{32,40},{40,48},{48,56},{56,64},{64,7... | collective-permute-start | bytes 786440 | tf_op jit(solution)/shard_map/ppermute | solution.py:24
  170.7 4.8 %collective-permute-done.21 = bf16[512,256]{0,1:T(8,128)(2,1)S(1)} collective-permute-done((bf16[512,256]{0,1:T(8,128)(2,1)S(1)}, bf16[512,256]{0,1:T(8,128)(2,1)S(1)}, u32[]{:S(2)}, u32[]{:S(2)}) %collective-permute-start.21) | collective-permute-done | bytes 262176 | tf_op jit(solution)/shard_map/ppermute | solution.py:24
  (88 shorter events, 31.1 us)
Async XLA Ops:
  7.2 126.4 %all-gather.2.cloned.1.call-start = ((), (), s32[]{:S(2)}) async-start(), calls=%async_computation | async-start | bytes 6488064 | tf_op jit(solution)/shard_map/all_gather | solution.py:211
  9.7 9.4 %collective-permute-start = (bf16[6,3,512]{2,0,1:T(8,128)(2,1)S(1)}, bf16[6,3,512]{2,0,1:T(8,128)(2,1)S(1)}, u32[]{:S(2)}, u32[]{:S(2)}) collective-permute-start(bf16[6,3,512]{2,0,1:T(8,128)(2,1)S(1)} %slice.27), channel_id=1, source_target_pairs={{0,8},{8,16},{16,24},{24,32},{32,40},{40,48},{48,56},{56,64},{64,7... | collective-permute-start | bytes 55304 | tf_op jit(solution)/shard_map/ppermute | solution.py:24
  29.5 6.0 %collective-permute-start.1 = (f32[16,512]{1,0:T(8,128)S(1)}, f32[16,512]{1,0:T(8,128)S(1)}, u32[]{:S(2)}, u32[]{:S(2)}) collective-permute-start(f32[16,512]{1,0:T(8,128)S(1)} %get-tuple-element.15), channel_id=1, source_target_pairs={{0,8},{8,16},{16,24},{24,32},{32,40},{40,48},{48,56},{56,0},{64,72... | collective-permute-start | bytes 98312 | tf_op jit(solution)/shard_map/ppermute | solution.py:171
  29.5 7.2 %collective-permute-start.2 = (f32[16,512]{1,0:T(8,128)S(1)}, f32[16,512]{1,0:T(8,128)S(1)}, u32[]{:S(2)}, u32[]{:S(2)}) collective-permute-start(f32[16,512]{1,0:T(8,128)S(1)} %get-tuple-element.15), channel_id=1, source_target_pairs={{0,16},{8,24},{16,32},{24,40},{32,48},{40,56},{48,0},{56,8},{64,80... | collective-permute-start | bytes 98312 | tf_op jit(solution)/shard_map/ppermute | solution.py:171
  29.9 7.7 %collective-permute-start.3 = (f32[16,512]{1,0:T(8,128)S(1)}, f32[16,512]{1,0:T(8,128)S(1)}, u32[]{:S(2)}, u32[]{:S(2)}) collective-permute-start(f32[16,512]{1,0:T(8,128)S(1)} %get-tuple-element.15), channel_id=1, source_target_pairs={{0,24},{8,32},{16,40},{24,48},{32,56},{40,0},{48,8},{56,16},{64,88... | collective-permute-start | bytes 98312 | tf_op jit(solution)/shard_map/ppermute | solution.py:171
  30.5 7.1 %collective-permute-start.4 = (f32[16,512]{1,0:T(8,128)S(1)}, f32[16,512]{1,0:T(8,128)S(1)}, u32[]{:S(2)}, u32[]{:S(2)}) collective-permute-start(f32[16,512]{1,0:T(8,128)S(1)} %get-tuple-element.15), channel_id=1, source_target_pairs={{0,32},{8,40},{16,48},{24,56},{32,0},{40,8},{48,16},{56,24},{64,96... | collective-permute-start | bytes 98312 | tf_op jit(solution)/shard_map/ppermute | solution.py:171
  33.9 3.7 %collective-permute-start.5 = (f32[16,512]{1,0:T(8,128)S(1)}, f32[16,512]{1,0:T(8,128)S(1)}, u32[]{:S(2)}, u32[]{:S(2)}) collective-permute-start(f32[16,512]{1,0:T(8,128)S(1)} %get-tuple-element.15), channel_id=1, source_target_pairs={{0,40},{8,48},{16,56},{24,0},{32,8},{40,16},{48,24},{56,32},{64,10... | collective-permute-start | bytes 98312 | tf_op jit(solution)/shard_map/ppermute | solution.py:171
  35.5 4.2 %collective-permute-start.6 = (f32[16,512]{1,0:T(8,128)S(1)}, f32[16,512]{1,0:T(8,128)S(1)}, u32[]{:S(2)}, u32[]{:S(2)}) collective-permute-start(f32[16,512]{1,0:T(8,128)S(1)} %get-tuple-element.15), channel_id=1, source_target_pairs={{0,48},{8,56},{16,0},{24,8},{32,16},{40,24},{48,32},{56,40},{64,11... | collective-permute-start | bytes 98312 | tf_op jit(solution)/shard_map/ppermute | solution.py:171
  36.7 3.0 %collective-permute-start.7 = (f32[16,512]{1,0:T(8,128)S(1)}, f32[16,512]{1,0:T(8,128)S(1)}, u32[]{:S(2)}, u32[]{:S(2)}) collective-permute-start(f32[16,512]{1,0:T(8,128)S(1)} %get-tuple-element.15), channel_id=1, source_target_pairs={{0,56},{8,0},{16,8},{24,16},{32,24},{40,32},{48,40},{56,48},{64,12... | collective-permute-start | bytes 98312 | tf_op jit(solution)/shard_map/ppermute | solution.py:171
  39.8 15.4 %collective-permute-start.10 = (f32[16,512]{1,0:T(8,128)S(1)}, f32[16,512]{1,0:T(8,128)S(1)}, u32[]{:S(2)}, u32[]{:S(2)}) collective-permute-start(f32[16,512]{1,0:T(8,128)S(1)} %multiply_add_fusion.1), channel_id=1, source_target_pairs={{0,192},{8,200},{16,208},{24,216},{32,224},{40,232},{48,240},{56,2... | collective-permute-start | bytes 98312 | tf_op jit(solution)/shard_map/ppermute | solution.py:24
  40.4 14.8 %collective-permute-start.8 = (f32[16,512]{1,0:T(8,128)S(1)}, f32[16,512]{1,0:T(8,128)S(1)}, u32[]{:S(2)}, u32[]{:S(2)}) collective-permute-start(f32[16,512]{1,0:T(8,128)S(1)} %multiply_add_fusion.1), channel_id=1, source_target_pairs={{0,64},{8,72},{16,80},{24,88},{32,96},{40,104},{48,112},{56,120},{... | collective-permute-start | bytes 98312 | tf_op jit(solution)/shard_map/ppermute | solution.py:24
  43.4 11.8 %collective-permute-start.9 = (f32[16,512]{1,0:T(8,128)S(1)}, f32[16,512]{1,0:T(8,128)S(1)}, u32[]{:S(2)}, u32[]{:S(2)}) collective-permute-start(f32[16,512]{1,0:T(8,128)S(1)} %multiply_add_fusion.1), channel_id=1, source_target_pairs={{0,128},{8,136},{16,144},{24,152},{32,160},{40,168},{48,176},{56,1... | collective-permute-start | bytes 98312 | tf_op jit(solution)/shard_map/ppermute | solution.py:24
  61.3 28.9 %collective-permute-start.11 = (bf16[512,512]{1,0:T(8,128)(2,1)}, bf16[512,512]{1,0:T(8,128)(2,1)S(1)}, u32[]{:S(2)}, u32[]{:S(2)}) collective-permute-start(bf16[512,512]{1,0:T(8,128)(2,1)} %shard_map.88), channel_id=1, source_target_pairs={{1,0},{2,1},{3,2},{4,3},{5,4},{6,5},{7,6},{0,7},{9,8},{10,9},{11,1... | collective-permute-start | bytes 1572872 | tf_op jit(solution)/shard_map/ppermute | solution.py:228
  64.7 27.9 %collective-permute-start.12 = (bf16[512,512]{1,0:T(8,128)(2,1)}, bf16[512,512]{1,0:T(8,128)(2,1)S(1)}, u32[]{:S(2)}, u32[]{:S(2)}) collective-permute-start(bf16[512,512]{1,0:T(8,128)(2,1)} %shard_map.88), channel_id=1, source_target_pairs={{2,0},{3,1},{4,2},{5,3},{6,4},{7,5},{0,6},{1,7},{10,8},{11,9},{12,... | collective-permute-start | bytes 1572872 | tf_op jit(solution)/shard_map/ppermute | solution.py:228
  65.5 46.1 %collective-permute-start.13 = (bf16[512,512]{1,0:T(8,128)(2,1)}, bf16[512,512]{1,0:T(8,128)(2,1)S(1)}, u32[]{:S(2)}, u32[]{:S(2)}) collective-permute-start(bf16[512,512]{1,0:T(8,128)(2,1)} %shard_map.88), channel_id=1, source_target_pairs={{3,0},{4,1},{5,2},{6,3},{7,4},{0,5},{1,6},{2,7},{11,8},{12,9},{13,... | collective-permute-start | bytes 1572872 | tf_op jit(solution)/shard_map/ppermute | solution.py:228
  66.4 45.2 %collective-permute-start.14 = (bf16[512,512]{1,0:T(8,128)(2,1)}, bf16[512,512]{1,0:T(8,128)(2,1)S(1)}, u32[]{:S(2)}, u32[]{:S(2)}) collective-permute-start(bf16[512,512]{1,0:T(8,128)(2,1)} %shard_map.88), channel_id=1, source_target_pairs={{4,0},{5,1},{6,2},{7,3},{0,4},{1,5},{2,6},{3,7},{12,8},{13,9},{14,... | collective-permute-start | bytes 1572872 | tf_op jit(solution)/shard_map/ppermute | solution.py:228
  69.4 59.5 %copy-start = (bf16[512,512]{1,0:T(8,128)(2,1)S(1)}, bf16[512,512]{1,0:T(8,128)(2,1)}, u32[]{:S(2)}) copy-start(bf16[512,512]{1,0:T(8,128)(2,1)} %shard_map.88) | copy-start | bytes 1572868
  69.4 47.1 %collective-permute-start.15 = (bf16[512,512]{1,0:T(8,128)(2,1)}, bf16[512,512]{1,0:T(8,128)(2,1)S(1)}, u32[]{:S(2)}, u32[]{:S(2)}) collective-permute-start(bf16[512,512]{1,0:T(8,128)(2,1)} %shard_map.88), channel_id=1, source_target_pairs={{5,0},{6,1},{7,2},{0,3},{1,4},{2,5},{3,6},{4,7},{13,8},{14,9},{15,... | collective-permute-start | bytes 1572872 | tf_op jit(solution)/shard_map/ppermute | solution.py:228
  90.1 38.6 %collective-permute-start.16 = (bf16[512,512]{1,0:T(8,128)(2,1)}, bf16[512,512]{1,0:T(8,128)(2,1)S(1)}, u32[]{:S(2)}, u32[]{:S(2)}) collective-permute-start(bf16[512,512]{1,0:T(8,128)(2,1)} %shard_map.88), channel_id=1, source_target_pairs={{6,0},{7,1},{0,2},{1,3},{2,4},{3,5},{4,6},{5,7},{14,8},{15,9},{8,1... | collective-permute-start | bytes 1572872 | tf_op jit(solution)/shard_map/ppermute | solution.py:228
  92.7 36.1 %collective-permute-start.17 = (bf16[512,512]{1,0:T(8,128)(2,1)}, bf16[512,512]{1,0:T(8,128)(2,1)S(1)}, u32[]{:S(2)}, u32[]{:S(2)}) collective-permute-start(bf16[512,512]{1,0:T(8,128)(2,1)} %shard_map.88), channel_id=1, source_target_pairs={{7,0},{0,1},{1,2},{2,3},{3,4},{4,5},{5,6},{6,7},{15,8},{8,9},{9,10... | collective-permute-start | bytes 1572872 | tf_op jit(solution)/shard_map/ppermute | solution.py:228
  143.6 12.0 %collective-permute-start.18 = (bf16[512,256]{0,1:T(8,128)(2,1)S(1)}, bf16[512,256]{0,1:T(8,128)(2,1)S(1)}, u32[]{:S(2)}, u32[]{:S(2)}) collective-permute-start(bf16[512,256]{0,1:T(8,128)(2,1)S(1)} %get-tuple-element.17), channel_id=1, source_target_pairs={{0,8},{8,16},{16,24},{24,32},{32,40},{40,48},{48,56},{56,64},{64,7... | collective-permute-start | bytes 786440 | tf_op jit(solution)/shard_map/ppermute | solution.py:24
  145.5 18.1 %collective-permute-start.20 = (bf16[512,256]{0,1:T(8,128)(2,1)S(1)}, bf16[512,256]{0,1:T(8,128)(2,1)S(1)}, u32[]{:S(2)}, u32[]{:S(2)}) collective-permute-start(bf16[512,256]{0,1:T(8,128)(2,1)S(1)} %get-tuple-element.18), channel_id=1, source_target_pairs={{0,8},{8,16},{16,24},{24,32},{32,40},{40,48},{48,56},{56,64},{64,7... | collective-permute-start | bytes 786440 | tf_op jit(solution)/shard_map/ppermute | solution.py:24
  155.6 11.9 %collective-permute-start.19 = (bf16[512,256]{0,1:T(8,128)(2,1)S(1)}, bf16[512,256]{0,1:T(8,128)(2,1)S(1)}, u32[]{:S(2)}, u32[]{:S(2)}) collective-permute-start(bf16[512,256]{0,1:T(8,128)(2,1)S(1)} %collective-permute-done.18), channel_id=1, source_target_pairs={{0,8},{8,16},{16,24},{24,32},{32,40},{40,48},{48,56},{56,64},{64,7... | collective-permute-start | bytes 786440 | tf_op jit(solution)/shard_map/ppermute | solution.py:24
  163.6 11.9 %collective-permute-start.21 = (bf16[512,256]{0,1:T(8,128)(2,1)S(1)}, bf16[512,256]{0,1:T(8,128)(2,1)S(1)}, u32[]{:S(2)}, u32[]{:S(2)}) collective-permute-start(bf16[512,256]{0,1:T(8,128)(2,1)S(1)} %collective-permute-done.20), channel_id=1, source_target_pairs={{0,8},{8,16},{16,24},{24,32},{32,40},{40,48},{48,56},{56,64},{64,7... | collective-permute-start | bytes 786440 | tf_op jit(solution)/shard_map/ppermute | solution.py:24
  (6 other events, 60.5 us)
Sparse Core Ops, SparseCore 0:
  11.0 75.2 all-gather.1

commit v6 on v5

--- a/solution.py
+++ b/solution.py
@@ -234,10 +234,11 @@
     inverse = lax.rsqrt(jnp.mean(as_float * as_float, axis=1, keepdims=True) + EPSILON)
     normed = (as_float * inverse * norm_gain[None]).astype(jnp.bfloat16)
     flat_rows = shard_rows.reshape(shard_rows.shape[0], 3 * head_cols)
-    kv_pair = jnp.dot(normed, flat_rows[:, head_cols:], preferred_element_type=jnp.float32).astype(jnp.bfloat16)
+    keys_own = jnp.dot(normed, flat_rows[:, head_cols : 2 * head_cols], preferred_element_type=jnp.float32)
+    values_own = jnp.dot(normed, flat_rows[:, 2 * head_cols :], preferred_element_type=jnp.float32)
     heads = head_cols // HD
-    blocks_k = [kv_pair[:, :head_cols]]
-    blocks_v = [kv_pair[:, head_cols:]]
+    blocks_k = [keys_own.astype(jnp.bfloat16)]
+    blocks_v = [values_own.astype(jnp.bfloat16)]
     for _ in range(WINDOW - 1):
         blocks_k.append(from_behind(blocks_k[-1], "ctx", 1))
         blocks_v.append(from_behind(blocks_v[-1], "ctx", 1))

time: 184 us -> 188 us (1.022); the launches traced: 184 us -> 186 us
    dot_general x1 -> x2, matrix products: 4.68 us -> 7.37 us  [the longest x1 4.37 us: block_body(): jnp.dot(normed, flat_rows[:, head_cols:2 * head_cols], preferred_element_...]
  transfers between devices with their start and end apart: 23 -> 23, of which waited for: 9 -> 9; matrix products, arithmetic and copies ran while one was open for 9% -> 8% of each run, Pallas kernels for 13% -> 13%
where the time goes in v6:
time: 188 us; the launch traced here: 186 us
  waiting for transfers between devices  59.6 us (32%)
  starting transfers between devices  53.3 us (28%)
  Pallas kernels  24.3 us (13%)
  local copies, waits for them, and re-layouts  16.6 us (9%)
  between operations  14.7 us (8%)
  matrix products  13.9 us (7%)
  other arithmetic  3.34 us (2%)
    ppermute x7, waiting for transfers between devices, block_body(): lax.ppermute(mixer, 'tp', [((source + shift) % parts, source) for source...  35.9 us
    ppermute x7, starting transfers between devices, block_body(): lax.ppermute(mixer, 'tp', [((source + shift) % parts, source) for source...  29.7 us
    ppermute x8, waiting for transfers between devices, from_behind(): lax.ppermute(value, axis, [(source, source + steps) for source in range(l...  21.6 us
    ppermute x8, starting transfers between devices, from_behind(): lax.ppermute(value, axis, [(source, source + steps) for source in range(l...  16.4 us
    unnamed x32, local copies, waits for them, and re-layouts  11.1 us
    pallas_call x1, Pallas kernels, intra_call(): pl.pallas_call(intra_kernel, out_shape=whole((tokens, channels), jnp.floa...  10.4 us
    pallas_call x1, Pallas kernels, front_call(): pl.pallas_call(front_kernel, out_shape=(whole((tokens, channels), jnp.flo...  8.79 us
    ppermute x7, starting transfers between devices, exchange_history(): arrived = lax.ppermute(block_end, 'ctx', pairs)  7.21 us
  transfers between devices with their start and end apart: 23, of which 9 were waited for; matrix products, arithmetic and copies ran while one was open for 8% of the time, Pallas kernels for 13%

profile of v6, /device:TPU:128, one launch (start us, length us, event | category | flops | bytes accessed | tf_op | source)
XLA Modules:
  0.0 185.8 jit_solution(13129600128365617582)
XLA Ops:
  16.4 2.7 %collective-permute-done = bf16[6,3,512]{2,0,1:T(8,128)(2,1)S(1)} collective-permute-done((bf16[6,3,512]{2,0,1:T(8,128)(2,1)S(1)}, bf16[6,3,512]{2,0,1:T(8,128)(2,1)S(1)}, u32[]{:S(2)}, u32[]{:S(2)}) %collective-permute-start) | collective-permute-done | bytes 18464 | tf_op jit(solution)/shard_map/ppermute | solution.py:24
  19.7 8.8 %shard_map.86 = (f32[512,512]{1,0:T(8,128)}, f32[512,512]{1,0:T(8,128)}, f32[16,4,512]{2,1,0:T(4,128)}) custom-call(bf16[512,1536]{1,0:T(8,128)(2,1)} %copy.27.feat_ref, bf16[6,1536]{1,0:T(8,128)(2,1)} %bitcast.80, f32[3,7,512]{2,1,0:T(8,128)} %taps_ref.1, f32[16,1,512]{2,1,0:T(1,128)} %broadcast_in_dim.56.decay_ref), custom_call_target="tpu_custom_call" | custom-call | flops 19398656 | bytes 3670016 | tf_op jit(solution)/shard_map/pallas_call | solution.py:98
  30.5 3.4 %collective-permute-start.4 = (f32[16,512]{1,0:T(8,128)S(1)}, f32[16,512]{1,0:T(8,128)S(1)}, u32[]{:S(2)}, u32[]{:S(2)}) collective-permute-start(f32[16,512]{1,0:T(8,128)S(1)} %get-tuple-element.15), channel_id=1, source_target_pairs={{0,32},{8,40},{16,48},{24,56},{32,0},{40,8},{48,16},{56,24},{64,96... | collective-permute-start | bytes 98312 | tf_op jit(solution)/shard_map/ppermute | solution.py:171
  37.6 2.1 %collective-permute-done.6 = f32[16,512]{1,0:T(8,128)S(1)} collective-permute-done((f32[16,512]{1,0:T(8,128)S(1)}, f32[16,512]{1,0:T(8,128)S(1)}, u32[]{:S(2)}, u32[]{:S(2)}) %collective-permute-start.6) | collective-permute-done | bytes 32800 | tf_op jit(solution)/shard_map/ppermute | solution.py:171
  40.4 2.9 %collective-permute-start.8 = (f32[16,512]{1,0:T(8,128)S(1)}, f32[16,512]{1,0:T(8,128)S(1)}, u32[]{:S(2)}, u32[]{:S(2)}) collective-permute-start(f32[16,512]{1,0:T(8,128)S(1)} %multiply_add_fusion.1), channel_id=1, source_target_pairs={{0,64},{8,72},{16,80},{24,88},{32,96},{40,104},{48,112},{56,120},{... | collective-permute-start | bytes 98312 | tf_op jit(solution)/shard_map/ppermute | solution.py:24
  44.7 10.4 %shard_map.87.intra_ref = f32[512,512]{1,0:T(8,128)} custom-call(f32[512,512]{1,0:T(8,128)} %get-tuple-element.5.gated_ref, f32[16,1,512]{2,1,0:T(1,128)} %broadcast_in_dim.56.decay_ref, f32[16,1,512]{2,1,0:T(1,128)} %broadcast_in_dim.57.mixing_ref), custom_call_target="tpu_custom_call" | custom-call | flops 2147483648 | bytes 2097152 | tf_op jit(solution)/shard_map/pallas_call | solution.py:146
  56.1 5.1 %shard_map.88 = bf16[512,512]{1,0:T(8,128)(2,1)} custom-call(f32[512,512]{1,0:T(8,128)} %shard_map.87.intra_ref, f32[16,4,512]{2,1,0:T(4,128)} %maximum_add_fusion.state_ref, f32[16,1,512]{2,1,0:T(1,128)} %broadcast_in_dim.56.decay_ref, f32[16,1,512]{2,1,0:T(1,128)} %broadcast_in_dim.57.mixing_ref, f32[512,512]{1,0:T(8,128)} %get-tuple-element.5.gated_ref, ...), custom_call_target="tpu_custom_call" | custom-call | flops 8388608 | bytes 3670016 | tf_op jit(solution)/shard_map/pallas_call | solution.py:185
  61.2 3.5 %collective-permute-start.11 = (bf16[512,512]{1,0:T(8,128)(2,1)}, bf16[512,512]{1,0:T(8,128)(2,1)S(1)}, u32[]{:S(2)}, u32[]{:S(2)}) collective-permute-start(bf16[512,512]{1,0:T(8,128)(2,1)} %shard_map.88), channel_id=1, source_target_pairs={{1,0},{2,1},{3,2},{4,3},{5,4},{6,5},{7,6},{0,7},{9,8},{10,9},{11,1... | collective-permute-start | bytes 1572872 | tf_op jit(solution)/shard_map/ppermute | solution.py:228
  66.4 2.9 %collective-permute-start.14 = (bf16[512,512]{1,0:T(8,128)(2,1)}, bf16[512,512]{1,0:T(8,128)(2,1)S(1)}, u32[]{:S(2)}, u32[]{:S(2)}) collective-permute-start(bf16[512,512]{1,0:T(8,128)(2,1)} %shard_map.88), channel_id=1, source_target_pairs={{4,0},{5,1},{6,2},{7,3},{0,4},{1,5},{2,6},{3,7},{12,8},{13,9},{14,... | collective-permute-start | bytes 1572872 | tf_op jit(solution)/shard_map/ppermute | solution.py:228
  70.8 19.0 %collective-permute-done.11 = bf16[512,512]{1,0:T(8,128)(2,1)S(1)} collective-permute-done((bf16[512,512]{1,0:T(8,128)(2,1)}, bf16[512,512]{1,0:T(8,128)(2,1)S(1)}, u32[]{:S(2)}, u32[]{:S(2)}) %collective-permute-start.11) | collective-permute-done | bytes 524320 | tf_op jit(solution)/shard_map/ppermute | solution.py:228
  89.7 2.8 %collective-permute-start.16 = (bf16[512,512]{1,0:T(8,128)(2,1)}, bf16[512,512]{1,0:T(8,128)(2,1)S(1)}, u32[]{:S(2)}, u32[]{:S(2)}) collective-permute-start(bf16[512,512]{1,0:T(8,128)(2,1)} %shard_map.88), channel_id=1, source_target_pairs={{6,0},{7,1},{0,2},{1,3},{2,4},{3,5},{4,6},{5,7},{14,8},{15,9},{8,1... | collective-permute-start | bytes 1572872 | tf_op jit(solution)/shard_map/ppermute | solution.py:228
  92.6 18.9 %collective-permute-start.17 = (bf16[512,512]{1,0:T(8,128)(2,1)}, bf16[512,512]{1,0:T(8,128)(2,1)S(1)}, u32[]{:S(2)}, u32[]{:S(2)}) collective-permute-start(bf16[512,512]{1,0:T(8,128)(2,1)} %shard_map.88), channel_id=1, source_target_pairs={{7,0},{0,1},{1,2},{2,3},{3,4},{4,5},{5,6},{6,7},{15,8},{8,9},{9,10... | collective-permute-start | bytes 1572872 | tf_op jit(solution)/shard_map/ppermute | solution.py:228
  111.7 4.7 %collective-permute-done.15 = bf16[512,512]{1,0:T(8,128)(2,1)S(1)} collective-permute-done((bf16[512,512]{1,0:T(8,128)(2,1)}, bf16[512,512]{1,0:T(8,128)(2,1)S(1)}, u32[]{:S(2)}, u32[]{:S(2)}) %collective-permute-start.15) | collective-permute-done | bytes 524320 | tf_op jit(solution)/shard_map/ppermute | solution.py:228
  116.4 12.2 %collective-permute-done.16 = bf16[512,512]{1,0:T(8,128)(2,1)S(1)} collective-permute-done((bf16[512,512]{1,0:T(8,128)(2,1)}, bf16[512,512]{1,0:T(8,128)(2,1)S(1)}, u32[]{:S(2)}, u32[]{:S(2)}) %collective-permute-start.16) | collective-permute-done | bytes 524320 | tf_op jit(solution)/shard_map/ppermute | solution.py:228
  129.3 3.2 %copy-done.1 = bf16[512,8192]{1,0:T(8,128)(2,1)} copy-done((bf16[512,8192]{1,0:T(8,128)(2,1)}, bf16[512,8192]{1,0:T(8,128)(2,1)S(1)}, u32[]{:S(2)}) %copy-start.1) | copy-done | bytes 8388632
  133.5 4.4 %fusion.27 = bf16[512,256]{0,1:T(8,128)(2,1)S(1)} fusion(bf16[4096,768]{0,1:T(8,128)(2,1)} %bitcast.75, f32[4096]{0:T(1024)S(1)} %copy-done.6, f32[512]{0:T(512)S(1)} %add_rsqrt_fusion, bf16[512,8192]{1,0:T(8,128)(2,1)} %copy-done.1, s32[]{:T(128)S(6)} %select_n.119), kind=kOutput, calls=%fused_computation.33 | convolution fusion | flops 1082261504 | bytes 6572036 | tf_op jit(solution)/shard_map/dot_general | solution.py:237
  138.8 3.0 %fusion.24 = bf16[512,256]{0,1:T(8,128)(2,1)S(1)} fusion(bf16[4096,768]{0,1:T(8,128)(2,1)} %bitcast.76, f32[4096]{0:T(1024)S(1)} %copy-done.6, f32[512]{0:T(512)S(1)} %add_rsqrt_fusion, bf16[512,8192]{1,0:T(8,128)(2,1)S(1)} %copy-done.2, s32[]{:T(128)S(6)} %select_n.119), kind=kOutput, calls=%fused_computation.32 | convolution fusion | flops 1082261504 | bytes 6572036 | tf_op jit(solution)/shard_map/dot_general | solution.py:245
  141.7 3.0 %fusion.21 = bf16[512,256]{0,1:T(8,128)(2,1)S(1)} fusion(bf16[4096,768]{0,1:T(8,128)(2,1)} %bitcast.77, f32[4096]{0:T(1024)S(1)} %copy-done.6, f32[512]{0:T(512)S(1)} %add_rsqrt_fusion, bf16[512,8192]{1,0:T(8,128)(2,1)S(1)} %copy-done.2, s32[]{:T(128)S(6)} %select_n.119), kind=kOutput, calls=%fused_computation.31 | convolution fusion | flops 1082261504 | bytes 6572036 | tf_op jit(solution)/shard_map/dot_general | solution.py:238
  146.7 3.6 %collective-permute-start.20 = (bf16[512,256]{0,1:T(8,128)(2,1)S(1)}, bf16[512,256]{0,1:T(8,128)(2,1)S(1)}, u32[]{:S(2)}, u32[]{:S(2)}) collective-permute-start(bf16[512,256]{0,1:T(8,128)(2,1)S(1)} %fusion.21), channel_id=1, source_target_pairs={{0,8},{8,16},{16,24},{24,32},{32,40},{40,48},{48,56},{56,64},{64,7... | collective-permute-start | bytes 786440 | tf_op jit(solution)/shard_map/ppermute | solution.py:24
  150.9 5.8 %collective-permute-done.18 = bf16[512,256]{0,1:T(8,128)(2,1)S(1)} collective-permute-done((bf16[512,256]{0,1:T(8,128)(2,1)S(1)}, bf16[512,256]{0,1:T(8,128)(2,1)S(1)}, u32[]{:S(2)}, u32[]{:S(2)}) %collective-permute-start.18) | collective-permute-done | bytes 262176 | tf_op jit(solution)/shard_map/ppermute | solution.py:24
  158.7 4.3 %collective-permute-done.20 = bf16[512,256]{0,1:T(8,128)(2,1)S(1)} collective-permute-done((bf16[512,256]{0,1:T(8,128)(2,1)S(1)}, bf16[512,256]{0,1:T(8,128)(2,1)S(1)}, u32[]{:S(2)}, u32[]{:S(2)}) %collective-permute-start.20) | collective-permute-done | bytes 262176 | tf_op jit(solution)/shard_map/ppermute | solution.py:24
  163.0 2.1 %collective-permute-start.21 = (bf16[512,256]{0,1:T(8,128)(2,1)S(1)}, bf16[512,256]{0,1:T(8,128)(2,1)S(1)}, u32[]{:S(2)}, u32[]{:S(2)}) collective-permute-start(bf16[512,256]{0,1:T(8,128)(2,1)S(1)} %collective-permute-done.20), channel_id=1, source_target_pairs={{0,8},{8,16},{16,24},{24,32},{32,40},{40,48},{48,56},{56,64},{64,7... | collective-permute-start | bytes 786440 | tf_op jit(solution)/shard_map/ppermute | solution.py:24
  165.6 3.1 %collective-permute-done.19 = bf16[512,256]{0,1:T(8,128)(2,1)S(1)} collective-permute-done((bf16[512,256]{0,1:T(8,128)(2,1)S(1)}, bf16[512,256]{0,1:T(8,128)(2,1)S(1)}, u32[]{:S(2)}, u32[]{:S(2)}) %collective-permute-start.19) | collective-permute-done | bytes 262176 | tf_op jit(solution)/shard_map/ppermute | solution.py:24
  172.0 5.5 %collective-permute-done.21 = bf16[512,256]{0,1:T(8,128)(2,1)S(1)} collective-permute-done((bf16[512,256]{0,1:T(8,128)(2,1)S(1)}, bf16[512,256]{0,1:T(8,128)(2,1)S(1)}, u32[]{:S(2)}, u32[]{:S(2)}) %collective-permute-start.21) | collective-permute-done | bytes 262176 | tf_op jit(solution)/shard_map/ppermute | solution.py:24
  (88 shorter events, 33.5 us)
Async XLA Ops:
  7.2 126.3 %all-gather.2.cloned.1.call-start = ((), (), s32[]{:S(2)}) async-start(), calls=%async_computation | async-start | bytes 6488064 | tf_op jit(solution)/shard_map/all_gather | solution.py:211
  9.7 9.4 %collective-permute-start = (bf16[6,3,512]{2,0,1:T(8,128)(2,1)S(1)}, bf16[6,3,512]{2,0,1:T(8,128)(2,1)S(1)}, u32[]{:S(2)}, u32[]{:S(2)}) collective-permute-start(bf16[6,3,512]{2,0,1:T(8,128)(2,1)S(1)} %slice.24), channel_id=1, source_target_pairs={{0,8},{8,16},{16,24},{24,32},{32,40},{40,48},{48,56},{56,64},{64,7... | collective-permute-start | bytes 55304 | tf_op jit(solution)/shard_map/ppermute | solution.py:24
  29.5 6.0 %collective-permute-start.1 = (f32[16,512]{1,0:T(8,128)S(1)}, f32[16,512]{1,0:T(8,128)S(1)}, u32[]{:S(2)}, u32[]{:S(2)}) collective-permute-start(f32[16,512]{1,0:T(8,128)S(1)} %get-tuple-element.15), channel_id=1, source_target_pairs={{0,8},{8,16},{16,24},{24,32},{32,40},{40,48},{48,56},{56,0},{64,72... | collective-permute-start | bytes 98312 | tf_op jit(solution)/shard_map/ppermute | solution.py:171
  29.5 7.2 %collective-permute-start.2 = (f32[16,512]{1,0:T(8,128)S(1)}, f32[16,512]{1,0:T(8,128)S(1)}, u32[]{:S(2)}, u32[]{:S(2)}) collective-permute-start(f32[16,512]{1,0:T(8,128)S(1)} %get-tuple-element.15), channel_id=1, source_target_pairs={{0,16},{8,24},{16,32},{24,40},{32,48},{40,56},{48,0},{56,8},{64,80... | collective-permute-start | bytes 98312 | tf_op jit(solution)/shard_map/ppermute | solution.py:171
  29.9 7.7 %collective-permute-start.3 = (f32[16,512]{1,0:T(8,128)S(1)}, f32[16,512]{1,0:T(8,128)S(1)}, u32[]{:S(2)}, u32[]{:S(2)}) collective-permute-start(f32[16,512]{1,0:T(8,128)S(1)} %get-tuple-element.15), channel_id=1, source_target_pairs={{0,24},{8,32},{16,40},{24,48},{32,56},{40,0},{48,8},{56,16},{64,88... | collective-permute-start | bytes 98312 | tf_op jit(solution)/shard_map/ppermute | solution.py:171
  30.5 7.1 %collective-permute-start.4 = (f32[16,512]{1,0:T(8,128)S(1)}, f32[16,512]{1,0:T(8,128)S(1)}, u32[]{:S(2)}, u32[]{:S(2)}) collective-permute-start(f32[16,512]{1,0:T(8,128)S(1)} %get-tuple-element.15), channel_id=1, source_target_pairs={{0,32},{8,40},{16,48},{24,56},{32,0},{40,8},{48,16},{56,24},{64,96... | collective-permute-start | bytes 98312 | tf_op jit(solution)/shard_map/ppermute | solution.py:171
  33.9 3.6 %collective-permute-start.5 = (f32[16,512]{1,0:T(8,128)S(1)}, f32[16,512]{1,0:T(8,128)S(1)}, u32[]{:S(2)}, u32[]{:S(2)}) collective-permute-start(f32[16,512]{1,0:T(8,128)S(1)} %get-tuple-element.15), channel_id=1, source_target_pairs={{0,40},{8,48},{16,56},{24,0},{32,8},{40,16},{48,24},{56,32},{64,10... | collective-permute-start | bytes 98312 | tf_op jit(solution)/shard_map/ppermute | solution.py:171
  35.5 4.2 %collective-permute-start.6 = (f32[16,512]{1,0:T(8,128)S(1)}, f32[16,512]{1,0:T(8,128)S(1)}, u32[]{:S(2)}, u32[]{:S(2)}) collective-permute-start(f32[16,512]{1,0:T(8,128)S(1)} %get-tuple-element.15), channel_id=1, source_target_pairs={{0,48},{8,56},{16,0},{24,8},{32,16},{40,24},{48,32},{56,40},{64,11... | collective-permute-start | bytes 98312 | tf_op jit(solution)/shard_map/ppermute | solution.py:171
  36.7 3.0 %collective-permute-start.7 = (f32[16,512]{1,0:T(8,128)S(1)}, f32[16,512]{1,0:T(8,128)S(1)}, u32[]{:S(2)}, u32[]{:S(2)}) collective-permute-start(f32[16,512]{1,0:T(8,128)S(1)} %get-tuple-element.15), channel_id=1, source_target_pairs={{0,56},{8,0},{16,8},{24,16},{32,24},{40,32},{48,40},{56,48},{64,12... | collective-permute-start | bytes 98312 | tf_op jit(solution)/shard_map/ppermute | solution.py:171
  39.7 15.4 %collective-permute-start.10 = (f32[16,512]{1,0:T(8,128)S(1)}, f32[16,512]{1,0:T(8,128)S(1)}, u32[]{:S(2)}, u32[]{:S(2)}) collective-permute-start(f32[16,512]{1,0:T(8,128)S(1)} %multiply_add_fusion.1), channel_id=1, source_target_pairs={{0,192},{8,200},{16,208},{24,216},{32,224},{40,232},{48,240},{56,2... | collective-permute-start | bytes 98312 | tf_op jit(solution)/shard_map/ppermute | solution.py:24
  40.4 14.8 %collective-permute-start.8 = (f32[16,512]{1,0:T(8,128)S(1)}, f32[16,512]{1,0:T(8,128)S(1)}, u32[]{:S(2)}, u32[]{:S(2)}) collective-permute-start(f32[16,512]{1,0:T(8,128)S(1)} %multiply_add_fusion.1), channel_id=1, source_target_pairs={{0,64},{8,72},{16,80},{24,88},{32,96},{40,104},{48,112},{56,120},{... | collective-permute-start | bytes 98312 | tf_op jit(solution)/shard_map/ppermute | solution.py:24
  43.4 11.8 %collective-permute-start.9 = (f32[16,512]{1,0:T(8,128)S(1)}, f32[16,512]{1,0:T(8,128)S(1)}, u32[]{:S(2)}, u32[]{:S(2)}) collective-permute-start(f32[16,512]{1,0:T(8,128)S(1)} %multiply_add_fusion.1), channel_id=1, source_target_pairs={{0,128},{8,136},{16,144},{24,152},{32,160},{40,168},{48,176},{56,1... | collective-permute-start | bytes 98312 | tf_op jit(solution)/shard_map/ppermute | solution.py:24
  61.2 28.5 %collective-permute-start.11 = (bf16[512,512]{1,0:T(8,128)(2,1)}, bf16[512,512]{1,0:T(8,128)(2,1)S(1)}, u32[]{:S(2)}, u32[]{:S(2)}) collective-permute-start(bf16[512,512]{1,0:T(8,128)(2,1)} %shard_map.88), channel_id=1, source_target_pairs={{1,0},{2,1},{3,2},{4,3},{5,4},{6,5},{7,6},{0,7},{9,8},{10,9},{11,1... | collective-permute-start | bytes 1572872 | tf_op jit(solution)/shard_map/ppermute | solution.py:228
  64.7 27.9 %collective-permute-start.12 = (bf16[512,512]{1,0:T(8,128)(2,1)}, bf16[512,512]{1,0:T(8,128)(2,1)S(1)}, u32[]{:S(2)}, u32[]{:S(2)}) collective-permute-start(bf16[512,512]{1,0:T(8,128)(2,1)} %shard_map.88), channel_id=1, source_target_pairs={{2,0},{3,1},{4,2},{5,3},{6,4},{7,5},{0,6},{1,7},{10,8},{11,9},{12,... | collective-permute-start | bytes 1572872 | tf_op jit(solution)/shard_map/ppermute | solution.py:228
  65.5 46.1 %collective-permute-start.13 = (bf16[512,512]{1,0:T(8,128)(2,1)}, bf16[512,512]{1,0:T(8,128)(2,1)S(1)}, u32[]{:S(2)}, u32[]{:S(2)}) collective-permute-start(bf16[512,512]{1,0:T(8,128)(2,1)} %shard_map.88), channel_id=1, source_target_pairs={{3,0},{4,1},{5,2},{6,3},{7,4},{0,5},{1,6},{2,7},{11,8},{12,9},{13,... | collective-permute-start | bytes 1572872 | tf_op jit(solution)/shard_map/ppermute | solution.py:228
  66.4 45.3 %collective-permute-start.14 = (bf16[512,512]{1,0:T(8,128)(2,1)}, bf16[512,512]{1,0:T(8,128)(2,1)S(1)}, u32[]{:S(2)}, u32[]{:S(2)}) collective-permute-start(bf16[512,512]{1,0:T(8,128)(2,1)} %shard_map.88), channel_id=1, source_target_pairs={{4,0},{5,1},{6,2},{7,3},{0,4},{1,5},{2,6},{3,7},{12,8},{13,9},{14,... | collective-permute-start | bytes 1572872 | tf_op jit(solution)/shard_map/ppermute | solution.py:228
  69.4 59.4 %copy-start = (bf16[512,512]{1,0:T(8,128)(2,1)S(1)}, bf16[512,512]{1,0:T(8,128)(2,1)}, u32[]{:S(2)}) copy-start(bf16[512,512]{1,0:T(8,128)(2,1)} %shard_map.88) | copy-start | bytes 1572868
  69.4 47.0 %collective-permute-start.15 = (bf16[512,512]{1,0:T(8,128)(2,1)}, bf16[512,512]{1,0:T(8,128)(2,1)S(1)}, u32[]{:S(2)}, u32[]{:S(2)}) collective-permute-start(bf16[512,512]{1,0:T(8,128)(2,1)} %shard_map.88), channel_id=1, source_target_pairs={{5,0},{6,1},{7,2},{0,3},{1,4},{2,5},{3,6},{4,7},{13,8},{14,9},{15,... | collective-permute-start | bytes 1572872 | tf_op jit(solution)/shard_map/ppermute | solution.py:228
  89.7 38.9 %collective-permute-start.16 = (bf16[512,512]{1,0:T(8,128)(2,1)}, bf16[512,512]{1,0:T(8,128)(2,1)S(1)}, u32[]{:S(2)}, u32[]{:S(2)}) collective-permute-start(bf16[512,512]{1,0:T(8,128)(2,1)} %shard_map.88), channel_id=1, source_target_pairs={{6,0},{7,1},{0,2},{1,3},{2,4},{3,5},{4,6},{5,7},{14,8},{15,9},{8,1... | collective-permute-start | bytes 1572872 | tf_op jit(solution)/shard_map/ppermute | solution.py:228
  92.6 36.1 %collective-permute-start.17 = (bf16[512,512]{1,0:T(8,128)(2,1)}, bf16[512,512]{1,0:T(8,128)(2,1)S(1)}, u32[]{:S(2)}, u32[]{:S(2)}) collective-permute-start(bf16[512,512]{1,0:T(8,128)(2,1)} %shard_map.88), channel_id=1, source_target_pairs={{7,0},{0,1},{1,2},{2,3},{3,4},{4,5},{5,6},{6,7},{15,8},{8,9},{9,10... | collective-permute-start | bytes 1572872 | tf_op jit(solution)/shard_map/ppermute | solution.py:228
  144.8 12.0 %collective-permute-start.18 = (bf16[512,256]{0,1:T(8,128)(2,1)S(1)}, bf16[512,256]{0,1:T(8,128)(2,1)S(1)}, u32[]{:S(2)}, u32[]{:S(2)}) collective-permute-start(bf16[512,256]{0,1:T(8,128)(2,1)S(1)} %fusion.27), channel_id=1, source_target_pairs={{0,8},{8,16},{16,24},{24,32},{32,40},{40,48},{48,56},{56,64},{64,7... | collective-permute-start | bytes 786440 | tf_op jit(solution)/shard_map/ppermute | solution.py:24
  146.7 16.3 %collective-permute-start.20 = (bf16[512,256]{0,1:T(8,128)(2,1)S(1)}, bf16[512,256]{0,1:T(8,128)(2,1)S(1)}, u32[]{:S(2)}, u32[]{:S(2)}) collective-permute-start(bf16[512,256]{0,1:T(8,128)(2,1)S(1)} %fusion.21), channel_id=1, source_target_pairs={{0,8},{8,16},{16,24},{24,32},{32,40},{40,48},{48,56},{56,64},{64,7... | collective-permute-start | bytes 786440 | tf_op jit(solution)/shard_map/ppermute | solution.py:24
  156.8 12.0 %collective-permute-start.19 = (bf16[512,256]{0,1:T(8,128)(2,1)S(1)}, bf16[512,256]{0,1:T(8,128)(2,1)S(1)}, u32[]{:S(2)}, u32[]{:S(2)}) collective-permute-start(bf16[512,256]{0,1:T(8,128)(2,1)S(1)} %collective-permute-done.18), channel_id=1, source_target_pairs={{0,8},{8,16},{16,24},{24,32},{32,40},{40,48},{48,56},{56,64},{64,7... | collective-permute-start | bytes 786440 | tf_op jit(solution)/shard_map/ppermute | solution.py:24
  163.0 14.5 %collective-permute-start.21 = (bf16[512,256]{0,1:T(8,128)(2,1)S(1)}, bf16[512,256]{0,1:T(8,128)(2,1)S(1)}, u32[]{:S(2)}, u32[]{:S(2)}) collective-permute-start(bf16[512,256]{0,1:T(8,128)(2,1)S(1)} %collective-permute-done.20), channel_id=1, source_target_pairs={{0,8},{8,16},{16,24},{24,32},{32,40},{40,48},{48,56},{56,64},{64,7... | collective-permute-start | bytes 786440 | tf_op jit(solution)/shard_map/ppermute | solution.py:24
  (6 other events, 60.4 us)
Sparse Core Ops, SparseCore 0:
  11.0 75.1 all-gather.1

commit v7 on v5

--- a/solution.py
+++ b/solution.py
@@ -236,11 +236,14 @@
     flat_rows = shard_rows.reshape(shard_rows.shape[0], 3 * head_cols)
     kv_pair = jnp.dot(normed, flat_rows[:, head_cols:], preferred_element_type=jnp.float32).astype(jnp.bfloat16)
     heads = head_cols // HD
-    blocks_k = [kv_pair[:, :head_cols]]
-    blocks_v = [kv_pair[:, head_cols:]]
+    head_k = [[kv_pair[:, h * HD : (h + 1) * HD]] for h in range(heads)]
+    head_v = [[kv_pair[:, head_cols + h * HD : head_cols + (h + 1) * HD]] for h in range(heads)]
     for _ in range(WINDOW - 1):
-        blocks_k.append(from_behind(blocks_k[-1], "ctx", 1))
-        blocks_v.append(from_behind(blocks_v[-1], "ctx", 1))
+        for h in range(heads):
+            head_k[h].append(from_behind(head_k[h][-1], "ctx", 1))
+            head_v[h].append(from_behind(head_v[h][-1], "ctx", 1))
+    blocks_k = [jnp.concatenate([head_k[h][lag] for h in range(heads)], axis=1) for lag in range(WINDOW)]
+    blocks_v = [jnp.concatenate([head_v[h][lag] for h in range(heads)], axis=1) for lag in range(WINDOW)]
     projected_q = jnp.dot(normed, flat_rows[:, :head_cols], preferred_element_type=jnp.float32).astype(jnp.bfloat16)
     query = projected_q.reshape(tok_dev, heads, HD)
     position = lax.axis_index("ctx")

time: 184 us -> 183 us (level)
  waiting for transfers between devices: 58.9 us -> 49.5 us
  starting transfers between devices: 53.2 us -> 61.6 us
    ppermute x8 -> x12, waiting for transfers between devices: 20.4 us -> 11 us  [from_behind(): lax.ppermute(value, axis, [(source, source + steps) for source in range(l...]
    ppermute x8 -> x12, starting transfers between devices: 16.6 us -> 25 us  [from_behind(): lax.ppermute(value, axis, [(source, source + steps) for source in range(l...]
  transfers between devices with their start and end apart: 23 -> 27, of which waited for: 9 -> 10; matrix products, arithmetic and copies ran while one was open for 9% -> 9% of each run, Pallas kernels for 13% -> 13%
where the time goes in v7:
time: 183 us; the launch traced here: 182 us
  starting transfers between devices  61.6 us (34%)
  waiting for transfers between devices  49.5 us (27%)
  Pallas kernels  24.3 us (13%)
  local copies, waits for them, and re-layouts  15.8 us (9%)
  between operations  14.8 us (8%)
  matrix products  12.6 us (7%)
  other arithmetic  3.41 us (2%)
    ppermute x7, waiting for transfers between devices, block_body(): lax.ppermute(mixer, 'tp', [((source + shift) % parts, source) for source...  36.3 us
    ppermute x7, starting transfers between devices, block_body(): lax.ppermute(mixer, 'tp', [((source + shift) % parts, source) for source...  29.3 us
    ppermute x12, starting transfers between devices, from_behind(): lax.ppermute(value, axis, [(source, source + steps) for source in range(l...  25 us
    ppermute x12, waiting for transfers between devices, from_behind(): lax.ppermute(value, axis, [(source, source + steps) for source in range(l...  11 us
    pallas_call x1, Pallas kernels, intra_call(): pl.pallas_call(intra_kernel, out_shape=whole((tokens, channels), jnp.floa...  10.4 us
    unnamed x32, local copies, waits for them, and re-layouts  10.3 us
    pallas_call x1, Pallas kernels, front_call(): pl.pallas_call(front_kernel, out_shape=(whole((tokens, channels), jnp.flo...  8.79 us
    ppermute x7, starting transfers between devices, exchange_history(): arrived = lax.ppermute(block_end, 'ctx', pairs)  7.21 us
  transfers between devices with their start and end apart: 27, of which 10 were waited for; matrix products, arithmetic and copies ran while one was open for 9% of the time, Pallas kernels for 13%

profile of v7, /device:TPU:128, one launch (start us, length us, event | category | flops | bytes accessed | tf_op | source)
XLA Modules:
  0.0 182.1 jit_solution(10829817741293033654)
XLA Ops:
  9.7 1.9 %collective-permute-start = (bf16[6,3,512]{2,0,1:T(8,128)(2,1)S(1)}, bf16[6,3,512]{2,0,1:T(8,128)(2,1)S(1)}, u32[]{:S(2)}, u32[]{:S(2)}) collective-permute-start(bf16[6,3,512]{2,0,1:T(8,128)(2,1)S(1)} %slice.35), channel_id=1, source_target_pairs={{0,8},{8,16},{16,24},{24,32},{32,40},{40,48},{48,56},{56,64},{64,7... | collective-permute-start | bytes 55304 | tf_op jit(solution)/shard_map/ppermute | solution.py:24
  16.4 2.7 %collective-permute-done = bf16[6,3,512]{2,0,1:T(8,128)(2,1)S(1)} collective-permute-done((bf16[6,3,512]{2,0,1:T(8,128)(2,1)S(1)}, bf16[6,3,512]{2,0,1:T(8,128)(2,1)S(1)}, u32[]{:S(2)}, u32[]{:S(2)}) %collective-permute-start) | collective-permute-done | bytes 18464 | tf_op jit(solution)/shard_map/ppermute | solution.py:24
  19.7 8.8 %shard_map.86 = (f32[512,512]{1,0:T(8,128)}, f32[512,512]{1,0:T(8,128)}, f32[16,4,512]{2,1,0:T(4,128)}) custom-call(bf16[512,1536]{1,0:T(8,128)(2,1)} %copy.27.feat_ref, bf16[6,1536]{1,0:T(8,128)(2,1)} %bitcast.79, f32[3,7,512]{2,1,0:T(8,128)} %taps_ref.1, f32[16,1,512]{2,1,0:T(1,128)} %broadcast_in_dim.56.decay_ref), custom_call_target="tpu_custom_call" | custom-call | flops 19398656 | bytes 3670016 | tf_op jit(solution)/shard_map/pallas_call | solution.py:98
  30.5 3.4 %collective-permute-start.4 = (f32[16,512]{1,0:T(8,128)S(1)}, f32[16,512]{1,0:T(8,128)S(1)}, u32[]{:S(2)}, u32[]{:S(2)}) collective-permute-start(f32[16,512]{1,0:T(8,128)S(1)} %get-tuple-element.15), channel_id=1, source_target_pairs={{0,32},{8,40},{16,48},{24,56},{32,0},{40,8},{48,16},{56,24},{64,96... | collective-permute-start | bytes 98312 | tf_op jit(solution)/shard_map/ppermute | solution.py:171
  37.6 2.1 %collective-permute-done.6 = f32[16,512]{1,0:T(8,128)S(1)} collective-permute-done((f32[16,512]{1,0:T(8,128)S(1)}, f32[16,512]{1,0:T(8,128)S(1)}, u32[]{:S(2)}, u32[]{:S(2)}) %collective-permute-start.6) | collective-permute-done | bytes 32800 | tf_op jit(solution)/shard_map/ppermute | solution.py:171
  40.4 2.9 %collective-permute-start.8 = (f32[16,512]{1,0:T(8,128)S(1)}, f32[16,512]{1,0:T(8,128)S(1)}, u32[]{:S(2)}, u32[]{:S(2)}) collective-permute-start(f32[16,512]{1,0:T(8,128)S(1)} %multiply_add_fusion.1), channel_id=1, source_target_pairs={{0,64},{8,72},{16,80},{24,88},{32,96},{40,104},{48,112},{56,120},{... | collective-permute-start | bytes 98312 | tf_op jit(solution)/shard_map/ppermute | solution.py:24
  44.7 10.4 %shard_map.87.intra_ref = f32[512,512]{1,0:T(8,128)} custom-call(f32[512,512]{1,0:T(8,128)} %get-tuple-element.5.gated_ref, f32[16,1,512]{2,1,0:T(1,128)} %broadcast_in_dim.56.decay_ref, f32[16,1,512]{2,1,0:T(1,128)} %broadcast_in_dim.57.mixing_ref), custom_call_target="tpu_custom_call" | custom-call | flops 2147483648 | bytes 2097152 | tf_op jit(solution)/shard_map/pallas_call | solution.py:146
  56.2 5.1 %shard_map.88 = bf16[512,512]{1,0:T(8,128)(2,1)} custom-call(f32[512,512]{1,0:T(8,128)} %shard_map.87.intra_ref, f32[16,4,512]{2,1,0:T(4,128)} %maximum_add_fusion.state_ref, f32[16,1,512]{2,1,0:T(1,128)} %broadcast_in_dim.56.decay_ref, f32[16,1,512]{2,1,0:T(1,128)} %broadcast_in_dim.57.mixing_ref, f32[512,512]{1,0:T(8,128)} %get-tuple-element.5.gated_ref, ...), custom_call_target="tpu_custom_call" | custom-call | flops 8388608 | bytes 3670016 | tf_op jit(solution)/shard_map/pallas_call | solution.py:185
  61.3 3.5 %collective-permute-start.11 = (bf16[512,512]{1,0:T(8,128)(2,1)}, bf16[512,512]{1,0:T(8,128)(2,1)S(1)}, u32[]{:S(2)}, u32[]{:S(2)}) collective-permute-start(bf16[512,512]{1,0:T(8,128)(2,1)} %shard_map.88), channel_id=1, source_target_pairs={{1,0},{2,1},{3,2},{4,3},{5,4},{6,5},{7,6},{0,7},{9,8},{10,9},{11,1... | collective-permute-start | bytes 1572872 | tf_op jit(solution)/shard_map/ppermute | solution.py:228
  66.4 2.9 %collective-permute-start.14 = (bf16[512,512]{1,0:T(8,128)(2,1)}, bf16[512,512]{1,0:T(8,128)(2,1)S(1)}, u32[]{:S(2)}, u32[]{:S(2)}) collective-permute-start(bf16[512,512]{1,0:T(8,128)(2,1)} %shard_map.88), channel_id=1, source_target_pairs={{4,0},{5,1},{6,2},{7,3},{0,4},{1,5},{2,6},{3,7},{12,8},{13,9},{14,... | collective-permute-start | bytes 1572872 | tf_op jit(solution)/shard_map/ppermute | solution.py:228
  70.8 19.4 %collective-permute-done.11 = bf16[512,512]{1,0:T(8,128)(2,1)S(1)} collective-permute-done((bf16[512,512]{1,0:T(8,128)(2,1)}, bf16[512,512]{1,0:T(8,128)(2,1)S(1)}, u32[]{:S(2)}, u32[]{:S(2)}) %collective-permute-start.11) | collective-permute-done | bytes 524320 | tf_op jit(solution)/shard_map/ppermute | solution.py:228
  90.1 2.5 %collective-permute-start.16 = (bf16[512,512]{1,0:T(8,128)(2,1)}, bf16[512,512]{1,0:T(8,128)(2,1)S(1)}, u32[]{:S(2)}, u32[]{:S(2)}) collective-permute-start(bf16[512,512]{1,0:T(8,128)(2,1)} %shard_map.88), channel_id=1, source_target_pairs={{6,0},{7,1},{0,2},{1,3},{2,4},{3,5},{4,6},{5,7},{14,8},{15,9},{8,1... | collective-permute-start | bytes 1572872 | tf_op jit(solution)/shard_map/ppermute | solution.py:228
  92.7 18.8 %collective-permute-start.17 = (bf16[512,512]{1,0:T(8,128)(2,1)}, bf16[512,512]{1,0:T(8,128)(2,1)S(1)}, u32[]{:S(2)}, u32[]{:S(2)}) collective-permute-start(bf16[512,512]{1,0:T(8,128)(2,1)} %shard_map.88), channel_id=1, source_target_pairs={{7,0},{0,1},{1,2},{2,3},{3,4},{4,5},{5,6},{6,7},{15,8},{8,9},{9,10... | collective-permute-start | bytes 1572872 | tf_op jit(solution)/shard_map/ppermute | solution.py:228
  111.7 4.8 %collective-permute-done.15 = bf16[512,512]{1,0:T(8,128)(2,1)S(1)} collective-permute-done((bf16[512,512]{1,0:T(8,128)(2,1)}, bf16[512,512]{1,0:T(8,128)(2,1)S(1)}, u32[]{:S(2)}, u32[]{:S(2)}) %collective-permute-start.15) | collective-permute-done | bytes 524320 | tf_op jit(solution)/shard_map/ppermute | solution.py:228
  116.6 12.2 %collective-permute-done.16 = bf16[512,512]{1,0:T(8,128)(2,1)S(1)} collective-permute-done((bf16[512,512]{1,0:T(8,128)(2,1)}, bf16[512,512]{1,0:T(8,128)(2,1)S(1)}, u32[]{:S(2)}, u32[]{:S(2)}) %collective-permute-start.16) | collective-permute-done | bytes 524320 | tf_op jit(solution)/shard_map/ppermute | solution.py:228
  129.4 3.2 %copy-done.1 = bf16[512,8192]{1,0:T(8,128)(2,1)} copy-done((bf16[512,8192]{1,0:T(8,128)(2,1)}, bf16[512,8192]{1,0:T(8,128)(2,1)S(1)}, u32[]{:S(2)}) %copy-start.1) | copy-done | bytes 8388632
  133.6 6.0 %fusion.16 = bf16[512,512]{0,1:T(8,128)(2,1)S(1)} fusion(bf16[4096,768]{0,1:T(8,128)(2,1)} %bitcast.77, f32[4096]{0:T(1024)S(1)} %copy-done.6, f32[512]{0:T(512)S(1)} %add_rsqrt_fusion, bf16[512,8192]{1,0:T(8,128)(2,1)} %copy-done.1, s32[]{:T(128)S(6)} %select_n.119), kind=kOutput, calls=%fused_computation.24 | convolution fusion | flops 2156134400 | bytes 8931332 | tf_op jit(solution)/shard_map/dot_general | solution.py:237
  139.7 3.0 %fusion.22 = bf16[512,256]{0,1:T(8,128)(2,1)S(1)} fusion(bf16[4096,768]{0,1:T(8,128)(2,1)} %bitcast.78, f32[4096]{0:T(1024)S(1)} %copy-done.6, f32[512]{0:T(512)S(1)} %add_rsqrt_fusion, bf16[512,8192]{1,0:T(8,128)(2,1)S(1)} %copy-done.2, s32[]{:T(128)S(6)} %select_n.119), kind=kOutput, calls=%fused_computation.30 | convolution fusion | flops 1082261504 | bytes 6572036 | tf_op jit(solution)/shard_map/dot_general | solution.py:247
  144.8 3.8 %collective-permute-start.19 = (bf16[512,128]{0,1:T(8,128)(2,1)S(1)}, bf16[512,128]{0,1:T(8,128)(2,1)S(1)}, u32[]{:S(2)}, u32[]{:S(2)}) collective-permute-start(bf16[512,128]{0,1:T(8,128)(2,1)S(1)} %get-tuple-element.19), channel_id=1, source_target_pairs={{0,8},{8,16},{16,24},{24,32},{32,40},{40,48},{48,56},{56,64},{64,7... | collective-permute-start | bytes 393224 | tf_op jit(solution)/shard_map/ppermute | solution.py:24
  150.5 2.2 %collective-permute-start.23 = (bf16[512,128]{0,1:T(8,128)(2,1)S(1)}, bf16[512,128]{0,1:T(8,128)(2,1)S(1)}, u32[]{:S(2)}, u32[]{:S(2)}) collective-permute-start(bf16[512,128]{0,1:T(8,128)(2,1)S(1)} %get-tuple-element.18), channel_id=1, source_target_pairs={{0,8},{8,16},{16,24},{24,32},{32,40},{40,48},{48,56},{56,64},{64,7... | collective-permute-start | bytes 393224 | tf_op jit(solution)/shard_map/ppermute | solution.py:24
  155.7 2.1 %collective-permute-done.19 = bf16[512,128]{0,1:T(8,128)(2,1)S(1)} collective-permute-done((bf16[512,128]{0,1:T(8,128)(2,1)S(1)}, bf16[512,128]{0,1:T(8,128)(2,1)S(1)}, u32[]{:S(2)}, u32[]{:S(2)}) %collective-permute-start.19) | collective-permute-done | bytes 131104 | tf_op jit(solution)/shard_map/ppermute | solution.py:24
  157.8 1.9 %collective-permute-start.21 = (bf16[512,128]{0,1:T(8,128)(2,1)S(1)}, bf16[512,128]{0,1:T(8,128)(2,1)S(1)}, u32[]{:S(2)}, u32[]{:S(2)}) collective-permute-start(bf16[512,128]{0,1:T(8,128)(2,1)S(1)} %collective-permute-done.19), channel_id=1, source_target_pairs={{0,8},{8,16},{16,24},{24,32},{32,40},{40,48},{48,56},{56,64},{64,7... | collective-permute-start | bytes 393224 | tf_op jit(solution)/shard_map/ppermute | solution.py:24
  162.6 2.5 %collective-permute-start.25 = (bf16[512,128]{0,1:T(8,128)(2,1)S(1)}, bf16[512,128]{0,1:T(8,128)(2,1)S(1)}, u32[]{:S(2)}, u32[]{:S(2)}) collective-permute-start(bf16[512,128]{0,1:T(8,128)(2,1)S(1)} %collective-permute-done.23), channel_id=1, source_target_pairs={{0,8},{8,16},{16,24},{24,32},{32,40},{40,48},{48,56},{56,64},{64,7... | collective-permute-start | bytes 393224 | tf_op jit(solution)/shard_map/ppermute | solution.py:24
  165.2 5.0 %collective-permute-done.21 = bf16[512,128]{0,1:T(8,128)(2,1)S(1)} collective-permute-done((bf16[512,128]{0,1:T(8,128)(2,1)S(1)}, bf16[512,128]{0,1:T(8,128)(2,1)S(1)}, u32[]{:S(2)}, u32[]{:S(2)}) %collective-permute-start.21) | collective-permute-done | bytes 131104 | tf_op jit(solution)/shard_map/ppermute | solution.py:24
  (101 shorter events, 36.0 us)
Async XLA Ops:
  7.2 126.4 %all-gather.2.cloned.1.call-start = ((), (), s32[]{:S(2)}) async-start(), calls=%async_computation | async-start | bytes 6488064 | tf_op jit(solution)/shard_map/all_gather | solution.py:211
  9.7 9.4 %collective-permute-start = (bf16[6,3,512]{2,0,1:T(8,128)(2,1)S(1)}, bf16[6,3,512]{2,0,1:T(8,128)(2,1)S(1)}, u32[]{:S(2)}, u32[]{:S(2)}) collective-permute-start(bf16[6,3,512]{2,0,1:T(8,128)(2,1)S(1)} %slice.35), channel_id=1, source_target_pairs={{0,8},{8,16},{16,24},{24,32},{32,40},{40,48},{48,56},{56,64},{64,7... | collective-permute-start | bytes 55304 | tf_op jit(solution)/shard_map/ppermute | solution.py:24
  29.5 6.0 %collective-permute-start.1 = (f32[16,512]{1,0:T(8,128)S(1)}, f32[16,512]{1,0:T(8,128)S(1)}, u32[]{:S(2)}, u32[]{:S(2)}) collective-permute-start(f32[16,512]{1,0:T(8,128)S(1)} %get-tuple-element.15), channel_id=1, source_target_pairs={{0,8},{8,16},{16,24},{24,32},{32,40},{40,48},{48,56},{56,0},{64,72... | collective-permute-start | bytes 98312 | tf_op jit(solution)/shard_map/ppermute | solution.py:171
  29.5 7.2 %collective-permute-start.2 = (f32[16,512]{1,0:T(8,128)S(1)}, f32[16,512]{1,0:T(8,128)S(1)}, u32[]{:S(2)}, u32[]{:S(2)}) collective-permute-start(f32[16,512]{1,0:T(8,128)S(1)} %get-tuple-element.15), channel_id=1, source_target_pairs={{0,16},{8,24},{16,32},{24,40},{32,48},{40,56},{48,0},{56,8},{64,80... | collective-permute-start | bytes 98312 | tf_op jit(solution)/shard_map/ppermute | solution.py:171
  29.9 7.7 %collective-permute-start.3 = (f32[16,512]{1,0:T(8,128)S(1)}, f32[16,512]{1,0:T(8,128)S(1)}, u32[]{:S(2)}, u32[]{:S(2)}) collective-permute-start(f32[16,512]{1,0:T(8,128)S(1)} %get-tuple-element.15), channel_id=1, source_target_pairs={{0,24},{8,32},{16,40},{24,48},{32,56},{40,0},{48,8},{56,16},{64,88... | collective-permute-start | bytes 98312 | tf_op jit(solution)/shard_map/ppermute | solution.py:171
  30.5 7.1 %collective-permute-start.4 = (f32[16,512]{1,0:T(8,128)S(1)}, f32[16,512]{1,0:T(8,128)S(1)}, u32[]{:S(2)}, u32[]{:S(2)}) collective-permute-start(f32[16,512]{1,0:T(8,128)S(1)} %get-tuple-element.15), channel_id=1, source_target_pairs={{0,32},{8,40},{16,48},{24,56},{32,0},{40,8},{48,16},{56,24},{64,96... | collective-permute-start | bytes 98312 | tf_op jit(solution)/shard_map/ppermute | solution.py:171
  39.8 15.4 %collective-permute-start.10 = (f32[16,512]{1,0:T(8,128)S(1)}, f32[16,512]{1,0:T(8,128)S(1)}, u32[]{:S(2)}, u32[]{:S(2)}) collective-permute-start(f32[16,512]{1,0:T(8,128)S(1)} %multiply_add_fusion.1), channel_id=1, source_target_pairs={{0,192},{8,200},{16,208},{24,216},{32,224},{40,232},{48,240},{56,2... | collective-permute-start | bytes 98312 | tf_op jit(solution)/shard_map/ppermute | solution.py:24
  40.4 14.8 %collective-permute-start.8 = (f32[16,512]{1,0:T(8,128)S(1)}, f32[16,512]{1,0:T(8,128)S(1)}, u32[]{:S(2)}, u32[]{:S(2)}) collective-permute-start(f32[16,512]{1,0:T(8,128)S(1)} %multiply_add_fusion.1), channel_id=1, source_target_pairs={{0,64},{8,72},{16,80},{24,88},{32,96},{40,104},{48,112},{56,120},{... | collective-permute-start | bytes 98312 | tf_op jit(solution)/shard_map/ppermute | solution.py:24
  43.4 11.9 %collective-permute-start.9 = (f32[16,512]{1,0:T(8,128)S(1)}, f32[16,512]{1,0:T(8,128)S(1)}, u32[]{:S(2)}, u32[]{:S(2)}) collective-permute-start(f32[16,512]{1,0:T(8,128)S(1)} %multiply_add_fusion.1), channel_id=1, source_target_pairs={{0,128},{8,136},{16,144},{24,152},{32,160},{40,168},{48,176},{56,1... | collective-permute-start | bytes 98312 | tf_op jit(solution)/shard_map/ppermute | solution.py:24
  61.3 28.9 %collective-permute-start.11 = (bf16[512,512]{1,0:T(8,128)(2,1)}, bf16[512,512]{1,0:T(8,128)(2,1)S(1)}, u32[]{:S(2)}, u32[]{:S(2)}) collective-permute-start(bf16[512,512]{1,0:T(8,128)(2,1)} %shard_map.88), channel_id=1, source_target_pairs={{1,0},{2,1},{3,2},{4,3},{5,4},{6,5},{7,6},{0,7},{9,8},{10,9},{11,1... | collective-permute-start | bytes 1572872 | tf_op jit(solution)/shard_map/ppermute | solution.py:228
  64.7 27.9 %collective-permute-start.12 = (bf16[512,512]{1,0:T(8,128)(2,1)}, bf16[512,512]{1,0:T(8,128)(2,1)S(1)}, u32[]{:S(2)}, u32[]{:S(2)}) collective-permute-start(bf16[512,512]{1,0:T(8,128)(2,1)} %shard_map.88), channel_id=1, source_target_pairs={{2,0},{3,1},{4,2},{5,3},{6,4},{7,5},{0,6},{1,7},{10,8},{11,9},{12,... | collective-permute-start | bytes 1572872 | tf_op jit(solution)/shard_map/ppermute | solution.py:228
  65.5 46.1 %collective-permute-start.13 = (bf16[512,512]{1,0:T(8,128)(2,1)}, bf16[512,512]{1,0:T(8,128)(2,1)S(1)}, u32[]{:S(2)}, u32[]{:S(2)}) collective-permute-start(bf16[512,512]{1,0:T(8,128)(2,1)} %shard_map.88), channel_id=1, source_target_pairs={{3,0},{4,1},{5,2},{6,3},{7,4},{0,5},{1,6},{2,7},{11,8},{12,9},{13,... | collective-permute-start | bytes 1572872 | tf_op jit(solution)/shard_map/ppermute | solution.py:228
  66.4 45.2 %collective-permute-start.14 = (bf16[512,512]{1,0:T(8,128)(2,1)}, bf16[512,512]{1,0:T(8,128)(2,1)S(1)}, u32[]{:S(2)}, u32[]{:S(2)}) collective-permute-start(bf16[512,512]{1,0:T(8,128)(2,1)} %shard_map.88), channel_id=1, source_target_pairs={{4,0},{5,1},{6,2},{7,3},{0,4},{1,5},{2,6},{3,7},{12,8},{13,9},{14,... | collective-permute-start | bytes 1572872 | tf_op jit(solution)/shard_map/ppermute | solution.py:228
  69.4 47.1 %collective-permute-start.15 = (bf16[512,512]{1,0:T(8,128)(2,1)}, bf16[512,512]{1,0:T(8,128)(2,1)S(1)}, u32[]{:S(2)}, u32[]{:S(2)}) collective-permute-start(bf16[512,512]{1,0:T(8,128)(2,1)} %shard_map.88), channel_id=1, source_target_pairs={{5,0},{6,1},{7,2},{0,3},{1,4},{2,5},{3,6},{4,7},{13,8},{14,9},{15,... | collective-permute-start | bytes 1572872 | tf_op jit(solution)/shard_map/ppermute | solution.py:228
  90.1 38.6 %collective-permute-start.16 = (bf16[512,512]{1,0:T(8,128)(2,1)}, bf16[512,512]{1,0:T(8,128)(2,1)S(1)}, u32[]{:S(2)}, u32[]{:S(2)}) collective-permute-start(bf16[512,512]{1,0:T(8,128)(2,1)} %shard_map.88), channel_id=1, source_target_pairs={{6,0},{7,1},{0,2},{1,3},{2,4},{3,5},{4,6},{5,7},{14,8},{15,9},{8,1... | collective-permute-start | bytes 1572872 | tf_op jit(solution)/shard_map/ppermute | solution.py:228
  92.7 36.1 %collective-permute-start.17 = (bf16[512,512]{1,0:T(8,128)(2,1)}, bf16[512,512]{1,0:T(8,128)(2,1)S(1)}, u32[]{:S(2)}, u32[]{:S(2)}) collective-permute-start(bf16[512,512]{1,0:T(8,128)(2,1)} %shard_map.88), channel_id=1, source_target_pairs={{7,0},{0,1},{1,2},{2,3},{3,4},{4,5},{5,6},{6,7},{15,8},{8,9},{9,10... | collective-permute-start | bytes 1572872 | tf_op jit(solution)/shard_map/ppermute | solution.py:228
  142.8 10.9 %collective-permute-start.18 = (bf16[512,128]{0,1:T(8,128)(2,1)S(1)}, bf16[512,128]{0,1:T(8,128)(2,1)S(1)}, u32[]{:S(2)}, u32[]{:S(2)}) collective-permute-start(bf16[512,128]{0,1:T(8,128)(2,1)S(1)} %get-tuple-element.20), channel_id=1, source_target_pairs={{0,8},{8,16},{16,24},{24,32},{32,40},{40,48},{48,56},{56,64},{64,7... | collective-permute-start | bytes 393224 | tf_op jit(solution)/shard_map/ppermute | solution.py:24
  144.8 13.0 %collective-permute-start.19 = (bf16[512,128]{0,1:T(8,128)(2,1)S(1)}, bf16[512,128]{0,1:T(8,128)(2,1)S(1)}, u32[]{:S(2)}, u32[]{:S(2)}) collective-permute-start(bf16[512,128]{0,1:T(8,128)(2,1)S(1)} %get-tuple-element.19), channel_id=1, source_target_pairs={{0,8},{8,16},{16,24},{24,32},{32,40},{40,48},{48,56},{56,64},{64,7... | collective-permute-start | bytes 393224 | tf_op jit(solution)/shard_map/ppermute | solution.py:24
  148.6 11.6 %collective-permute-start.22 = (bf16[512,128]{0,1:T(8,128)(2,1)S(1)}, bf16[512,128]{0,1:T(8,128)(2,1)S(1)}, u32[]{:S(2)}, u32[]{:S(2)}) collective-permute-start(bf16[512,128]{0,1:T(8,128)(2,1)S(1)} %get-tuple-element.17), channel_id=1, source_target_pairs={{0,8},{8,16},{16,24},{24,32},{32,40},{40,48},{48,56},{56,64},{64,7... | collective-permute-start | bytes 393224 | tf_op jit(solution)/shard_map/ppermute | solution.py:24
  150.5 12.0 %collective-permute-start.23 = (bf16[512,128]{0,1:T(8,128)(2,1)S(1)}, bf16[512,128]{0,1:T(8,128)(2,1)S(1)}, u32[]{:S(2)}, u32[]{:S(2)}) collective-permute-start(bf16[512,128]{0,1:T(8,128)(2,1)S(1)} %get-tuple-element.18), channel_id=1, source_target_pairs={{0,8},{8,16},{16,24},{24,32},{32,40},{40,48},{48,56},{56,64},{64,7... | collective-permute-start | bytes 393224 | tf_op jit(solution)/shard_map/ppermute | solution.py:24
  153.8 11.4 %collective-permute-start.20 = (bf16[512,128]{0,1:T(8,128)(2,1)S(1)}, bf16[512,128]{0,1:T(8,128)(2,1)S(1)}, u32[]{:S(2)}, u32[]{:S(2)}) collective-permute-start(bf16[512,128]{0,1:T(8,128)(2,1)S(1)} %collective-permute-done.18), channel_id=1, source_target_pairs={{0,8},{8,16},{16,24},{24,32},{32,40},{40,48},{48,56},{56,64},{64,7... | collective-permute-start | bytes 393224 | tf_op jit(solution)/shard_map/ppermute | solution.py:24
  157.8 12.3 %collective-permute-start.21 = (bf16[512,128]{0,1:T(8,128)(2,1)S(1)}, bf16[512,128]{0,1:T(8,128)(2,1)S(1)}, u32[]{:S(2)}, u32[]{:S(2)}) collective-permute-start(bf16[512,128]{0,1:T(8,128)(2,1)S(1)} %collective-permute-done.19), channel_id=1, source_target_pairs={{0,8},{8,16},{16,24},{24,32},{32,40},{40,48},{48,56},{56,64},{64,7... | collective-permute-start | bytes 393224 | tf_op jit(solution)/shard_map/ppermute | solution.py:24
  160.2 13.1 %collective-permute-start.24 = (bf16[512,128]{0,1:T(8,128)(2,1)S(1)}, bf16[512,128]{0,1:T(8,128)(2,1)S(1)}, u32[]{:S(2)}, u32[]{:S(2)}) collective-permute-start(bf16[512,128]{0,1:T(8,128)(2,1)S(1)} %collective-permute-done.22), channel_id=1, source_target_pairs={{0,8},{8,16},{16,24},{24,32},{32,40},{40,48},{48,56},{56,64},{64,7... | collective-permute-start | bytes 393224 | tf_op jit(solution)/shard_map/ppermute | solution.py:24
  162.6 11.2 %collective-permute-start.25 = (bf16[512,128]{0,1:T(8,128)(2,1)S(1)}, bf16[512,128]{0,1:T(8,128)(2,1)S(1)}, u32[]{:S(2)}, u32[]{:S(2)}) collective-permute-start(bf16[512,128]{0,1:T(8,128)(2,1)S(1)} %collective-permute-done.23), channel_id=1, source_target_pairs={{0,8},{8,16},{16,24},{24,32},{32,40},{40,48},{48,56},{56,64},{64,7... | collective-permute-start | bytes 393224 | tf_op jit(solution)/shard_map/ppermute | solution.py:24
  (10 other events, 131.6 us)
Sparse Core Ops, SparseCore 0:
  11.0 75.2 all-gather.1
